TPU v7x, 256 devices: a whole 4x4x8 slice. The times are simulated.
256 devices in a mesh: rows: 32 (over x, z), centers: 8 (over y, core).
Axes of the slice: x: 4, y: 4, z: 8, core: 2. Of those that a mesh axis runs over, the one named last changes fastest.
Arguments:
- features: bfloat16 [440, 32768], P(None, 'rows'), may hold values from -16 to 16
- labels: int32 [32768], P('rows'), may hold values from 0 to 146
- center_index: int32 [8, 2048], P('centers'), may hold values from 0 to 32767
- warm_coef: float32 [147, 16384], P(None, 'centers'), may hold values from -10 to 10
Outputs:
- coef_out: float32 [147, 16384], P(None, 'centers')
- logits_out: float32 [147, 32768], P(None, ('rows', 'centers'))
All inputs are finite; a program needn't handle non-finite values.
Results may differ from a plain program's by a relative error of at most 0.0067.
Values may be sent and summed in bfloat16 or wider, within the bound.
No kernel may reach another device: no remote copies, remote signals or barrier semaphores. Data moves between devices by JAX's collectives and lax.ppermute only.
A program may use at most 64 MiB of HBM per device.

v0:
```python
import jax
import jax.numpy as jnp
from jax import lax
from jax.sharding import PartitionSpec as P

ROUNDS = 2
PASSES = 2


step_size = 0.1


def total_of_pieces(value, axis):
    return lax.all_gather(value, axis).sum(0)


def split_up(value, dim, count):
    before, after = (value.shape[:dim], value.shape[dim + 1 :])
    return jnp.moveaxis(value.reshape(*before, count, -1, *after), dim, 0)


def sum_at_owner(value, axis, dim):
    tiles = split_up(value, dim, lax.axis_size(axis))
    arrived = lax.all_to_all(tiles, axis, split_axis=0, concat_axis=0, tiled=True)
    return arrived.sum(axis=0)


def sent_to_all(value, axis):
    copies = jnp.broadcast_to(value, (lax.axis_size(axis), *value.shape))
    return lax.all_to_all(copies, axis, split_axis=0, concat_axis=0, tiled=True)


def laid_out(tiles, dim):
    tiles = jnp.moveaxis(tiles, 0, dim)
    lengths = tiles.shape
    return tiles.reshape(*lengths[:dim], lengths[dim] * lengths[dim + 1], *lengths[dim + 2 :])


def gather_directly(value, axis, dim):
    tiles = sent_to_all(value, axis)
    return laid_out(tiles, dim)


def build_kernel(features, centers, row_norms):
    center_norms = jnp.sum(jnp.square(centers.astype(jnp.float32)), axis=0)
    feat_count = features.shape[0]
    center_total = centers.shape[1]
    block_rows = min(512, center_total)
    pieces = []
    for begin in range(0, center_total, block_rows):
        finish = min(begin + block_rows, center_total)
        cross_term = lax.dot_general(
            centers[:, begin:finish],
            features,
            (((0,), (0,)), ((), ())),
            preferred_element_type=jnp.float32,
        )
        dist_sq = center_norms[begin:finish, None] + row_norms[None, :] - 2.0 * cross_term
        pieces.append(jnp.exp(-dist_sq / feat_count).astype(jnp.bfloat16))
    return jnp.concatenate(pieces, axis=0)


def body(features, labels, center_index, warm_coef):
    row_count = features.shape[1]
    class_count = warm_coef.shape[0]
    center_total = center_index.shape[1]
    local_idx = center_index[0] - lax.axis_index("rows") * row_count
    inside = ((local_idx >= 0) & (local_idx < row_count)).astype(jnp.bfloat16)
    picked = jnp.take(features, jnp.clip(local_idx, 0, row_count - 1), axis=1) * inside[None, :]
    centers = lax.psum(picked, "rows").astype(jnp.float32).astype(jnp.bfloat16)
    row_norms = jnp.sum(jnp.square(features.astype(jnp.float32)), axis=0)
    one_hot = (labels[None, :] == jnp.arange(class_count, dtype=jnp.int32)[:, None]).astype(
        jnp.float32
    )
    cached = build_kernel(features, centers, row_norms)

    def current():
        return cached

    share_cols = center_total // lax.axis_size("rows")
    my_part = lax.dynamic_slice_in_dim(
        warm_coef, lax.axis_index("rows") * share_cols, share_cols, 1
    )
    coef_low = warm_coef.astype(jnp.bfloat16)
    for round_idx in range(ROUNDS):
        kernel = current()
        own_part = jnp.dot(coef_low, kernel, preferred_element_type=jnp.float32)
        summed = total_of_pieces(own_part, "centers")
        base_part = summed - own_part
        group_part = own_part
        for pass_idx in range(PASSES):
            if pass_idx > 0:
                kernel = current()
                group_part = jnp.dot(coef_low, kernel, preferred_element_type=jnp.float32)
            logits = base_part + group_part
            raised = jnp.exp(logits)
            class_prob = raised / jnp.sum(raised, axis=0, keepdims=True)
            residual = (class_prob - one_hot).astype(jnp.bfloat16)
            local_grad = lax.dot_general(
                residual, kernel, (((1,), (1,)), ((), ())), preferred_element_type=jnp.float32
            )
            gradient = sum_at_owner(local_grad, "rows", 1)
            my_part = my_part - step_size * gradient
            coef_low = gather_directly(my_part.astype(jnp.bfloat16), "rows", 1)
    kernel = current()
    final_part = jnp.dot(coef_low, kernel, preferred_element_type=jnp.float32)
    logits_out = sum_at_owner(final_part, "centers", 1)
    coef_out = gather_directly(my_part, "rows", 1)
    return (coef_out, logits_out)


def solution(mesh):
    return jax.shard_map(
        body,
        mesh=mesh,
        in_specs=(P(None, "rows"), P("rows"), P("centers", None), P(None, "centers")),
        out_specs=(P(None, "centers"), P(None, ("rows", "centers"))),
        check_vma=False,
    )
```

profile of v0, /device:TPU:1, one launch (start us, length us, event | category | flops | bytes accessed | tf_op | source)
XLA Modules:
  0.0 761.6 jit_solution(18298936240424593603)
XLA Ops:
  10.2 7.5 gather_fusion
  19.7 153.6 %all-reduce.2.cloned.1.call-done = bf16[440,2048]{0,1:T(8,128)(2,1)} async-done(((bf16[440,2048]{0,1:T(8,128)(2,1)}), bf16[440,2048]{0,1:T(8,128)(2,1)}) %all-reduce.2.cloned.1.call-update) | async-done | bytes 1802256 | tf_op jit(solution)/shard_map/psum | solution.py:70
  182.8 40.1 %all-gather.7.cloned.1.call-done = f32[8,147,1024]{2,1,0:T(8,128)} async-done(((f32[1,147,1024]{2,1,0:T(8,128)}), f32[8,147,1024]{2,1,0:T(8,128)}) %all-gather.7.cloned.1.call-update) | async-done | bytes 4816912 | tf_op jit(solution)/shard_map/all_gather | solution.py:14
  223.0 3.0 reduce_sum.119
  226.8 4.1 fusion.19
  233.1 2.4 copy.28
  235.5 9.5 %all-to-all-start = ((f32[32,147,64]{1,2,0:T(8,128)}), f32[32,147,64]{1,2,0:T(8,128)S(1)}, u32[]{:S(2)}, u32[]{:S(2)}) async-start(f32[32,147,64]{1,2,0:T(8,128)} %copy.28), calls=%async_computation | async-start | bytes 4194304 | tf_op jit(solution)/shard_map/all_to_all | solution.py:24
  246.2 47.8 %all-to-all-done = f32[32,147,64]{1,2,0:T(8,128)S(1)} async-done(((f32[32,147,64]{1,2,0:T(8,128)}), f32[32,147,64]{1,2,0:T(8,128)S(1)}, u32[]{:S(2)}, u32[]{:S(2)}) %all-to-all-start) | async-done | bytes 1204256 | tf_op jit(solution)/shard_map/all_to_all | solution.py:24
  294.2 32.2 %all_to_all.50 = bf16[32,147,64]{1,2,0:T(8,128)(2,1)S(1)} all-to-all(bf16[32,147,64]{1,2,0:T(8,128)(2,1)S(1)} %broadcast_in_dim.22), channel_id=1, replica_groups=mesh['rows'=32,'centers'=8] {'rows'}, dimensions={0} | all-to-all | bytes 1204224 | tf_op jit(solution)/shard_map/all_to_all | solution.py:30
  326.5 3.4 fusion.40
  330.1 2.6 fusion.17
  337.2 56.0 %all_to_all.51 = f32[32,147,64]{1,2,0:T(8,128)S(1)} all-to-all(f32[32,147,64]{1,2,0:T(8,128)} %copy.30), channel_id=1, replica_groups=mesh['rows'=32,'centers'=8] {'rows'}, dimensions={0} | all-to-all | bytes 2408448 | tf_op jit(solution)/shard_map/all_to_all | solution.py:24
  394.1 33.1 %all_to_all.52 = bf16[32,147,64]{1,2,0:T(8,128)(2,1)S(1)} all-to-all(bf16[32,147,64]{1,2,0:T(8,128)(2,1)S(1)} %broadcast_in_dim.23), channel_id=1, replica_groups=mesh['rows'=32,'centers'=8] {'rows'}, dimensions={0} | all-to-all | bytes 1204224 | tf_op jit(solution)/shard_map/all_to_all | solution.py:30
  427.2 5.4 fusion.36
  432.7 37.5 %all-gather.9.cloned.1.call-done = f32[8,147,1024]{2,1,0:T(8,128)} async-done(((f32[1,147,1024]{2,1,0:T(8,128)}), f32[8,147,1024]{2,1,0:T(8,128)}) %all-gather.9.cloned.1.call-update) | async-done | bytes 4816912 | tf_op jit(solution)/shard_map/all_gather | solution.py:14
  470.1 3.0 reduce_sum.124
  474.1 4.1 fusion.15
  480.3 2.4 copy.32
  482.8 57.3 %all_to_all.53 = f32[32,147,64]{1,2,0:T(8,128)S(1)} all-to-all(f32[32,147,64]{1,2,0:T(8,128)} %copy.32), channel_id=1, replica_groups=mesh['rows'=32,'centers'=8] {'rows'}, dimensions={0} | all-to-all | bytes 2408448 | tf_op jit(solution)/shard_map/all_to_all | solution.py:24
  540.4 33.1 %all_to_all.54 = bf16[32,147,64]{1,2,0:T(8,128)(2,1)S(1)} all-to-all(bf16[32,147,64]{1,2,0:T(8,128)(2,1)S(1)} %broadcast_in_dim.24), channel_id=1, replica_groups=mesh['rows'=32,'centers'=8] {'rows'}, dimensions={0} | all-to-all | bytes 1204224 | tf_op jit(solution)/shard_map/all_to_all | solution.py:30
  573.4 5.1 fusion.41
  578.6 2.6 fusion.13
  583.3 2.4 copy.34
  585.7 55.7 %all_to_all.55 = f32[32,147,64]{1,2,0:T(8,128)S(1)} all-to-all(f32[32,147,64]{1,2,0:T(8,128)} %copy.34), channel_id=1, replica_groups=mesh['rows'=32,'centers'=8] {'rows'}, dimensions={0} | all-to-all | bytes 2408448 | tf_op jit(solution)/shard_map/all_to_all | solution.py:24
  643.3 8.1 %all-to-all-start.8 = ((bf16[32,147,64]{1,2,0:T(8,128)(2,1)}), bf16[32,147,64]{1,2,0:T(8,128)(2,1)S(1)}, u32[]{:S(2)}, u32[]{:S(2)}) async-start(bf16[32,147,64]{1,2,0:T(8,128)(2,1)} %broadcast_in_dim.46), calls=%async_computation.8 | async-start | bytes 2097152 | tf_op jit(solution)/shard_map/all_to_all | solution.py:30
  651.5 3.5 fusion.35
  654.9 6.5 copy.43
  661.5 15.2 %all-to-all-done.8 = bf16[32,147,64]{1,2,0:T(8,128)(2,1)S(1)} async-done(((bf16[32,147,64]{1,2,0:T(8,128)(2,1)}), bf16[32,147,64]{1,2,0:T(8,128)(2,1)S(1)}, u32[]{:S(2)}, u32[]{:S(2)}) %all-to-all-start.8) | async-done | bytes 602144 | tf_op jit(solution)/shard_map/all_to_all | solution.py:30
  676.6 3.8 convolution_bitcast_fusion
  680.4 17.9 %all_to_all.56 = f32[8,147,128]{2,1,0:T(8,128)S(1)} all-to-all(f32[8,147,128]{2,1,0:T(8,128)S(1)} %convolution_bitcast_fusion), channel_id=1, replica_groups=mesh['rows'=32,'centers'=8] {'centers'}, dimensions={0} | all-to-all | bytes 1204224 | tf_op jit(solution)/shard_map/all_to_all | solution.py:24
  699.9 4.7 all-to-all-start.7
  705.2 48.2 %all-to-all-done.7 = f32[32,147,64]{1,2,0:T(8,128)S(1)} async-done(((f32[32,147,64]{1,2,0:T(8,128)}), f32[32,147,64]{1,2,0:T(8,128)S(1)}, u32[]{:S(2)}, u32[]{:S(2)}) %all-to-all-start.7) | async-done | bytes 1204256 | tf_op jit(solution)/shard_map/all_to_all | solution.py:30
  (98 shorter events, 35.5 us)
Async XLA Ops:
  7.2 166.2 %all-reduce.2.cloned.1.call-start = ((), (), s32[]{:S(2)}) async-start(), calls=%async_computation.10 | async-start | bytes 4194304 | tf_op jit(solution)/shard_map/psum | solution.py:70
  17.7 1.8 copy-start
  19.4 203.5 %all-gather.7.cloned.1.call-start = ((), (), s32[]{:S(2)}) async-start(), calls=%async_computation.11 | async-start | bytes 5603328 | tf_op jit(solution)/shard_map/all_gather | solution.py:14
  173.3 4.2 copy-start.4
  177.5 48.6 %copy-start.5 = (bf16[512,1024]{1,0:T(8,128)(2,1)}, bf16[512,1024]{1,0:T(8,128)(2,1)S(1)}, u32[]{:S(2)}) copy-start(bf16[512,1024]{1,0:T(8,128)(2,1)S(1)} %exponential_convert_fusion.3) | copy-start | bytes 3145732
  178.5 1.8 copy-start.8
  179.4 3.4 copy-start.13
  179.4 1.7 copy-start.25
  181.1 1.8 copy-start.16
  182.8 43.1 %copy-start.1 = (f32[1024,147]{0,1:T(8,128)S(1)}, f32[1024,147]{0,1:T(8,128)}, u32[]{:S(2)}) copy-start(f32[1024,147]{0,1:T(8,128)} %fusion.7) | copy-start | bytes 1806340
  182.8 44.0 %copy-start.26 = (s32[1024]{0:T(1024)S(1)}, s32[1024]{0:T(1024)}, u32[]{:S(2)}) copy-start(s32[1024]{0:T(1024)} %param.5) | copy-start | bytes 12292
  226.0 0.8 copy-start.3
  235.5 58.5 %all-to-all-start = ((f32[32,147,64]{1,2,0:T(8,128)}), f32[32,147,64]{1,2,0:T(8,128)S(1)}, u32[]{:S(2)}, u32[]{:S(2)}) async-start(f32[32,147,64]{1,2,0:T(8,128)} %copy.28), calls=%async_computation | async-start | bytes 4194304 | tf_op jit(solution)/shard_map/all_to_all | solution.py:24
  245.0 225.1 %all-gather.9.cloned.1.call-start = ((), (), s32[]{:S(2)}) async-start(), calls=%async_computation.12 | async-start | bytes 5603328 | tf_op jit(solution)/shard_map/all_gather | solution.py:14
  246.2 83.7 %copy-start.20 = (f32[147,64]{0,1:T(8,128)}, f32[147,64]{0,1:T(8,128)S(1)}, u32[]{:S(2)}) copy-start(f32[147,64]{0,1:T(8,128)S(1)} %copy.44) | copy-start | bytes 112900
  326.5 3.4 copy-start.6
  326.5 3.4 copy-start.9
  326.5 3.4 copy-start.14
  326.5 3.6 copy-start.17
  337.2 56.1 %copy-start.21 = (f32[147,64]{0,1:T(8,128)S(1)}, f32[147,64]{0,1:T(8,128)}, u32[]{:S(2)}) copy-start(f32[147,64]{0,1:T(8,128)} %copy-done.20) | copy-start | bytes 112900
  337.2 90.0 %copy-start.7 = (bf16[512,1024]{1,0:T(8,128)(2,1)S(1)}, bf16[512,1024]{1,0:T(8,128)(2,1)}, u32[]{:S(2)}) copy-start(bf16[512,1024]{1,0:T(8,128)(2,1)} %copy-done.5) | copy-start | bytes 3145732
  432.6 40.5 %copy-start.2 = (f32[147,1024]{1,0:T(8,128)S(1)}, f32[147,1024]{1,0:T(8,128)}, u32[]{:S(2)}) copy-start(f32[147,1024]{1,0:T(8,128)} %fusion.36) | copy-start | bytes 1806340
  432.6 41.5 %copy-start.10 = (bf16[512,1024]{1,0:T(8,128)(2,1)S(1)}, bf16[512,1024]{1,0:T(8,128)(2,1)}, u32[]{:S(2)}) copy-start(bf16[512,1024]{1,0:T(8,128)(2,1)} %copy-done.8) | copy-start | bytes 3145732
  482.8 57.5 %copy-start.22 = (f32[147,64]{0,1:T(8,128)S(1)}, f32[147,64]{0,1:T(8,128)}, u32[]{:S(2)}) copy-start(f32[147,64]{0,1:T(8,128)} %get-tuple-element.7) | copy-start | bytes 112900
  573.4 5.1 copy-start.11
  573.4 5.1 copy-start.15
  573.4 5.1 copy-start.18
  585.7 55.9 %copy-start.23 = (f32[147,64]{0,1:T(8,128)S(1)}, f32[147,64]{0,1:T(8,128)}, u32[]{:S(2)}) copy-start(f32[147,64]{0,1:T(8,128)} %get-tuple-element.7) | copy-start | bytes 112900
  641.6 9.9 %copy-start.12 = (bf16[512,1024]{1,0:T(8,128)(2,1)S(1)}, bf16[512,1024]{1,0:T(8,128)(2,1)}, u32[]{:S(2)}) copy-start(bf16[512,1024]{1,0:T(8,128)(2,1)} %copy-done.8) | copy-start | bytes 3145732
  643.3 33.3 %all-to-all-start.8 = ((bf16[32,147,64]{1,2,0:T(8,128)(2,1)}), bf16[32,147,64]{1,2,0:T(8,128)(2,1)S(1)}, u32[]{:S(2)}, u32[]{:S(2)}) async-start(bf16[32,147,64]{1,2,0:T(8,128)(2,1)} %broadcast_in_dim.46), calls=%async_computation.8 | async-start | bytes 2097152 | tf_op jit(solution)/shard_map/all_to_all | solution.py:30
  676.6 21.7 %copy-start.24 = (f32[147,64]{0,1:T(8,128)S(1)}, f32[147,64]{0,1:T(8,128)}, u32[]{:S(2)}) copy-start(f32[147,64]{0,1:T(8,128)} %get-tuple-element.3) | copy-start | bytes 112900
  699.9 53.6 %all-to-all-start.7 = ((f32[32,147,64]{1,2,0:T(8,128)}), f32[32,147,64]{1,2,0:T(8,128)S(1)}, u32[]{:S(2)}, u32[]{:S(2)}) async-start(f32[32,147,64]{1,2,0:T(8,128)} %broadcast_in_dim.25), calls=%async_computation.7 | async-start | bytes 4194304 | tf_op jit(solution)/shard_map/all_to_all | solution.py:30
  (1 other events, 0.8 us)
Sparse Core Ops, SparseCore 0:
  19.6 153.7 all-reduce.1
  183.0 39.9 all-gather.6
  432.8 37.2 all-gather.8
where the time goes:
time: 763 us; the launch traced here: 762 us
  waiting for transfers between devices  342 us (45%)
  blocking collectives  285 us (37%)
  local copies, waits for them, and re-layouts  41.8 us (5%)
  matrix products  37.4 us (5%)
  starting transfers between devices  22.5 us (3%)
  other arithmetic  17.9 us (2%)
  between operations  14.2 us (2%)
    all_to_all x4, blocking collectives, sum_at_owner(): lax.all_to_all(tiles, axis, split_axis=0, concat_axis=0, tiled=True)  187 us
    psum x1, waiting for transfers between devices, body(): centers = lax.psum(picked, 'rows').astype(jnp.float32).astype(jnp.bfloat16)  154 us
    all_to_all x3, blocking collectives, sent_to_all(): return lax.all_to_all(copies, axis, split_axis=0, concat_axis=0, tiled=True)  98.4 us
    all_gather x2, waiting for transfers between devices, total_of_pieces(): return lax.all_gather(value, axis).sum(0)  77.6 us
    all_to_all x2, waiting for transfers between devices, sent_to_all(): return lax.all_to_all(copies, axis, split_axis=0, concat_axis=0, tiled=True)  63.4 us
    all_to_all x1, waiting for transfers between devices, sum_at_owner(): lax.all_to_all(tiles, axis, split_axis=0, concat_axis=0, tiled=True)  47.8 us
  transfers between devices with their start and end apart: 6, of which 6 were waited for; matrix products, arithmetic and copies ran while one was open for 2% of the time, Pallas kernels for 0%

commit v1 on v0

v1 whole, which is shorter than its diff:
```python
import jax
import jax.numpy as jnp
from jax import lax
from jax.experimental import pallas as pl
from jax.experimental.pallas import tpu as pltpu
from jax.sharding import PartitionSpec as P

ROUNDS = 2
PASSES = 2
STEP = 0.1

X, Z, Y, CORES = 4, 8, 4, 2
CLASSES = 147
PAD = 160
WIRE = 152
FEAT = 440
FPAD = 448
LANES = 128
CHUNK = X * LANES
PART = CHUNK // 4
BLOCK = 256

F32 = jnp.float32
BF16 = jnp.bfloat16
LOG2E = 1.4426950408889634

X_GROUPS = [[x * Z + z for x in range(X)] for z in range(Z)]
Z_GROUPS = [[x * Z + z for z in range(Z)] for x in range(X)]
Y_GROUPS = [[y * CORES + k for y in range(Y)] for k in range(CORES)]
CORE_SWAP = [(y * CORES + k, y * CORES + 1 - k) for y in range(Y) for k in range(CORES)]


def x_shift(d):
    return [(x * Z + z, (x + d) % X * Z + z) for x in range(X) for z in range(Z)]


def call(kernel, outs, scratch=(), name=None):
    vmem = pl.BlockSpec(memory_space=pltpu.VMEM)
    many = isinstance(outs, (list, tuple))
    return lambda *args: pl.pallas_call(
        kernel,
        out_shape=outs,
        in_specs=[vmem] * len(args),
        out_specs=[vmem] * len(outs) if many else vmem,
        scratch_shapes=list(scratch),
        name=name,
    )(*args)


def like(shape, dtype):
    return jax.ShapeDtypeStruct(shape, dtype)


def my_x():
    return lax.axis_index("rows") // Z


def my_core():
    return lax.rem(lax.axis_index("centers"), CORES)


def chunk_of(d):
    return lax.rem(my_x() + X - d, X)


def spot(z, rows):
    top, left = z // 4 * rows, z % 4 * PART
    return slice(top, top + rows), left


def dot(a, b):
    return jnp.dot(a, b, preferred_element_type=F32)


def dot_nt(a, b):
    return lax.dot_general(a, b, (((1,), (1,)), ((), ())), preferred_element_type=F32)


def select_kernel(feat_ref, index_ref, out_ref):
    rows = feat_ref.shape[1]
    first = lax.axis_index("rows") * rows
    half = FPAD // 2

    @pl.loop(0, X)
    def _(c):
        wanted = index_ref[:, pl.ds(pl.multiple_of(c * CHUNK, CHUNK), CHUNK)] - first
        hot = lax.broadcasted_iota(jnp.int32, (rows, CHUNK), 0) == wanted
        got = dot(feat_ref[...], jnp.where(hot, 1.0, 0.0).astype(BF16))
        got = jnp.concatenate([got, jnp.zeros((FPAD - FEAT, CHUNK), F32)], axis=0).astype(BF16)
        for z in range(Z):
            height, left = spot(z, half)
            out_ref[c * Z + z] = got[height, left : left + PART]


def sum_kernel(in_ref, out_ref):
    total = in_ref[0].astype(F32)
    for i in range(1, in_ref.shape[0]):
        total = total + in_ref[i].astype(F32)
    total = total.astype(BF16)
    for i in range(out_ref.shape[0]):
        out_ref[i] = total


def split_halves(own_ref, keep_ref, send_ref):
    core = my_core()
    width = keep_ref.shape[1]
    keep_ref[...] = own_ref[:WIRE, pl.ds(pl.multiple_of(core * width, width), width)]
    send_ref[...] = own_ref[:WIRE, pl.ds(pl.multiple_of((1 - core) * width, width), width)]


def own_scores(low_ref, kern_ref, own_ref):
    @pl.loop(0, kern_ref.shape[0] // BLOCK)
    def _(n):
        at = pl.ds(pl.multiple_of(n * BLOCK, BLOCK), BLOCK)
        own_ref[:, at] = dot_nt(low_ref[...], kern_ref[at, :])


def build_kernel(
    feat_ref, norm_ref, c0, c1, c2, c3, warm_ref,
    kern_ref, coef_ref, own_ref, keep_ref, send_ref, cent_ref, low_ref,
):
    scale = LOG2E / FEAT
    half = FPAD // 2
    norms = []
    for d, c_ref in enumerate((c0, c1, c2, c3)):
        for z in range(Z):
            height, left = spot(z, half)
            left += d * CHUNK
            cent_ref[height, left : left + PART] = c_ref[z]
        cols = slice(d * CHUNK, (d + 1) * CHUNK)
        norms.append(
            jnp.sum(jnp.square(cent_ref[:, cols].astype(F32)), axis=0, keepdims=True) * scale
        )
        warm = warm_ref[:, pl.ds(pl.multiple_of(chunk_of(d) * CHUNK, CHUNK), CHUNK)]
        warm = jnp.concatenate([warm, jnp.zeros((PAD - CLASSES, CHUNK), F32)], axis=0)
        coef_ref[:, cols] = warm
        low_ref[:, cols] = warm.astype(BF16)

    @pl.loop(0, kern_ref.shape[0] // BLOCK)
    def _(n):
        at = pl.ds(pl.multiple_of(n * BLOCK, BLOCK), BLOCK)
        feats = feat_ref[at, :]
        row_norm = norm_ref[at, :] * scale
        for d in range(X):
            cols = slice(d * CHUNK, (d + 1) * CHUNK)
            cross = dot(feats, cent_ref[:, cols])
            kern_ref[at, cols] = jnp.exp2(cross * (2.0 * scale) - norms[d] - row_norm).astype(BF16)

    own_scores(low_ref, kern_ref, own_ref)
    split_halves(own_ref, keep_ref, send_ref)


def residual_of(logits, labels):
    classes = lax.broadcasted_iota(jnp.int32, logits.shape, 0)
    logits = jnp.where(classes < CLASSES, logits, -1e30)
    raised = jnp.exp(logits - jnp.max(logits, axis=0, keepdims=True))
    prob = raised / jnp.sum(raised, axis=0, keepdims=True)
    return (prob - jnp.where(classes == labels, 1.0, 0.0)).astype(BF16)


def gradient_pieces(res_ref, kern_ref, out_ref):
    half = PAD // 2

    @pl.loop(0, X)
    def _(d):
        cols = pl.ds(pl.multiple_of(d * CHUNK, CHUNK), CHUNK)
        grad = dot(res_ref[...], kern_ref[:, cols]).astype(BF16)
        for z in range(Z):
            height, left = spot(z, half)
            out_ref[chunk_of(d) * Z + z] = grad[height, left : left + PART]


def first_kernel(mine_ref, theirs_ref, own_ref, kern_ref, label_ref, out_ref, base_ref, res_ref, sum_ref):
    core = my_core()
    width = mine_ref.shape[1]
    sum_ref[:WIRE, pl.ds(pl.multiple_of(core * width, width), width)] = mine_ref[...]
    sum_ref[:WIRE, pl.ds(pl.multiple_of((1 - core) * width, width), width)] = theirs_ref[...]
    for n in range(sum_ref.shape[1] // BLOCK):
        at = slice(n * BLOCK, (n + 1) * BLOCK)
        res_ref[:, at] = residual_of(sum_ref[:, at], label_ref[:, at])
    base_ref[...] = sum_ref[...] - own_ref[...]
    gradient_pieces(res_ref, kern_ref, out_ref)


def update(coef_ref, grads, new_ref, low_ref):
    half = PAD // 2
    for d, g_ref in enumerate(grads):
        for z in range(Z):
            height, left = spot(z, half)
            cols = slice(d * CHUNK + left, d * CHUNK + left + PART)
            fresh = coef_ref[height, cols] - STEP * g_ref[z].astype(F32)
            new_ref[height, cols] = fresh
            low_ref[height, cols] = fresh.astype(BF16)


def second_kernel(coef_ref, g0, g1, g2, g3, base_ref, kern_ref, label_ref, out_ref, new_ref, res_ref, low_ref):
    update(coef_ref, (g0, g1, g2, g3), new_ref, low_ref)

    @pl.loop(0, kern_ref.shape[0] // BLOCK)
    def _(n):
        at = pl.ds(pl.multiple_of(n * BLOCK, BLOCK), BLOCK)
        logits = base_ref[:, at] + dot_nt(low_ref[...], kern_ref[at, :])
        res_ref[:, at] = residual_of(logits, label_ref[:, at])

    gradient_pieces(res_ref, kern_ref, out_ref)


def score_kernel(coef_ref, g0, g1, g2, g3, kern_ref, new_ref, own_ref, keep_ref, send_ref, low_ref):
    update(coef_ref, (g0, g1, g2, g3), new_ref, low_ref)
    own_scores(low_ref, kern_ref, own_ref)
    split_halves(own_ref, keep_ref, send_ref)


def final_kernel(coef_ref, g0, g1, g2, g3, kern_ref, coef_out_ref, keep_ref, send_ref, new_ref, low_ref, own_ref):
    update(coef_ref, (g0, g1, g2, g3), new_ref, low_ref)
    for d in range(X):
        cols = slice(d * CHUNK, (d + 1) * CHUNK)
        to = pl.ds(pl.multiple_of(chunk_of(d) * CHUNK, CHUNK), CHUNK)
        coef_out_ref[:, to] = new_ref[:CLASSES, cols]
    own_scores(low_ref, kern_ref, own_ref)
    core = my_core()
    for y in range(Y):
        for ref, k in ((keep_ref, core), (send_ref, 1 - core)):
            ref[y] = own_ref[:WIRE, pl.ds(pl.multiple_of((y * CORES + k) * LANES, LANES), LANES)]


def exchange(value, axis, groups=None):
    return lax.all_to_all(
        value, axis, split_axis=0, concat_axis=0, tiled=True, axis_index_groups=groups
    )


def sum_and_gather(pieces):
    arrived = exchange(pieces, "rows")
    copies = call(sum_kernel, like((Z, *pieces.shape[1:]), BF16), name="sum_at_owner")(arrived)
    mine = exchange(copies, "rows", Z_GROUPS)
    return [mine] + [lax.ppermute(mine, "rows", x_shift(d)) for d in range(1, X)]


def sum_over_groups(keep, send):
    half = keep + lax.ppermute(send, "centers", CORE_SWAP)
    half = exchange(jnp.broadcast_to(half, (Y, *half.shape)), "centers", Y_GROUPS).sum(axis=0)
    return half, lax.ppermute(half, "centers", CORE_SWAP)


def body(features, labels, center_index, warm_coef):
    rows = features.shape[1]
    centers = center_index.shape[1]
    labels = labels.reshape(1, rows)
    kern_type = like((rows, centers), BF16)
    coef_type = like((PAD, centers), F32)
    own_type = like((PAD, rows), F32)
    half_type = like((WIRE, rows // CORES), F32)
    last_type = like((Y, WIRE, LANES), F32)
    grad_type = like((X * Z, PAD // 2, PART), BF16)
    low = pltpu.VMEM((PAD, centers), BF16)
    res = pltpu.VMEM((PAD, rows), BF16)
    score = pltpu.VMEM((PAD, rows), F32)
    coef_scratch = pltpu.VMEM((PAD, centers), F32)

    picked = call(select_kernel, like((X * Z, FPAD // 2, PART), BF16), name="select")(
        features, center_index
    )
    row_norms = jnp.sum(jnp.square(features.astype(F32)), axis=0).reshape(rows, 1)
    feat_rows = jnp.pad(features, ((0, FPAD - FEAT), (0, 0))).T
    cents = sum_and_gather(picked)
    kern, coef, own, keep, send = call(
        build_kernel,
        [kern_type, coef_type, own_type, half_type, half_type],
        [pltpu.VMEM((FPAD, centers), BF16), low],
        name="build",
    )(feat_rows, row_norms, *cents, warm_coef)

    for round_idx in range(ROUNDS):
        mine, theirs = sum_over_groups(keep, send)
        pieces, base = call(first_kernel, [grad_type, own_type], [res, score], name="first")(
            mine, theirs, own, kern, labels
        )
        for _ in range(1, PASSES):
            grads = sum_and_gather(pieces)
            pieces, coef = call(second_kernel, [grad_type, coef_type], [res, low], name="second")(
                coef, *grads, base, kern, labels
            )
        grads = sum_and_gather(pieces)
        if round_idx < ROUNDS - 1:
            coef, own, keep, send = call(
                score_kernel, [coef_type, own_type, half_type, half_type], [low], name="scores"
            )(coef, *grads, kern)
    coef_out, keep, send = call(
        final_kernel,
        [like((CLASSES, centers), F32), last_type, last_type],
        [coef_scratch, low, score],
        name="final",
    )(coef, *grads, kern)
    part = keep + lax.ppermute(send, "centers", CORE_SWAP)
    logits_out = exchange(part, "centers", Y_GROUPS).sum(axis=0)[:CLASSES]
    return coef_out, logits_out


def solution(mesh):
    return jax.shard_map(
        body,
        mesh=mesh,
        in_specs=(P(None, "rows"), P("rows"), P("centers", None), P(None, "centers")),
        out_specs=(P(None, "centers"), P(None, ("rows", "centers"))),
        check_vma=False,
    )
```

time: 763 us -> 421 us (0.55)
  waiting for transfers between devices: 342 us -> 51.6 us
  Pallas kernels: 0 us -> 64.4 us
  matrix products: 37.4 us -> 0 us
  local copies, waits for them, and re-layouts: 41.8 us -> 7.23 us
  blocking collectives: 285 us -> 258 us
  other arithmetic: 17.9 us -> 4.15 us
  between operations: 14.2 us -> 0.76 us
  starting transfers between devices: 22.5 us -> 33.4 us
    psum x1 -> x0, waiting for transfers between devices: 154 us -> none  [body(): centers = lax.psum(picked, 'rows').astype(jnp.float32).astype(jnp.bfloat16)]
    all_to_all x3 -> x0, waiting for transfers between devices: 111 us -> none  [the longest x2 63.4 us: sent_to_all(): return lax.all_to_all(copies, axis, split_axis=0, concat_axis=0, tiled=True)]
    all_gather x2 -> x0, waiting for transfers between devices: 77.6 us -> none  [total_of_pieces(): return lax.all_gather(value, axis).sum(0)]
    pallas_call x0 -> x13, Pallas kernels: none -> 64.4 us  [call(): pl.pallas_call(kernel, out_shape=outs, in_specs=[vmem] * len(args), out_s...]
    ppermute x0 -> x20, waiting for transfers between devices: none -> 51.6 us  [the longest x15 44.8 us: sum_and_gather(): lax.ppermute(mine, 'rows', x_shift(d))]
    dot_general x13 -> x0, matrix products: 37.4 us -> none  [the longest x4 13.4 us: body(): lax.dot_general(residual, kernel, (((1,), (1,)), ((), ())), preferred_ele...]
    ppermute x0 -> x20, starting transfers between devices: none -> 33.4 us  [the longest x15 15.1 us: sum_and_gather(): lax.ppermute(mine, 'rows', x_shift(d))]
    all_to_all x7 -> x13, blocking collectives: 285 us -> 258 us  [exchange(): lax.all_to_all(value, axis, split_axis=0, concat_axis=0, tiled=True, axis...]
  transfers between devices with their start and end apart: 6 -> 20, of which waited for: 6 -> 20; matrix products, arithmetic and copies ran while one was open for 2% -> 1% of each run, Pallas kernels for 0% -> 0%
where the time goes in v1:
time: 421 us; the launch traced here: 420 us
  blocking collectives  258 us (61%)
  Pallas kernels  64.4 us (15%)
  waiting for transfers between devices  51.6 us (12%)
  starting transfers between devices  33.4 us (8%)
  local copies, waits for them, and re-layouts  7.23 us (2%)
    all_to_all x13, blocking collectives, exchange(): lax.all_to_all(value, axis, split_axis=0, concat_axis=0, tiled=True, axis...  258 us
    pallas_call x13, Pallas kernels, call(): pl.pallas_call(kernel, out_shape=outs, in_specs=[vmem] * len(args), out_s...  64.4 us
    ppermute x15, waiting for transfers between devices, sum_and_gather(): lax.ppermute(mine, 'rows', x_shift(d))  44.8 us
    ppermute x15, starting transfers between devices, sum_and_gather(): lax.ppermute(mine, 'rows', x_shift(d))  15.1 us
  transfers between devices with their start and end apart: 20, of which 20 were waited for; matrix products, arithmetic and copies ran while one was open for 1% of the time, Pallas kernels for 0%

profile of v1, /device:TPU:1, one launch (start us, length us, event | category | flops | bytes accessed | tf_op | source)
XLA Modules:
  0.0 419.7 jit_solution(14993808513366524020)
XLA Ops:
  0.6 5.0 %select.2 = bf16[32,224,128]{2,1,0:T(8,128)(2,1)} custom-call(bf16[440,1024]{1,0:T(8,128)(2,1)} %feat_ref.1, s32[1,2048]{1,0:T(1,128)} %index_ref.1), custom_call_target="tpu_custom_call" | custom-call | tf_op jit(solution)/shard_map/select/pallas_call | solution.py:40
  5.7 53.4 %all_to_all.65.in_ref = bf16[32,224,128]{2,1,0:T(8,128)(2,1)} all-to-all(bf16[32,224,128]{2,1,0:T(8,128)(2,1)} %select.2), channel_id=1, replica_groups=mesh['rows'=32,'centers'=8] {'rows'}, dimensions={0} | all-to-all | bytes 3670016 | tf_op jit(solution)/shard_map/all_to_all | solution.py:228
  59.1 2.6 sum_at_owner.5
  61.7 20.4 %all_to_all.66.c0 = bf16[8,224,128]{2,1,0:T(8,128)(2,1)S(1)} all-to-all(bf16[8,224,128]{2,1,0:T(8,128)(2,1)} %sum_at_owner.5), channel_id=1, replica_groups={{0,8,16,24,32,40,48,56},{64,72,80,88,96,104,112,120},{128,136,144,152,1..., dimensions={0} | all-to-all | bytes 917504 | tf_op jit(solution)/shard_map/all_to_all | solution.py:228
  82.1 2.1 collective-permute-start.2
  88.3 3.9 collective-permute-done.2.c3
  92.3 2.5 collective-permute-done.1.c2
  94.8 13.3 %collective-permute-done.c1 = bf16[8,224,128]{2,1,0:T(8,128)(2,1)} collective-permute-done((bf16[8,224,128]{2,1,0:T(8,128)(2,1)S(1)}, bf16[8,224,128]{2,1,0:T(8,128)(2,1)}, u32[]{:S(2)}, u32[]{:S(2)}) %collective-permute-start) | collective-permute-done | bytes 458784 | tf_op jit(solution)/shard_map/ppermute | solution.py:237
  108.1 10.4 %build.1 = (bf16[1024,2048]{1,0:T(8,128)(2,1)}, f32[160,2048]{1,0:T(8,128)}, f32[160,1024]{1,0:T(8,128)}, f32[152,512]{1,0:T(8,128)}, f32[152,512]{1,0:T(8,128)}) custom-call(bf16[1024,448]{1,0:T(8,128)(2,1)} %pad_bitcast_fusion.feat_ref, f32[1024,1]{1,0:T(8,128)} %copy.10.norm_ref, bf16[8,224,128]{2,1,0:T(8,128)(2,1)} %copy-done.1, ...), custom_call_target="tpu_custom_call" | custom-call | tf_op jit(solution)/shard_map/build/pallas_call | solution.py:40
  121.6 20.6 %all_to_all.67 = f32[4,152,512]{2,1,0:T(8,128)S(1)} all-to-all(f32[4,152,512]{2,1,0:T(8,128)S(1)} %broadcast_in_dim.6), channel_id=1, replica_groups={{0,2,4,6},{1,3,5,7},{8,10,12,14},{9,11,13,15},{16,18,20,22},{17,19,21,2..., dimensions={0} | all-to-all | bytes 2490368 | tf_op jit(solution)/shard_map/all_to_all | solution.py:228
  145.9 5.2 %first.2 = (bf16[32,80,128]{2,1,0:T(8,128)(2,1)}, f32[160,1024]{1,0:T(8,128)}) custom-call(f32[152,512]{1,0:T(8,128)} %copy-done.2, f32[152,512]{1,0:T(8,128)} %copy-done.10, f32[160,1024]{1,0:T(8,128)} %get-tuple-element.25.own_ref, bf16[1024,2048]{1,0:T(8,128)(2,1)} %get-tuple-element.26.kern_ref, s32[1,1024]{1,0:T(1,128)} %bitcast.6), custom_call_target="tpu_custom_call" | custom-call | tf_op jit(solution)/shard_map/first/pallas_call | solution.py:40
  151.2 21.3 %all_to_all.68.in_ref = bf16[32,80,128]{2,1,0:T(8,128)(2,1)} all-to-all(bf16[32,80,128]{2,1,0:T(8,128)(2,1)} %get-tuple-element.27), channel_id=1, replica_groups=mesh['rows'=32,'centers'=8] {'rows'}, dimensions={0} | all-to-all | bytes 1310720 | tf_op jit(solution)/shard_map/all_to_all | solution.py:228
  174.3 14.5 %all_to_all.69.g0 = bf16[8,80,128]{2,1,0:T(8,128)(2,1)S(1)} all-to-all(bf16[8,80,128]{2,1,0:T(8,128)(2,1)} %sum_at_owner.6), channel_id=1, replica_groups={{0,8,16,24,32,40,48,56},{64,72,80,88,96,104,112,120},{128,136,144,152,1..., dimensions={0} | all-to-all | bytes 327680 | tf_op jit(solution)/shard_map/all_to_all | solution.py:228
  193.0 2.9 collective-permute-done.6.g2
  198.6 8.1 %second.2 = (bf16[32,80,128]{2,1,0:T(8,128)(2,1)}, f32[160,2048]{1,0:T(8,128)}) custom-call(f32[160,2048]{1,0:T(8,128)} %get-tuple-element.22.coef_ref, bf16[8,80,128]{2,1,0:T(8,128)(2,1)} %copy-done.4, bf16[8,80,128]{2,1,0:T(8,128)(2,1)} %copy-done.20, bf16[8,80,128]{2,1,0:T(8,128)(2,1)} %copy-done.16, bf16[8,80,128]{2,1,0:T(8,128)(2,1)} %copy-done.12, ...), custom_call_target="tpu_custom_call" | custom-call | tf_op jit(solution)/shard_map/second/pallas_call | solution.py:40
  206.7 18.5 %all_to_all.70.in_ref = bf16[32,80,128]{2,1,0:T(8,128)(2,1)} all-to-all(bf16[32,80,128]{2,1,0:T(8,128)(2,1)} %get-tuple-element.30), channel_id=1, replica_groups=mesh['rows'=32,'centers'=8] {'rows'}, dimensions={0} | all-to-all | bytes 1310720 | tf_op jit(solution)/shard_map/all_to_all | solution.py:228
  227.0 13.6 %all_to_all.71.g0 = bf16[8,80,128]{2,1,0:T(8,128)(2,1)S(1)} all-to-all(bf16[8,80,128]{2,1,0:T(8,128)(2,1)} %sum_at_owner.7), channel_id=1, replica_groups={{0,8,16,24,32,40,48,56},{64,72,80,88,96,104,112,120},{128,136,144,152,1..., dimensions={0} | all-to-all | bytes 327680 | tf_op jit(solution)/shard_map/all_to_all | solution.py:228
  243.8 2.7 collective-permute-done.10.g3
  250.6 6.2 %scores.1 = (f32[160,2048]{1,0:T(8,128)}, f32[160,1024]{1,0:T(8,128)}, f32[152,512]{1,0:T(8,128)}, f32[152,512]{1,0:T(8,128)}) custom-call(f32[160,2048]{1,0:T(8,128)} %get-tuple-element.29.coef_ref, bf16[8,80,128]{2,1,0:T(8,128)(2,1)} %copy-done.5, bf16[8,80,128]{2,1,0:T(8,128)(2,1)} %copy-done.21, bf16[8,80,128]{2,1,0:T(8,128)(2,1)} %copy-done.17, ...), custom_call_target="tpu_custom_call" | custom-call | tf_op jit(solution)/shard_map/scores/pallas_call | solution.py:40
  256.8 7.3 %collective-permute-start.11 = (f32[152,512]{1,0:T(8,128)}, f32[152,512]{1,0:T(8,128)S(1)}, u32[]{:S(2)}, u32[]{:S(2)}) collective-permute-start(f32[152,512]{1,0:T(8,128)} %get-tuple-element.33), channel_id=1, source_target_pairs={{0,1},{1,0},{2,3},{3,2},{4,5},{5,4},{6,7},{7,6},{8,9},{9,8},{10,11... | collective-permute-start | bytes 933896 | tf_op jit(solution)/shard_map/ppermute | solution.py:241
  266.7 19.1 %all_to_all.72 = f32[4,152,512]{2,1,0:T(8,128)S(1)} all-to-all(f32[4,152,512]{2,1,0:T(8,128)S(1)} %broadcast_in_dim.7), channel_id=1, replica_groups={{0,2,4,6},{1,3,5,7},{8,10,12,14},{9,11,13,15},{16,18,20,22},{17,19,21,2..., dimensions={0} | all-to-all | bytes 2490368 | tf_op jit(solution)/shard_map/all_to_all | solution.py:228
  289.4 5.2 %first.3 = (bf16[32,80,128]{2,1,0:T(8,128)(2,1)}, f32[160,1024]{1,0:T(8,128)}) custom-call(f32[152,512]{1,0:T(8,128)} %copy-done.3, f32[152,512]{1,0:T(8,128)} %copy-done.11, f32[160,1024]{1,0:T(8,128)} %get-tuple-element.34.own_ref, bf16[1024,2048]{1,0:T(8,128)(2,1)} %get-tuple-element.26.kern_ref, s32[1,1024]{1,0:T(1,128)} %bitcast.8), custom_call_target="tpu_custom_call" | custom-call | tf_op jit(solution)/shard_map/first/pallas_call | solution.py:40
  294.7 21.3 %all_to_all.73.in_ref = bf16[32,80,128]{2,1,0:T(8,128)(2,1)} all-to-all(bf16[32,80,128]{2,1,0:T(8,128)(2,1)} %get-tuple-element.35), channel_id=1, replica_groups=mesh['rows'=32,'centers'=8] {'rows'}, dimensions={0} | all-to-all | bytes 1310720 | tf_op jit(solution)/shard_map/all_to_all | solution.py:228
  317.8 14.5 %all_to_all.74.g0 = bf16[8,80,128]{2,1,0:T(8,128)(2,1)S(1)} all-to-all(bf16[8,80,128]{2,1,0:T(8,128)(2,1)} %sum_at_owner.8), channel_id=1, replica_groups={{0,8,16,24,32,40,48,56},{64,72,80,88,96,104,112,120},{128,136,144,152,1..., dimensions={0} | all-to-all | bytes 327680 | tf_op jit(solution)/shard_map/all_to_all | solution.py:228
  336.5 2.9 collective-permute-done.14.g2
  342.1 8.1 %second.3 = (bf16[32,80,128]{2,1,0:T(8,128)(2,1)}, f32[160,2048]{1,0:T(8,128)}) custom-call(f32[160,2048]{1,0:T(8,128)} %get-tuple-element.31.coef_ref, bf16[8,80,128]{2,1,0:T(8,128)(2,1)} %copy-done.6, bf16[8,80,128]{2,1,0:T(8,128)(2,1)} %copy-done.22, bf16[8,80,128]{2,1,0:T(8,128)(2,1)} %copy-done.18, bf16[8,80,128]{2,1,0:T(8,128)(2,1)} %copy-done.14, ...), custom_call_target="tpu_custom_call" | custom-call | tf_op jit(solution)/shard_map/second/pallas_call | solution.py:40
  350.2 18.5 %all_to_all.75.in_ref = bf16[32,80,128]{2,1,0:T(8,128)(2,1)} all-to-all(bf16[32,80,128]{2,1,0:T(8,128)(2,1)} %get-tuple-element.38), channel_id=1, replica_groups=mesh['rows'=32,'centers'=8] {'rows'}, dimensions={0} | all-to-all | bytes 1310720 | tf_op jit(solution)/shard_map/all_to_all | solution.py:228
  370.5 13.6 %all_to_all.76.g0 = bf16[8,80,128]{2,1,0:T(8,128)(2,1)S(1)} all-to-all(bf16[8,80,128]{2,1,0:T(8,128)(2,1)} %sum_at_owner.9), channel_id=1, replica_groups={{0,8,16,24,32,40,48,56},{64,72,80,88,96,104,112,120},{128,136,144,152,1..., dimensions={0} | all-to-all | bytes 327680 | tf_op jit(solution)/shard_map/all_to_all | solution.py:228
  387.3 2.7 collective-permute-done.18.g3
  394.1 6.2 %final.1 = (f32[147,2048]{1,0:T(8,128)}, f32[4,152,128]{2,1,0:T(8,128)}, f32[4,152,128]{2,1,0:T(8,128)}) custom-call(f32[160,2048]{1,0:T(8,128)} %get-tuple-element.37.coef_ref, bf16[8,80,128]{2,1,0:T(8,128)(2,1)} %copy-done.7, bf16[8,80,128]{2,1,0:T(8,128)(2,1)} %copy-done.23, bf16[8,80,128]{2,1,0:T(8,128)(2,1)} %copy-done.19, ...), custom_call_target="tpu_custom_call" | custom-call | tf_op jit(solution)/shard_map/final/pallas_call | solution.py:40
  400.2 7.3 %collective-permute-start.19 = (f32[4,152,128]{2,1,0:T(8,128)}, f32[4,152,128]{2,1,0:T(8,128)S(1)}, u32[]{:S(2)}, u32[]{:S(2)}) collective-permute-start(f32[4,152,128]{2,1,0:T(8,128)} %get-tuple-element.41), channel_id=1, source_target_pairs={{0,1},{1,0},{2,3},{3,2},{4,5},{5,4},{6,7},{7,6},{8,9},{9,8},{10,11... | collective-permute-start | bytes 933896 | tf_op jit(solution)/shard_map/ppermute | solution.py:295
  410.0 9.0 %all_to_all.77 = f32[4,152,128]{2,1,0:T(8,128)S(1)} all-to-all(f32[4,152,128]{2,1,0:T(8,128)S(1)} %add.13), channel_id=1, replica_groups={{0,2,4,6},{1,3,5,7},{8,10,12,14},{9,11,13,15},{16,18,20,22},{17,19,21,2..., dimensions={0} | all-to-all | bytes 622592 | tf_op jit(solution)/shard_map/all_to_all | solution.py:228
  (94 shorter events, 56.3 us)
Async XLA Ops:
  59.1 26.3 %copy-start = (bf16[440,1024]{1,0:T(8,128)(2,1)S(1)}, bf16[440,1024]{1,0:T(8,128)(2,1)}, u32[]{:S(2)}) copy-start(bf16[440,1024]{1,0:T(8,128)(2,1)} %feat_ref.1) | copy-start | bytes 2703364
  82.1 4.1 copy-start.1
  82.1 10.2 %collective-permute-start.2 = (bf16[8,224,128]{2,1,0:T(8,128)(2,1)S(1)}, bf16[8,224,128]{2,1,0:T(8,128)(2,1)S(1)}, u32[]{:S(2)}, u32[]{:S(2)}) collective-permute-start(bf16[8,224,128]{2,1,0:T(8,128)(2,1)S(1)} %all_to_all.66.c0), channel_id=1, source_target_pairs={{0,192},{8,200},{16,208},{24,216},{32,224},{40,232},{48,240},{56,2... | collective-permute-start | bytes 1376264 | tf_op jit(solution)/shard_map/ppermute | solution.py:237
  84.2 10.6 %collective-permute-start.1 = (bf16[8,224,128]{2,1,0:T(8,128)(2,1)S(1)}, bf16[8,224,128]{2,1,0:T(8,128)(2,1)S(1)}, u32[]{:S(2)}, u32[]{:S(2)}) collective-permute-start(bf16[8,224,128]{2,1,0:T(8,128)(2,1)S(1)} %all_to_all.66.c0), channel_id=1, source_target_pairs={{0,128},{8,136},{16,144},{24,152},{32,160},{40,168},{48,176},{56,1... | collective-permute-start | bytes 1376264 | tf_op jit(solution)/shard_map/ppermute | solution.py:237
  85.1 22.9 %collective-permute-start = (bf16[8,224,128]{2,1,0:T(8,128)(2,1)S(1)}, bf16[8,224,128]{2,1,0:T(8,128)(2,1)}, u32[]{:S(2)}, u32[]{:S(2)}) collective-permute-start(bf16[8,224,128]{2,1,0:T(8,128)(2,1)S(1)} %all_to_all.66.c0), channel_id=1, source_target_pairs={{0,64},{8,72},{16,80},{24,88},{32,96},{40,104},{48,112},{56,120},{... | collective-permute-start | bytes 1376264 | tf_op jit(solution)/shard_map/ppermute | solution.py:237
  92.3 15.8 %copy-start.8 = (bf16[8,224,128]{2,1,0:T(8,128)(2,1)}, bf16[8,224,128]{2,1,0:T(8,128)(2,1)S(1)}, u32[]{:S(2)}) copy-start(bf16[8,224,128]{2,1,0:T(8,128)(2,1)S(1)} %collective-permute-done.2.c3) | copy-start | bytes 1376260
  94.8 13.3 %copy-start.9 = (bf16[8,224,128]{2,1,0:T(8,128)(2,1)}, bf16[8,224,128]{2,1,0:T(8,128)(2,1)S(1)}, u32[]{:S(2)}) copy-start(bf16[8,224,128]{2,1,0:T(8,128)(2,1)S(1)} %collective-permute-done.1.c2) | copy-start | bytes 1376260
  118.5 1.9 collective-permute-start.3
  142.4 2.8 collective-permute-start.4
  188.8 9.1 %copy-start.4 = (bf16[8,80,128]{2,1,0:T(8,128)(2,1)}, bf16[8,80,128]{2,1,0:T(8,128)(2,1)S(1)}, u32[]{:S(2)}) copy-start(bf16[8,80,128]{2,1,0:T(8,128)(2,1)S(1)} %all_to_all.69.g0) | copy-start | bytes 491524
  188.8 4.2 collective-permute-start.7
  190.1 5.8 %collective-permute-start.6 = (bf16[8,80,128]{2,1,0:T(8,128)(2,1)S(1)}, bf16[8,80,128]{2,1,0:T(8,128)(2,1)S(1)}, u32[]{:S(2)}, u32[]{:S(2)}) collective-permute-start(bf16[8,80,128]{2,1,0:T(8,128)(2,1)S(1)} %all_to_all.69.g0), channel_id=1, source_target_pairs={{0,128},{8,136},{16,144},{24,152},{32,160},{40,168},{48,176},{56,1... | collective-permute-start | bytes 491528 | tf_op jit(solution)/shard_map/ppermute | solution.py:237
  191.4 6.5 %collective-permute-start.5 = (bf16[8,80,128]{2,1,0:T(8,128)(2,1)S(1)}, bf16[8,80,128]{2,1,0:T(8,128)(2,1)S(1)}, u32[]{:S(2)}, u32[]{:S(2)}) collective-permute-start(bf16[8,80,128]{2,1,0:T(8,128)(2,1)S(1)} %all_to_all.69.g0), channel_id=1, source_target_pairs={{0,64},{8,72},{16,80},{24,88},{32,96},{40,104},{48,112},{56,120},{... | collective-permute-start | bytes 491528 | tf_op jit(solution)/shard_map/ppermute | solution.py:237
  193.0 4.9 %copy-start.12 = (bf16[8,80,128]{2,1,0:T(8,128)(2,1)}, bf16[8,80,128]{2,1,0:T(8,128)(2,1)S(1)}, u32[]{:S(2)}) copy-start(bf16[8,80,128]{2,1,0:T(8,128)(2,1)S(1)} %collective-permute-done.7.g3) | copy-start | bytes 491524
  240.6 9.4 %copy-start.5 = (bf16[8,80,128]{2,1,0:T(8,128)(2,1)}, bf16[8,80,128]{2,1,0:T(8,128)(2,1)S(1)}, u32[]{:S(2)}) copy-start(bf16[8,80,128]{2,1,0:T(8,128)(2,1)S(1)} %all_to_all.71.g0) | copy-start | bytes 491524
  240.6 5.9 %collective-permute-start.10 = (bf16[8,80,128]{2,1,0:T(8,128)(2,1)S(1)}, bf16[8,80,128]{2,1,0:T(8,128)(2,1)S(1)}, u32[]{:S(2)}, u32[]{:S(2)}) collective-permute-start(bf16[8,80,128]{2,1,0:T(8,128)(2,1)S(1)} %all_to_all.71.g0), channel_id=1, source_target_pairs={{0,192},{8,200},{16,208},{24,216},{32,224},{40,232},{48,240},{56,2... | collective-permute-start | bytes 491528 | tf_op jit(solution)/shard_map/ppermute | solution.py:237
  242.5 5.8 %collective-permute-start.9 = (bf16[8,80,128]{2,1,0:T(8,128)(2,1)S(1)}, bf16[8,80,128]{2,1,0:T(8,128)(2,1)S(1)}, u32[]{:S(2)}, u32[]{:S(2)}) collective-permute-start(bf16[8,80,128]{2,1,0:T(8,128)(2,1)S(1)} %all_to_all.71.g0), channel_id=1, source_target_pairs={{0,128},{8,136},{16,144},{24,152},{32,160},{40,168},{48,176},{56,1... | collective-permute-start | bytes 491528 | tf_op jit(solution)/shard_map/ppermute | solution.py:237
  243.5 6.4 %collective-permute-start.8 = (bf16[8,80,128]{2,1,0:T(8,128)(2,1)S(1)}, bf16[8,80,128]{2,1,0:T(8,128)(2,1)S(1)}, u32[]{:S(2)}, u32[]{:S(2)}) collective-permute-start(bf16[8,80,128]{2,1,0:T(8,128)(2,1)S(1)} %all_to_all.71.g0), channel_id=1, source_target_pairs={{0,64},{8,72},{16,80},{24,88},{32,96},{40,104},{48,112},{56,120},{... | collective-permute-start | bytes 491528 | tf_op jit(solution)/shard_map/ppermute | solution.py:237
  246.5 3.4 copy-start.13
  256.8 8.7 %collective-permute-start.11 = (f32[152,512]{1,0:T(8,128)}, f32[152,512]{1,0:T(8,128)S(1)}, u32[]{:S(2)}, u32[]{:S(2)}) collective-permute-start(f32[152,512]{1,0:T(8,128)} %get-tuple-element.33), channel_id=1, source_target_pairs={{0,1},{1,0},{2,3},{3,2},{4,5},{5,4},{6,7},{7,6},{8,9},{9,8},{10,11... | collective-permute-start | bytes 933896 | tf_op jit(solution)/shard_map/ppermute | solution.py:241
  285.9 2.8 collective-permute-start.12
  332.3 9.1 %copy-start.6 = (bf16[8,80,128]{2,1,0:T(8,128)(2,1)}, bf16[8,80,128]{2,1,0:T(8,128)(2,1)S(1)}, u32[]{:S(2)}) copy-start(bf16[8,80,128]{2,1,0:T(8,128)(2,1)S(1)} %all_to_all.74.g0) | copy-start | bytes 491524
  332.3 4.2 collective-permute-start.15
  333.6 5.8 %collective-permute-start.14 = (bf16[8,80,128]{2,1,0:T(8,128)(2,1)S(1)}, bf16[8,80,128]{2,1,0:T(8,128)(2,1)S(1)}, u32[]{:S(2)}, u32[]{:S(2)}) collective-permute-start(bf16[8,80,128]{2,1,0:T(8,128)(2,1)S(1)} %all_to_all.74.g0), channel_id=1, source_target_pairs={{0,128},{8,136},{16,144},{24,152},{32,160},{40,168},{48,176},{56,1... | collective-permute-start | bytes 491528 | tf_op jit(solution)/shard_map/ppermute | solution.py:237
  334.9 6.5 %collective-permute-start.13 = (bf16[8,80,128]{2,1,0:T(8,128)(2,1)S(1)}, bf16[8,80,128]{2,1,0:T(8,128)(2,1)S(1)}, u32[]{:S(2)}, u32[]{:S(2)}) collective-permute-start(bf16[8,80,128]{2,1,0:T(8,128)(2,1)S(1)} %all_to_all.74.g0), channel_id=1, source_target_pairs={{0,64},{8,72},{16,80},{24,88},{32,96},{40,104},{48,112},{56,120},{... | collective-permute-start | bytes 491528 | tf_op jit(solution)/shard_map/ppermute | solution.py:237
  336.5 4.9 %copy-start.14 = (bf16[8,80,128]{2,1,0:T(8,128)(2,1)}, bf16[8,80,128]{2,1,0:T(8,128)(2,1)S(1)}, u32[]{:S(2)}) copy-start(bf16[8,80,128]{2,1,0:T(8,128)(2,1)S(1)} %collective-permute-done.15.g3) | copy-start | bytes 491524
  384.1 9.4 %copy-start.7 = (bf16[8,80,128]{2,1,0:T(8,128)(2,1)}, bf16[8,80,128]{2,1,0:T(8,128)(2,1)S(1)}, u32[]{:S(2)}) copy-start(bf16[8,80,128]{2,1,0:T(8,128)(2,1)S(1)} %all_to_all.76.g0) | copy-start | bytes 491524
  384.1 5.9 %collective-permute-start.18 = (bf16[8,80,128]{2,1,0:T(8,128)(2,1)S(1)}, bf16[8,80,128]{2,1,0:T(8,128)(2,1)S(1)}, u32[]{:S(2)}, u32[]{:S(2)}) collective-permute-start(bf16[8,80,128]{2,1,0:T(8,128)(2,1)S(1)} %all_to_all.76.g0), channel_id=1, source_target_pairs={{0,192},{8,200},{16,208},{24,216},{32,224},{40,232},{48,240},{56,2... | collective-permute-start | bytes 491528 | tf_op jit(solution)/shard_map/ppermute | solution.py:237
  386.0 5.8 %collective-permute-start.17 = (bf16[8,80,128]{2,1,0:T(8,128)(2,1)S(1)}, bf16[8,80,128]{2,1,0:T(8,128)(2,1)S(1)}, u32[]{:S(2)}, u32[]{:S(2)}) collective-permute-start(bf16[8,80,128]{2,1,0:T(8,128)(2,1)S(1)} %all_to_all.76.g0), channel_id=1, source_target_pairs={{0,128},{8,136},{16,144},{24,152},{32,160},{40,168},{48,176},{56,1... | collective-permute-start | bytes 491528 | tf_op jit(solution)/shard_map/ppermute | solution.py:237
  387.0 6.4 %collective-permute-start.16 = (bf16[8,80,128]{2,1,0:T(8,128)(2,1)S(1)}, bf16[8,80,128]{2,1,0:T(8,128)(2,1)S(1)}, u32[]{:S(2)}, u32[]{:S(2)}) collective-permute-start(bf16[8,80,128]{2,1,0:T(8,128)(2,1)S(1)} %all_to_all.76.g0), channel_id=1, source_target_pairs={{0,64},{8,72},{16,80},{24,88},{32,96},{40,104},{48,112},{56,120},{... | collective-permute-start | bytes 491528 | tf_op jit(solution)/shard_map/ppermute | solution.py:237
  390.0 3.4 copy-start.15
  400.2 8.7 %collective-permute-start.19 = (f32[4,152,128]{2,1,0:T(8,128)}, f32[4,152,128]{2,1,0:T(8,128)S(1)}, u32[]{:S(2)}, u32[]{:S(2)}) collective-permute-start(f32[4,152,128]{2,1,0:T(8,128)} %get-tuple-element.41), channel_id=1, source_target_pairs={{0,1},{1,0},{2,3},{3,2},{4,5},{5,4},{6,7},{7,6},{8,9},{9,8},{10,11... | collective-permute-start | bytes 933896 | tf_op jit(solution)/shard_map/ppermute | solution.py:295
  (12 other events, 17.4 us)

commit v2 on v1

--- a/solution.py
+++ b/solution.py
@@ -19,6 +19,8 @@
 CHUNK = X * LANES
 PART = CHUNK // 4
 BLOCK = 256
+GRANT = 20 * 2**20
+FLOPS = 2**30
 
 F32 = jnp.float32
 BF16 = jnp.bfloat16
@@ -32,6 +34,10 @@
 
 def x_shift(d):
     return [(x * Z + z, (x + d) % X * Z + z) for x in range(X) for z in range(Z)]
+
+
+def y_shift(d):
+    return [(y * CORES + k, (y + d) % Y * CORES + k) for y in range(Y) for k in range(CORES)]
 
 
 def call(kernel, outs, scratch=(), name=None):
@@ -43,6 +49,8 @@
         in_specs=[vmem] * len(args),
         out_specs=[vmem] * len(outs) if many else vmem,
         scratch_shapes=list(scratch),
+        compiler_params=pltpu.CompilerParams(vmem_limit_bytes=GRANT),
+        cost_estimate=pl.CostEstimate(flops=FLOPS, bytes_accessed=2**22, transcendentals=0),
         name=name,
     )(*args)
 
@@ -115,37 +123,38 @@
         own_ref[:, at] = dot_nt(low_ref[...], kern_ref[at, :])
 
 
+def kernel_columns(feat_ref, norm_ref, c_ref, cent_ref, kern_ref, left):
+    scale = LOG2E / FEAT
+    for z in range(Z):
+        height, at = spot(z, FPAD // 2)
+        cent_ref[height, at : at + PART] = c_ref[z]
+    center_norm = jnp.sum(jnp.square(cent_ref[...].astype(F32)), axis=0, keepdims=True) * scale
+
+    @pl.loop(0, kern_ref.shape[0] // BLOCK)
+    def _(n):
+        at = pl.ds(pl.multiple_of(n * BLOCK, BLOCK), BLOCK)
+        cross = dot(feat_ref[at, :], cent_ref[...])
+        power = cross * (2.0 * scale) - center_norm - norm_ref[at, :] * scale
+        kern_ref[at, left : left + CHUNK] = jnp.exp2(power).astype(BF16)
+
+
+def chunk_kernel(feat_ref, norm_ref, c_ref, kern_ref, cent_ref):
+    kernel_columns(feat_ref, norm_ref, c_ref, cent_ref, kern_ref, 0)
+
+
 def build_kernel(
-    feat_ref, norm_ref, c0, c1, c2, c3, warm_ref,
+    feat_ref, norm_ref, c_ref, k0, k2, k3, warm_ref,
     kern_ref, coef_ref, own_ref, keep_ref, send_ref, cent_ref, low_ref,
 ):
-    scale = LOG2E / FEAT
-    half = FPAD // 2
-    norms = []
-    for d, c_ref in enumerate((c0, c1, c2, c3)):
-        for z in range(Z):
-            height, left = spot(z, half)
-            left += d * CHUNK
-            cent_ref[height, left : left + PART] = c_ref[z]
+    for d, k_ref in ((0, k0), (2, k2), (3, k3)):
+        kern_ref[:, d * CHUNK : (d + 1) * CHUNK] = k_ref[...]
+    for d in range(X):
         cols = slice(d * CHUNK, (d + 1) * CHUNK)
-        norms.append(
-            jnp.sum(jnp.square(cent_ref[:, cols].astype(F32)), axis=0, keepdims=True) * scale
-        )
         warm = warm_ref[:, pl.ds(pl.multiple_of(chunk_of(d) * CHUNK, CHUNK), CHUNK)]
         warm = jnp.concatenate([warm, jnp.zeros((PAD - CLASSES, CHUNK), F32)], axis=0)
         coef_ref[:, cols] = warm
         low_ref[:, cols] = warm.astype(BF16)
-
-    @pl.loop(0, kern_ref.shape[0] // BLOCK)
-    def _(n):
-        at = pl.ds(pl.multiple_of(n * BLOCK, BLOCK), BLOCK)
-        feats = feat_ref[at, :]
-        row_norm = norm_ref[at, :] * scale
-        for d in range(X):
-            cols = slice(d * CHUNK, (d + 1) * CHUNK)
-            cross = dot(feats, cent_ref[:, cols])
-            kern_ref[at, cols] = jnp.exp2(cross * (2.0 * scale) - norms[d] - row_norm).astype(BF16)
-
+    kernel_columns(feat_ref, norm_ref, c_ref, cent_ref, kern_ref, CHUNK)
     own_scores(low_ref, kern_ref, own_ref)
     split_halves(own_ref, keep_ref, send_ref)
 
@@ -239,7 +248,8 @@
 
 def sum_over_groups(keep, send):
     half = keep + lax.ppermute(send, "centers", CORE_SWAP)
-    half = exchange(jnp.broadcast_to(half, (Y, *half.shape)), "centers", Y_GROUPS).sum(axis=0)
+    others = [lax.ppermute(half, "centers", y_shift(d)) for d in (2, 1, 3)]
+    half = half + others[0] + (others[1] + others[2])
     return half, lax.ppermute(half, "centers", CORE_SWAP)
 
 
@@ -264,12 +274,16 @@
     row_norms = jnp.sum(jnp.square(features.astype(F32)), axis=0).reshape(rows, 1)
     feat_rows = jnp.pad(features, ((0, FPAD - FEAT), (0, 0))).T
     cents = sum_and_gather(picked)
+    build_chunk = call(
+        chunk_kernel, like((rows, CHUNK), BF16), [pltpu.VMEM((FPAD, CHUNK), BF16)], name="chunk"
+    )
+    chunks = [build_chunk(feat_rows, row_norms, cents[d]) for d in (0, 2, 3)]
     kern, coef, own, keep, send = call(
         build_kernel,
         [kern_type, coef_type, own_type, half_type, half_type],
-        [pltpu.VMEM((FPAD, centers), BF16), low],
+        [pltpu.VMEM((FPAD, CHUNK), BF16), low],
         name="build",
-    )(feat_rows, row_norms, *cents, warm_coef)
+    )(feat_rows, row_norms, cents[1], *chunks, warm_coef)
 
     for round_idx in range(ROUNDS):
         mine, theirs = sum_over_groups(keep, send)

time: 421 us -> 364 us (0.86)
  blocking collectives: 258 us -> 214 us
  Pallas kernels: 64.4 us -> 28.4 us
  waiting for transfers between devices: 51.6 us -> 71.2 us
  starting transfers between devices: 33.4 us -> 43.1 us
    all_to_all x13 -> x11, blocking collectives: 258 us -> 214 us  [exchange(): lax.all_to_all(value, axis, split_axis=0, concat_axis=0, tiled=True, axis...]
    pallas_call x13 -> x16, Pallas kernels: 64.4 us -> 28.4 us  [call(): pl.pallas_call(kernel, out_shape=outs, in_specs=[vmem] * len(args), out_s...]
    ppermute x0 -> x6, waiting for transfers between devices: none -> 27 us  [sum_over_groups(): others = [lax.ppermute(half, 'centers', y_shift(d)) for d in (2, 1, 3)]]
    ppermute x15, waiting for transfers between devices: 44.8 us -> 38 us  [sum_and_gather(): lax.ppermute(mine, 'rows', x_shift(d))]
    ppermute x0 -> x6, starting transfers between devices: none -> 6.28 us  [sum_over_groups(): others = [lax.ppermute(half, 'centers', y_shift(d)) for d in (2, 1, 3)]]
  transfers between devices with their start and end apart: 20 -> 26, of which waited for: 20 -> 24; matrix products, arithmetic and copies ran while one was open for 1% -> 1% of each run, Pallas kernels for 0% -> 1%
where the time goes in v2:
time: 364 us; the launch traced here: 363 us
  blocking collectives  214 us (59%)
  waiting for transfers between devices  71.2 us (20%)
  starting transfers between devices  43.1 us (12%)
  Pallas kernels  28.4 us (8%)
  local copies, waits for them, and re-layouts  4.77 us (1%)
    all_to_all x11, blocking collectives, exchange(): lax.all_to_all(value, axis, split_axis=0, concat_axis=0, tiled=True, axis...  214 us
    ppermute x15, waiting for transfers between devices, sum_and_gather(): lax.ppermute(mine, 'rows', x_shift(d))  38 us
    pallas_call x16, Pallas kernels, call(): pl.pallas_call(kernel, out_shape=outs, in_specs=[vmem] * len(args), out_s...  28.4 us
    ppermute x6, waiting for transfers between devices, sum_over_groups(): others = [lax.ppermute(half, 'centers', y_shift(d)) for d in (2, 1, 3)]  27 us
    ppermute x15, starting transfers between devices, sum_and_gather(): lax.ppermute(mine, 'rows', x_shift(d))  15.4 us
    ppermute x2, starting transfers between devices, sum_over_groups(): half = keep + lax.ppermute(send, 'centers', CORE_SWAP)  8.96 us
    ppermute x1, starting transfers between devices, body(): part = keep + lax.ppermute(send, 'centers', CORE_SWAP)  7.35 us
  transfers between devices with their start and end apart: 26, of which 24 were waited for; matrix products, arithmetic and copies ran while one was open for 1% of the time, Pallas kernels for 1%

profile of v2, /device:TPU:1, one launch (start us, length us, event | category | flops | bytes accessed | tf_op | source)
XLA Modules:
  0.0 363.5 jit_solution(4635497739990343829)
XLA Ops:
  2.5 2.6 select.2
  5.1 53.1 %all_to_all.55.in_ref = bf16[32,224,128]{2,1,0:T(8,128)(2,1)S(1)} all-to-all(bf16[32,224,128]{2,1,0:T(8,128)(2,1)S(1)} %select.2), channel_id=1, replica_groups=mesh['rows'=32,'centers'=8] {'rows'}, dimensions={0} | all-to-all | bytes 3670016 | tf_op jit(solution)/shard_map/all_to_all | solution.py:237
  58.5 20.3 %all_to_all.56.c_ref = bf16[8,224,128]{2,1,0:T(8,128)(2,1)S(1)} all-to-all(bf16[8,224,128]{2,1,0:T(8,128)(2,1)S(1)} %sum_at_owner.5), channel_id=1, replica_groups={{0,8,16,24,32,40,48,56},{64,72,80,88,96,104,112,120},{128,136,144,152,1..., dimensions={0} | all-to-all | bytes 917504 | tf_op jit(solution)/shard_map/all_to_all | solution.py:237
  78.8 2.5 collective-permute-start.1
  90.5 10.8 %collective-permute-done.2.c_ref = bf16[8,224,128]{2,1,0:T(8,128)(2,1)S(1)} collective-permute-done((bf16[8,224,128]{2,1,0:T(8,128)(2,1)S(1)}, bf16[8,224,128]{2,1,0:T(8,128)(2,1)S(1)}, u32[]{:S(2)}, u32[]{:S(2)}) %collective-permute-start.2) | collective-permute-done | bytes 458784 | tf_op jit(solution)/shard_map/ppermute | solution.py:246
  102.7 3.9 %build.1 = (bf16[1024,2048]{1,0:T(8,128)(2,1)S(1)}, f32[160,2048]{1,0:T(8,128)S(1)}, f32[160,1024]{1,0:T(8,128)S(1)}, f32[152,512]{1,0:T(8,128)S(1)}, f32[152,512]{1,0:T(8,128)S(1)}) custom-call(bf16[1024,448]{1,0:T(8,128)(2,1)S(1)} %pad_bitcast_fusion.feat_ref, f32[1024,1]{1,0:T(8,128)S(1)} %copy.11.norm_ref, ...), custom_call_target="tpu_custom_call" | custom-call | flops 1073741824 | bytes 4194304 | tf_op jit(solution)/shard_map/build/pallas_call | solution.py:46
  109.5 2.8 collective-permute-start.6
  114.0 11.2 %collective-permute-done.6 = f32[152,512]{1,0:T(8,128)S(1)} collective-permute-done((f32[152,512]{1,0:T(8,128)S(1)}, f32[152,512]{1,0:T(8,128)S(1)}, u32[]{:S(2)}, u32[]{:S(2)}) %collective-permute-start.6) | collective-permute-done | bytes 311328 | tf_op jit(solution)/shard_map/ppermute | solution.py:251
  125.2 2.3 collective-permute-done.4
  127.6 2.6 collective-permute-start.7
  133.3 22.1 %all_to_all.57.in_ref = bf16[32,80,128]{2,1,0:T(8,128)(2,1)S(1)} all-to-all(bf16[32,80,128]{2,1,0:T(8,128)(2,1)S(1)} %get-tuple-element.27), channel_id=1, replica_groups=mesh['rows'=32,'centers'=8] {'rows'}, dimensions={0} | all-to-all | bytes 1310720 | tf_op jit(solution)/shard_map/all_to_all | solution.py:237
  155.5 14.3 %all_to_all.58.g0 = bf16[8,80,128]{2,1,0:T(8,128)(2,1)S(1)} all-to-all(bf16[8,80,128]{2,1,0:T(8,128)(2,1)S(1)} %sum_at_owner.6), channel_id=1, replica_groups={{0,8,16,24,32,40,48,56},{64,72,80,88,96,104,112,120},{128,136,144,152,1..., dimensions={0} | all-to-all | bytes 327680 | tf_op jit(solution)/shard_map/all_to_all | solution.py:237
  174.0 2.9 collective-permute-done.9.g2
  179.0 4.0 %second.2 = (bf16[32,80,128]{2,1,0:T(8,128)(2,1)S(1)}, f32[160,2048]{1,0:T(8,128)S(1)}) custom-call(f32[160,2048]{1,0:T(8,128)S(1)} %get-tuple-element.22.coef_ref, bf16[8,80,128]{2,1,0:T(8,128)(2,1)S(1)} %all_to_all.58.g0, bf16[8,80,128]{2,1,0:T(8,128)(2,1)S(1)} %collective-permute-done.8.g1, bf16[8,80,128]{2,1,0:T(8,128)(2,1)S(1)} %collective-permute-done.9.g2, ...), custom_call_target="tpu_custom_call" | custom-call | flops 1073741824 | bytes 4194304 | tf_op jit(solution)/shard_map/second/pallas_call | solution.py:46
  183.0 16.8 %all_to_all.59.in_ref = bf16[32,80,128]{2,1,0:T(8,128)(2,1)S(1)} all-to-all(bf16[32,80,128]{2,1,0:T(8,128)(2,1)S(1)} %get-tuple-element.30), channel_id=1, replica_groups=mesh['rows'=32,'centers'=8] {'rows'}, dimensions={0} | all-to-all | bytes 1310720 | tf_op jit(solution)/shard_map/all_to_all | solution.py:237
  199.9 13.5 %all_to_all.60.g0 = bf16[8,80,128]{2,1,0:T(8,128)(2,1)S(1)} all-to-all(bf16[8,80,128]{2,1,0:T(8,128)(2,1)S(1)} %sum_at_owner.7), channel_id=1, replica_groups={{0,8,16,24,32,40,48,56},{64,72,80,88,96,104,112,120},{128,136,144,152,1..., dimensions={0} | all-to-all | bytes 327680 | tf_op jit(solution)/shard_map/all_to_all | solution.py:237
  216.6 2.8 collective-permute-done.13.g3
  222.7 2.3 scores.1
  225.1 7.3 %collective-permute-start.14 = (f32[152,512]{1,0:T(8,128)S(1)}, f32[152,512]{1,0:T(8,128)S(1)}, u32[]{:S(2)}, u32[]{:S(2)}) collective-permute-start(f32[152,512]{1,0:T(8,128)S(1)} %get-tuple-element.33), channel_id=1, source_target_pairs={{0,1},{1,0},{2,3},{3,2},{4,5},{5,4},{6,7},{7,6},{8,9},{9,8},{10,11... | collective-permute-start | bytes 933896 | tf_op jit(solution)/shard_map/ppermute | solution.py:250
  235.5 6.8 %collective-permute-done.17 = f32[152,512]{1,0:T(8,128)S(1)} collective-permute-done((f32[152,512]{1,0:T(8,128)S(1)}, f32[152,512]{1,0:T(8,128)S(1)}, u32[]{:S(2)}, u32[]{:S(2)}) %collective-permute-start.17) | collective-permute-done | bytes 311328 | tf_op jit(solution)/shard_map/ppermute | solution.py:251
  244.5 4.5 %collective-permute-done.15 = f32[152,512]{1,0:T(8,128)S(1)} collective-permute-done((f32[152,512]{1,0:T(8,128)S(1)}, f32[152,512]{1,0:T(8,128)S(1)}, u32[]{:S(2)}, u32[]{:S(2)}) %collective-permute-start.15) | collective-permute-done | bytes 311328 | tf_op jit(solution)/shard_map/ppermute | solution.py:251
  249.1 2.6 collective-permute-start.18
  254.8 19.7 %all_to_all.61.in_ref = bf16[32,80,128]{2,1,0:T(8,128)(2,1)S(1)} all-to-all(bf16[32,80,128]{2,1,0:T(8,128)(2,1)S(1)} %get-tuple-element.35), channel_id=1, replica_groups=mesh['rows'=32,'centers'=8] {'rows'}, dimensions={0} | all-to-all | bytes 1310720 | tf_op jit(solution)/shard_map/all_to_all | solution.py:237
  274.6 14.3 %all_to_all.62.g0 = bf16[8,80,128]{2,1,0:T(8,128)(2,1)S(1)} all-to-all(bf16[8,80,128]{2,1,0:T(8,128)(2,1)S(1)} %sum_at_owner.8), channel_id=1, replica_groups={{0,8,16,24,32,40,48,56},{64,72,80,88,96,104,112,120},{128,136,144,152,1..., dimensions={0} | all-to-all | bytes 327680 | tf_op jit(solution)/shard_map/all_to_all | solution.py:237
  293.0 2.9 collective-permute-done.20.g2
  297.9 4.0 %second.3 = (bf16[32,80,128]{2,1,0:T(8,128)(2,1)S(1)}, f32[160,2048]{1,0:T(8,128)S(1)}) custom-call(f32[160,2048]{1,0:T(8,128)S(1)} %get-tuple-element.31.coef_ref, bf16[8,80,128]{2,1,0:T(8,128)(2,1)S(1)} %all_to_all.62.g0, bf16[8,80,128]{2,1,0:T(8,128)(2,1)S(1)} %collective-permute-done.19.g1, bf16[8,80,128]{2,1,0:T(8,128)(2,1)S(1)} %collective-permute-done.20.g2, ...), custom_call_target="tpu_custom_call" | custom-call | flops 1073741824 | bytes 4194304 | tf_op jit(solution)/shard_map/second/pallas_call | solution.py:46
  302.0 17.1 %all_to_all.63.in_ref = bf16[32,80,128]{2,1,0:T(8,128)(2,1)S(1)} all-to-all(bf16[32,80,128]{2,1,0:T(8,128)(2,1)S(1)} %get-tuple-element.38), channel_id=1, replica_groups=mesh['rows'=32,'centers'=8] {'rows'}, dimensions={0} | all-to-all | bytes 1310720 | tf_op jit(solution)/shard_map/all_to_all | solution.py:237
  319.2 13.3 %all_to_all.64.g0 = bf16[8,80,128]{2,1,0:T(8,128)(2,1)S(1)} all-to-all(bf16[8,80,128]{2,1,0:T(8,128)(2,1)S(1)} %sum_at_owner.9), channel_id=1, replica_groups={{0,8,16,24,32,40,48,56},{64,72,80,88,96,104,112,120},{128,136,144,152,1..., dimensions={0} | all-to-all | bytes 327680 | tf_op jit(solution)/shard_map/all_to_all | solution.py:237
  335.8 2.7 collective-permute-done.24.g3
  341.9 2.9 final.1
  344.8 7.4 %collective-permute-start.25 = (f32[4,152,128]{2,1,0:T(8,128)S(1)}, f32[4,152,128]{2,1,0:T(8,128)S(1)}, u32[]{:S(2)}, u32[]{:S(2)}) collective-permute-start(f32[4,152,128]{2,1,0:T(8,128)S(1)} %get-tuple-element.41), channel_id=1, source_target_pairs={{0,1},{1,0},{2,3},{3,2},{4,5},{5,4},{6,7},{7,6},{8,9},{9,8},{10,11... | collective-permute-start | bytes 933896 | tf_op jit(solution)/shard_map/ppermute | solution.py:309
  353.4 9.4 %all_to_all.65 = f32[4,152,128]{2,1,0:T(8,128)S(1)} all-to-all(f32[4,152,128]{2,1,0:T(8,128)S(1)} %add.37), channel_id=1, replica_groups={{0,2,4,6},{1,3,5,7},{8,10,12,14},{9,11,13,15},{16,18,20,22},{17,19,21,2..., dimensions={0} | all-to-all | bytes 622592 | tf_op jit(solution)/shard_map/all_to_all | solution.py:237
  (67 shorter events, 57.0 us)
Async XLA Ops:
  0.6 1.2 copy-start
  1.8 0.7 copy-start.4
  58.5 24.3 %copy-start.1 = (bf16[440,1024]{1,0:T(8,128)(2,1)S(1)}, bf16[440,1024]{1,0:T(8,128)(2,1)}, u32[]{:S(2)}) copy-start(bf16[440,1024]{1,0:T(8,128)(2,1)} %feat_ref.1) | copy-start | bytes 2703364
  78.8 10.2 %collective-permute-start.1 = (bf16[8,224,128]{2,1,0:T(8,128)(2,1)S(1)}, bf16[8,224,128]{2,1,0:T(8,128)(2,1)S(1)}, u32[]{:S(2)}, u32[]{:S(2)}) collective-permute-start(bf16[8,224,128]{2,1,0:T(8,128)(2,1)S(1)} %all_to_all.56.c_ref), channel_id=1, source_target_pairs={{0,128},{8,136},{16,144},{24,152},{32,160},{40,168},{48,176},{56,1... | collective-permute-start | bytes 1376264 | tf_op jit(solution)/shard_map/ppermute | solution.py:246
  81.3 20.0 %collective-permute-start.2 = (bf16[8,224,128]{2,1,0:T(8,128)(2,1)S(1)}, bf16[8,224,128]{2,1,0:T(8,128)(2,1)S(1)}, u32[]{:S(2)}, u32[]{:S(2)}) collective-permute-start(bf16[8,224,128]{2,1,0:T(8,128)(2,1)S(1)} %all_to_all.56.c_ref), channel_id=1, source_target_pairs={{0,192},{8,200},{16,208},{24,216},{32,224},{40,232},{48,240},{56,2... | collective-permute-start | bytes 1376264 | tf_op jit(solution)/shard_map/ppermute | solution.py:246
  82.5 20.3 %collective-permute-start = (bf16[8,224,128]{2,1,0:T(8,128)(2,1)S(1)}, bf16[8,224,128]{2,1,0:T(8,128)(2,1)S(1)}, u32[]{:S(2)}, u32[]{:S(2)}) collective-permute-start(bf16[8,224,128]{2,1,0:T(8,128)(2,1)S(1)} %all_to_all.56.c_ref), channel_id=1, source_target_pairs={{0,64},{8,72},{16,80},{24,88},{32,96},{40,104},{48,112},{56,120},{... | collective-permute-start | bytes 1376264 | tf_op jit(solution)/shard_map/ppermute | solution.py:246
  90.5 12.2 %copy-start.2 = (f32[147,2048]{1,0:T(8,128)S(1)}, f32[147,2048]{1,0:T(8,128)}, u32[]{:S(2)}) copy-start(f32[147,2048]{1,0:T(8,128)} %warm_ref.1) | copy-start | bytes 3612676
  106.6 24.8 %copy-start.3 = (s32[1024]{0:T(1024)S(1)}, s32[1024]{0:T(1024)}, u32[]{:S(2)}) copy-start(s32[1024]{0:T(1024)} %param.5) | copy-start | bytes 12292
  106.6 2.9 collective-permute-start.3
  109.5 15.7 %collective-permute-start.6 = (f32[152,512]{1,0:T(8,128)S(1)}, f32[152,512]{1,0:T(8,128)S(1)}, u32[]{:S(2)}, u32[]{:S(2)}) collective-permute-start(f32[152,512]{1,0:T(8,128)S(1)} %add.29), channel_id=1, source_target_pairs={{0,6},{1,7},{2,0},{3,1},{4,2},{5,3},{6,4},{7,5},{8,14},{9,15},{10,... | collective-permute-start | bytes 933896 | tf_op jit(solution)/shard_map/ppermute | solution.py:251
  112.4 12.9 %collective-permute-start.5 = (f32[152,512]{1,0:T(8,128)S(1)}, f32[152,512]{1,0:T(8,128)S(1)}, u32[]{:S(2)}, u32[]{:S(2)}) collective-permute-start(f32[152,512]{1,0:T(8,128)S(1)} %add.29), channel_id=1, source_target_pairs={{0,2},{1,3},{2,4},{3,5},{4,6},{5,7},{6,0},{7,1},{8,10},{9,11},{10,... | collective-permute-start | bytes 933896 | tf_op jit(solution)/shard_map/ppermute | solution.py:251
  112.4 15.2 %collective-permute-start.4 = (f32[152,512]{1,0:T(8,128)S(1)}, f32[152,512]{1,0:T(8,128)S(1)}, u32[]{:S(2)}, u32[]{:S(2)}) collective-permute-start(f32[152,512]{1,0:T(8,128)S(1)} %add.29), channel_id=1, source_target_pairs={{0,4},{1,5},{2,6},{3,7},{4,0},{5,1},{6,2},{7,3},{8,12},{9,13},{10,... | collective-permute-start | bytes 933896 | tf_op jit(solution)/shard_map/ppermute | solution.py:251
  127.6 3.8 %collective-permute-start.7 = (f32[152,512]{1,0:T(8,128)S(1)}, f32[152,512]{1,0:T(8,128)S(1)}, u32[]{:S(2)}, u32[]{:S(2)}) collective-permute-start(f32[152,512]{1,0:T(8,128)S(1)} %add_add_fusion.1.mine_ref), channel_id=1, source_target_pairs={{0,1},{1,0},{2,3},{3,2},{4,5},{5,4},{6,7},{7,6},{8,9},{9,8},{10,11... | collective-permute-start | bytes 933896 | tf_op jit(solution)/shard_map/ppermute | solution.py:253
  169.8 4.2 %collective-permute-start.10 = (bf16[8,80,128]{2,1,0:T(8,128)(2,1)S(1)}, bf16[8,80,128]{2,1,0:T(8,128)(2,1)S(1)}, u32[]{:S(2)}, u32[]{:S(2)}) collective-permute-start(bf16[8,80,128]{2,1,0:T(8,128)(2,1)S(1)} %all_to_all.58.g0), channel_id=1, source_target_pairs={{0,192},{8,200},{16,208},{24,216},{32,224},{40,232},{48,240},{56,2... | collective-permute-start | bytes 491528 | tf_op jit(solution)/shard_map/ppermute | solution.py:246
  171.1 5.8 %collective-permute-start.9 = (bf16[8,80,128]{2,1,0:T(8,128)(2,1)S(1)}, bf16[8,80,128]{2,1,0:T(8,128)(2,1)S(1)}, u32[]{:S(2)}, u32[]{:S(2)}) collective-permute-start(bf16[8,80,128]{2,1,0:T(8,128)(2,1)S(1)} %all_to_all.58.g0), channel_id=1, source_target_pairs={{0,128},{8,136},{16,144},{24,152},{32,160},{40,168},{48,176},{56,1... | collective-permute-start | bytes 491528 | tf_op jit(solution)/shard_map/ppermute | solution.py:246
  172.2 6.8 %collective-permute-start.8 = (bf16[8,80,128]{2,1,0:T(8,128)(2,1)S(1)}, bf16[8,80,128]{2,1,0:T(8,128)(2,1)S(1)}, u32[]{:S(2)}, u32[]{:S(2)}) collective-permute-start(bf16[8,80,128]{2,1,0:T(8,128)(2,1)S(1)} %all_to_all.58.g0), channel_id=1, source_target_pairs={{0,64},{8,72},{16,80},{24,88},{32,96},{40,104},{48,112},{56,120},{... | collective-permute-start | bytes 491528 | tf_op jit(solution)/shard_map/ppermute | solution.py:246
  213.4 6.0 %collective-permute-start.13 = (bf16[8,80,128]{2,1,0:T(8,128)(2,1)S(1)}, bf16[8,80,128]{2,1,0:T(8,128)(2,1)S(1)}, u32[]{:S(2)}, u32[]{:S(2)}) collective-permute-start(bf16[8,80,128]{2,1,0:T(8,128)(2,1)S(1)} %all_to_all.60.g0), channel_id=1, source_target_pairs={{0,192},{8,200},{16,208},{24,216},{32,224},{40,232},{48,240},{56,2... | collective-permute-start | bytes 491528 | tf_op jit(solution)/shard_map/ppermute | solution.py:246
  215.3 5.8 %collective-permute-start.12 = (bf16[8,80,128]{2,1,0:T(8,128)(2,1)S(1)}, bf16[8,80,128]{2,1,0:T(8,128)(2,1)S(1)}, u32[]{:S(2)}, u32[]{:S(2)}) collective-permute-start(bf16[8,80,128]{2,1,0:T(8,128)(2,1)S(1)} %all_to_all.60.g0), channel_id=1, source_target_pairs={{0,128},{8,136},{16,144},{24,152},{32,160},{40,168},{48,176},{56,1... | collective-permute-start | bytes 491528 | tf_op jit(solution)/shard_map/ppermute | solution.py:246
  216.2 6.5 %collective-permute-start.11 = (bf16[8,80,128]{2,1,0:T(8,128)(2,1)S(1)}, bf16[8,80,128]{2,1,0:T(8,128)(2,1)S(1)}, u32[]{:S(2)}, u32[]{:S(2)}) collective-permute-start(bf16[8,80,128]{2,1,0:T(8,128)(2,1)S(1)} %all_to_all.60.g0), channel_id=1, source_target_pairs={{0,64},{8,72},{16,80},{24,88},{32,96},{40,104},{48,112},{56,120},{... | collective-permute-start | bytes 491528 | tf_op jit(solution)/shard_map/ppermute | solution.py:246
  225.1 8.6 %collective-permute-start.14 = (f32[152,512]{1,0:T(8,128)S(1)}, f32[152,512]{1,0:T(8,128)S(1)}, u32[]{:S(2)}, u32[]{:S(2)}) collective-permute-start(f32[152,512]{1,0:T(8,128)S(1)} %get-tuple-element.33), channel_id=1, source_target_pairs={{0,1},{1,0},{2,3},{3,2},{4,5},{5,4},{6,7},{7,6},{8,9},{9,8},{10,11... | collective-permute-start | bytes 933896 | tf_op jit(solution)/shard_map/ppermute | solution.py:250
  233.7 8.6 %collective-permute-start.17 = (f32[152,512]{1,0:T(8,128)S(1)}, f32[152,512]{1,0:T(8,128)S(1)}, u32[]{:S(2)}, u32[]{:S(2)}) collective-permute-start(f32[152,512]{1,0:T(8,128)S(1)} %add.33), channel_id=1, source_target_pairs={{0,6},{1,7},{2,0},{3,1},{4,2},{5,3},{6,4},{7,5},{8,14},{9,15},{10,... | collective-permute-start | bytes 933896 | tf_op jit(solution)/shard_map/ppermute | solution.py:251
  233.7 10.7 %collective-permute-start.16 = (f32[152,512]{1,0:T(8,128)S(1)}, f32[152,512]{1,0:T(8,128)S(1)}, u32[]{:S(2)}, u32[]{:S(2)}) collective-permute-start(f32[152,512]{1,0:T(8,128)S(1)} %add.33), channel_id=1, source_target_pairs={{0,2},{1,3},{2,4},{3,5},{4,6},{5,7},{6,0},{7,1},{8,10},{9,11},{10,... | collective-permute-start | bytes 933896 | tf_op jit(solution)/shard_map/ppermute | solution.py:251
  235.2 13.8 %collective-permute-start.15 = (f32[152,512]{1,0:T(8,128)S(1)}, f32[152,512]{1,0:T(8,128)S(1)}, u32[]{:S(2)}, u32[]{:S(2)}) collective-permute-start(f32[152,512]{1,0:T(8,128)S(1)} %add.33), channel_id=1, source_target_pairs={{0,4},{1,5},{2,6},{3,7},{4,0},{5,1},{6,2},{7,3},{8,12},{9,13},{10,... | collective-permute-start | bytes 933896 | tf_op jit(solution)/shard_map/ppermute | solution.py:251
  249.1 3.8 %collective-permute-start.18 = (f32[152,512]{1,0:T(8,128)S(1)}, f32[152,512]{1,0:T(8,128)S(1)}, u32[]{:S(2)}, u32[]{:S(2)}) collective-permute-start(f32[152,512]{1,0:T(8,128)S(1)} %add_add_fusion.mine_ref), channel_id=1, source_target_pairs={{0,1},{1,0},{2,3},{3,2},{4,5},{5,4},{6,7},{7,6},{8,9},{9,8},{10,11... | collective-permute-start | bytes 933896 | tf_op jit(solution)/shard_map/ppermute | solution.py:253
  288.9 4.2 %collective-permute-start.21 = (bf16[8,80,128]{2,1,0:T(8,128)(2,1)S(1)}, bf16[8,80,128]{2,1,0:T(8,128)(2,1)S(1)}, u32[]{:S(2)}, u32[]{:S(2)}) collective-permute-start(bf16[8,80,128]{2,1,0:T(8,128)(2,1)S(1)} %all_to_all.62.g0), channel_id=1, source_target_pairs={{0,192},{8,200},{16,208},{24,216},{32,224},{40,232},{48,240},{56,2... | collective-permute-start | bytes 491528 | tf_op jit(solution)/shard_map/ppermute | solution.py:246
  290.2 5.8 %collective-permute-start.20 = (bf16[8,80,128]{2,1,0:T(8,128)(2,1)S(1)}, bf16[8,80,128]{2,1,0:T(8,128)(2,1)S(1)}, u32[]{:S(2)}, u32[]{:S(2)}) collective-permute-start(bf16[8,80,128]{2,1,0:T(8,128)(2,1)S(1)} %all_to_all.62.g0), channel_id=1, source_target_pairs={{0,128},{8,136},{16,144},{24,152},{32,160},{40,168},{48,176},{56,1... | collective-permute-start | bytes 491528 | tf_op jit(solution)/shard_map/ppermute | solution.py:246
  291.5 6.5 %collective-permute-start.19 = (bf16[8,80,128]{2,1,0:T(8,128)(2,1)S(1)}, bf16[8,80,128]{2,1,0:T(8,128)(2,1)S(1)}, u32[]{:S(2)}, u32[]{:S(2)}) collective-permute-start(bf16[8,80,128]{2,1,0:T(8,128)(2,1)S(1)} %all_to_all.62.g0), channel_id=1, source_target_pairs={{0,64},{8,72},{16,80},{24,88},{32,96},{40,104},{48,112},{56,120},{... | collective-permute-start | bytes 491528 | tf_op jit(solution)/shard_map/ppermute | solution.py:246
  332.5 5.9 %collective-permute-start.24 = (bf16[8,80,128]{2,1,0:T(8,128)(2,1)S(1)}, bf16[8,80,128]{2,1,0:T(8,128)(2,1)S(1)}, u32[]{:S(2)}, u32[]{:S(2)}) collective-permute-start(bf16[8,80,128]{2,1,0:T(8,128)(2,1)S(1)} %all_to_all.64.g0), channel_id=1, source_target_pairs={{0,192},{8,200},{16,208},{24,216},{32,224},{40,232},{48,240},{56,2... | collective-permute-start | bytes 491528 | tf_op jit(solution)/shard_map/ppermute | solution.py:246
  334.4 5.8 %collective-permute-start.23 = (bf16[8,80,128]{2,1,0:T(8,128)(2,1)S(1)}, bf16[8,80,128]{2,1,0:T(8,128)(2,1)S(1)}, u32[]{:S(2)}, u32[]{:S(2)}) collective-permute-start(bf16[8,80,128]{2,1,0:T(8,128)(2,1)S(1)} %all_to_all.64.g0), channel_id=1, source_target_pairs={{0,128},{8,136},{16,144},{24,152},{32,160},{40,168},{48,176},{56,1... | collective-permute-start | bytes 491528 | tf_op jit(solution)/shard_map/ppermute | solution.py:246
  335.5 6.4 %collective-permute-start.22 = (bf16[8,80,128]{2,1,0:T(8,128)(2,1)S(1)}, bf16[8,80,128]{2,1,0:T(8,128)(2,1)S(1)}, u32[]{:S(2)}, u32[]{:S(2)}) collective-permute-start(bf16[8,80,128]{2,1,0:T(8,128)(2,1)S(1)} %all_to_all.64.g0), channel_id=1, source_target_pairs={{0,64},{8,72},{16,80},{24,88},{32,96},{40,104},{48,112},{56,120},{... | collective-permute-start | bytes 491528 | tf_op jit(solution)/shard_map/ppermute | solution.py:246
  344.8 8.6 %collective-permute-start.25 = (f32[4,152,128]{2,1,0:T(8,128)S(1)}, f32[4,152,128]{2,1,0:T(8,128)S(1)}, u32[]{:S(2)}, u32[]{:S(2)}) collective-permute-start(f32[4,152,128]{2,1,0:T(8,128)S(1)} %get-tuple-element.41), channel_id=1, source_target_pairs={{0,1},{1,0},{2,3},{3,2},{4,5},{5,4},{6,7},{7,6},{8,9},{9,8},{10,11... | collective-permute-start | bytes 933896 | tf_op jit(solution)/shard_map/ppermute | solution.py:309

commit v3 on v2

--- a/solution.py
+++ b/solution.py
@@ -1,3 +1,5 @@
+import functools
+
 import jax
 import jax.numpy as jnp
 from jax import lax
@@ -19,6 +21,7 @@
 CHUNK = X * LANES
 PART = CHUNK // 4
 BLOCK = 256
+SLOTS = 32
 GRANT = 20 * 2**20
 FLOPS = 2**30
 
@@ -40,13 +43,14 @@
     return [(y * CORES + k, (y + d) % Y * CORES + k) for y in range(Y) for k in range(CORES)]
 
 
-def call(kernel, outs, scratch=(), name=None):
+def call(kernel, outs, scratch=(), name=None, scalars=0):
     vmem = pl.BlockSpec(memory_space=pltpu.VMEM)
+    smem = pl.BlockSpec(memory_space=pltpu.SMEM)
     many = isinstance(outs, (list, tuple))
     return lambda *args: pl.pallas_call(
         kernel,
         out_shape=outs,
-        in_specs=[vmem] * len(args),
+        in_specs=[smem] * scalars + [vmem] * (len(args) - scalars),
         out_specs=[vmem] * len(outs) if many else vmem,
         scratch_shapes=list(scratch),
         compiler_params=pltpu.CompilerParams(vmem_limit_bytes=GRANT),
@@ -84,27 +88,76 @@
     return lax.dot_general(a, b, (((1,), (1,)), ((), ())), preferred_element_type=F32)
 
 
-def select_kernel(feat_ref, index_ref, out_ref):
+def block_ranks(index_ref, rank_ref, rows):
+    before = lax.broadcasted_iota(jnp.int32, (PART, PART), 0) < lax.broadcasted_iota(
+        jnp.int32, (PART, PART), 1
+    )
+    before = jnp.where(before, 1.0, 0.0).astype(BF16)
+    owners = lax.broadcasted_iota(jnp.int32, (X * Z, PART), 0)
+
+    def block(b, top):
+        cols = pl.ds(pl.multiple_of(b * PART, PART), PART)
+        owned = jnp.where(lax.div(index_ref[:, cols], rows) == owners, 1.0, 0.0)
+        rank = jnp.sum(dot(owned.astype(BF16), before) * owned, axis=0, keepdims=True)
+        rank_ref[:, cols] = rank
+        return jnp.maximum(top, rank)
+
+    return lax.fori_loop(0, rank_ref.shape[1] // PART, block, jnp.zeros((1, PART), F32))
+
+
+def select_kernel(turn_ref, feat_ref, index_ref, out_ref, rank_ref, top_ref, hot_ref):
     rows = feat_ref.shape[1]
+    half = FPAD // 2
+    top_ref[...] = jnp.broadcast_to(
+        jnp.max(block_ranks(index_ref, rank_ref, rows), axis=1, keepdims=True), top_ref.shape
+    )
     first = lax.axis_index("rows") * rows
-    half = FPAD // 2
-
-    @pl.loop(0, X)
-    def _(c):
-        wanted = index_ref[:, pl.ds(pl.multiple_of(c * CHUNK, CHUNK), CHUNK)] - first
-        hot = lax.broadcasted_iota(jnp.int32, (rows, CHUNK), 0) == wanted
-        got = dot(feat_ref[...], jnp.where(hot, 1.0, 0.0).astype(BF16))
-        got = jnp.concatenate([got, jnp.zeros((FPAD - FEAT, CHUNK), F32)], axis=0).astype(BF16)
-        for z in range(Z):
-            height, left = spot(z, half)
-            out_ref[c * Z + z] = got[height, left : left + PART]
+    skip = (turn_ref[0] * SLOTS).astype(F32)
+    slots = lax.broadcasted_iota(jnp.int32, (SLOTS, PART), 0).astype(F32)
+    places = lax.broadcasted_iota(jnp.int32, (SLOTS, rows), 1).astype(F32)
+
+    @pl.loop(0, rank_ref.shape[1] // PART)
+    def _(b):
+        cols = pl.ds(pl.multiple_of(b * PART, PART), PART)
+        local = index_ref[:, cols] - first
+        inside = (local >= 0) & (local < rows)
+        chosen = inside & (rank_ref[:, cols] - skip == slots)
+        place = jnp.sum(
+            jnp.where(chosen, (local + 1).astype(F32), 0.0), axis=1, keepdims=True
+        )
+        hot_ref[pl.ds(pl.multiple_of(b * SLOTS, SLOTS), SLOTS), :] = jnp.where(places == place - 1.0, 1.0, 0.0).astype(BF16)
+    out_ref[...] = jnp.zeros_like(out_ref)
+    for h, stop in ((0, half), (1, FEAT)):
+        got = dot_nt(hot_ref[...], feat_ref[h * half : stop, :]).astype(BF16)
+        for b in range(rank_ref.shape[1] // PART):
+            to = b // 4 * Z + h * 4 + b % 4
+            out_ref[to, :, : stop - h * half] = got[b * SLOTS : (b + 1) * SLOTS]
+
+
+def place_kernel(turn_ref, in_ref, index_ref, rank_ref, out_ref, *, rows):
+    me = lax.axis_index("rows")
+    block = lax.div(me, Z) * 4 + lax.rem(me, 4)
+    cols = pl.ds(pl.multiple_of(block * PART, PART), PART)
+    rank = rank_ref[:, cols].astype(jnp.int32) - turn_ref[0] * SLOTS
+    slot = lax.div(index_ref[:, cols], rows) * SLOTS + rank
+    slot = jnp.where((rank >= 0) & (rank < SLOTS), slot, -1)
+    count = in_ref.shape[0] * SLOTS
+    hot = lax.broadcasted_iota(jnp.int32, (count, PART), 0) == slot
+    hot = jnp.where(hot, 1.0, 0.0).astype(BF16)
+    arrived = in_ref[...].reshape(count, in_ref.shape[2])
+    placed = lax.dot_general(
+        arrived, hot, (((0,), (0,)), ((), ())), preferred_element_type=F32
+    ).astype(BF16)
+    for i in range(out_ref.shape[0]):
+        out_ref[i] = placed[: FPAD // 2]
 
 
 def sum_kernel(in_ref, out_ref):
-    total = in_ref[0].astype(F32)
-    for i in range(1, in_ref.shape[0]):
-        total = total + in_ref[i].astype(F32)
-    total = total.astype(BF16)
+    total = lax.fori_loop(
+        0, in_ref.shape[0] // 4,
+        lambda i, total: total + sum(in_ref[i * 4 + j].astype(F32) for j in range(4)),
+        jnp.zeros(in_ref.shape[1:], F32),
+    ).astype(BF16)
     for i in range(out_ref.shape[0]):
         out_ref[i] = total
 
@@ -179,11 +232,13 @@
             out_ref[chunk_of(d) * Z + z] = grad[height, left : left + PART]
 
 
-def first_kernel(mine_ref, theirs_ref, own_ref, kern_ref, label_ref, out_ref, base_ref, res_ref, sum_ref):
+def first_kernel(m0, m1, t0, t1, own_ref, kern_ref, label_ref, out_ref, base_ref, res_ref, sum_ref):
     core = my_core()
-    width = mine_ref.shape[1]
-    sum_ref[:WIRE, pl.ds(pl.multiple_of(core * width, width), width)] = mine_ref[...]
-    sum_ref[:WIRE, pl.ds(pl.multiple_of((1 - core) * width, width), width)] = theirs_ref[...]
+    width = m0.shape[1]
+    for side, refs in ((core, (m0, m1)), (1 - core, (t0, t1))):
+        for i, ref in enumerate(refs):
+            to = pl.multiple_of((side * 2 + i) * width, width)
+            sum_ref[:WIRE, pl.ds(to, width)] = ref[...]
     for n in range(sum_ref.shape[1] // BLOCK):
         at = slice(n * BLOCK, (n + 1) * BLOCK)
         res_ref[:, at] = residual_of(sum_ref[:, at], label_ref[:, at])
@@ -193,10 +248,13 @@
 
 def update(coef_ref, grads, new_ref, low_ref):
     half = PAD // 2
-    for d, g_ref in enumerate(grads):
-        for z in range(Z):
-            height, left = spot(z, half)
-            cols = slice(d * CHUNK + left, d * CHUNK + left + PART)
+
+    @pl.loop(0, Z)
+    def _(z):
+        height = pl.ds(pl.multiple_of(lax.div(z, 4) * half, half), half)
+        for d, g_ref in enumerate(grads):
+            left = pl.multiple_of(d * CHUNK + lax.rem(z, 4) * PART, PART)
+            cols = pl.ds(left, PART)
             fresh = coef_ref[height, cols] - STEP * g_ref[z].astype(F32)
             new_ref[height, cols] = fresh
             low_ref[height, cols] = fresh.astype(BF16)
@@ -239,18 +297,76 @@
     )
 
 
+def gather(copies):
+    mine = exchange(copies, "rows", Z_GROUPS)
+    return [mine] + [lax.ppermute(mine, "rows", x_shift(d)) for d in range(1, X)]
+
+
 def sum_and_gather(pieces):
     arrived = exchange(pieces, "rows")
     copies = call(sum_kernel, like((Z, *pieces.shape[1:]), BF16), name="sum_at_owner")(arrived)
-    mine = exchange(copies, "rows", Z_GROUPS)
-    return [mine] + [lax.ppermute(mine, "rows", x_shift(d)) for d in range(1, X)]
+    return gather(copies)
+
+
+def gather_centers(features, center_index):
+    rows = features.shape[1]
+    centers = center_index.shape[1]
+
+    def select(turn):
+        return call(
+            select_kernel,
+            [
+                like((X * Z, SLOTS, 256), BF16),
+                like((1, centers), F32),
+                like((8, LANES), F32),
+            ],
+            [pltpu.VMEM((centers // PART * SLOTS, rows), BF16)],
+            name="select",
+            scalars=1,
+        )(turn, features, center_index)
+
+    def place(turn, pieces, rank):
+        arrived = exchange(pieces, "rows")
+        return call(
+            functools.partial(place_kernel, rows=rows),
+            like((Z, FPAD // 2, PART), BF16),
+            name="place",
+            scalars=1,
+        )(turn, arrived, center_index, rank)
+
+    start = jnp.zeros((1,), jnp.int32)
+    pieces, rank, top = select(start)
+    top = jnp.maximum(top, lax.ppermute(top, "centers", CORE_SWAP))
+    pieces, top = lax.optimization_barrier((pieces, top))
+    tops = [lax.ppermute(top, "centers", y_shift(d)) for d in (2, 1, 3)]
+    copies = place(start, pieces, rank)
+    for other in tops:
+        top = jnp.maximum(top, other)
+    last = top[0, 0].astype(jnp.int32)
+
+    def another(state):
+        turn, copies = state
+        pieces, rank, _ = select(turn)
+        return turn + 1, copies + place(turn, pieces, rank)
+
+    _, copies = lax.while_loop(
+        lambda state: state[0][0] * SLOTS <= last, another, (start + 1, copies)
+    )
+    return gather(copies)
+
+
+def pairwise(axis_map):
+    return [(y * CORES + k, axis_map(y) * CORES + k) for y in range(Y) for k in range(CORES)]
 
 
 def sum_over_groups(keep, send):
     half = keep + lax.ppermute(send, "centers", CORE_SWAP)
-    others = [lax.ppermute(half, "centers", y_shift(d)) for d in (2, 1, 3)]
-    half = half + others[0] + (others[1] + others[2])
-    return half, lax.ppermute(half, "centers", CORE_SWAP)
+    width = half.shape[1] // 2
+    steps = (pairwise(lambda y: y ^ 1), pairwise(lambda y: Y - 1 - y))
+    parts = [half[:, :width], half[:, width:]]
+    for order in (steps, steps[::-1]):
+        parts = [p + lax.ppermute(p, "centers", step) for p, step in zip(parts, order)]
+    return parts + [lax.ppermute(p, "centers", CORE_SWAP) for p in parts]
 
 
 def body(features, labels, center_index, warm_coef):
@@ -268,12 +384,9 @@
     score = pltpu.VMEM((PAD, rows), F32)
     coef_scratch = pltpu.VMEM((PAD, centers), F32)
 
-    picked = call(select_kernel, like((X * Z, FPAD // 2, PART), BF16), name="select")(
-        features, center_index
-    )
     row_norms = jnp.sum(jnp.square(features.astype(F32)), axis=0).reshape(rows, 1)
     feat_rows = jnp.pad(features, ((0, FPAD - FEAT), (0, 0))).T
-    cents = sum_and_gather(picked)
+    cents = gather_centers(features, center_index)
     build_chunk = call(
         chunk_kernel, like((rows, CHUNK), BF16), [pltpu.VMEM((FPAD, CHUNK), BF16)], name="chunk"
     )
@@ -286,9 +399,9 @@
     )(feat_rows, row_norms, cents[1], *chunks, warm_coef)
 
     for round_idx in range(ROUNDS):
-        mine, theirs = sum_over_groups(keep, send)
+        sums = sum_over_groups(keep, send)
         pieces, base = call(first_kernel, [grad_type, own_type], [res, score], name="first")(
-            mine, theirs, own, kern, labels
+            *sums, own, kern, labels
         )
         for _ in range(1, PASSES):
             grads = sum_and_gather(pieces)

time: 364 us -> 334 us (0.918)
  blocking collectives: 214 us -> 160 us
  starting transfers between devices: 43.1 us -> 62 us
  Pallas kernels: 28.4 us -> 33.3 us
    all_to_all x11 -> x10, blocking collectives: 214 us -> 160 us  [exchange(): lax.all_to_all(value, axis, split_axis=0, concat_axis=0, tiled=True, axis...]
    ppermute x23 -> x31, starting transfers between devices: 26.8 us -> 37.4 us  [the longest x15 14.4 us: gather(): lax.ppermute(mine, 'rows', x_shift(d))]
    all_to_all x0 -> x1, starting transfers between devices: none -> 9.33 us  [exchange(): lax.all_to_all(value, axis, split_axis=0, concat_axis=0, tiled=True, axis...]
    all_to_all x0 -> x1, waiting for transfers between devices: none -> 6.19 us  [exchange(): lax.all_to_all(value, axis, split_axis=0, concat_axis=0, tiled=True, axis...]
    ppermute x23 -> x31, waiting for transfers between devices: 67.5 us -> 61.8 us  [the longest x15 41.2 us: gather(): lax.ppermute(mine, 'rows', x_shift(d))]
    pallas_call x16, Pallas kernels: 28.4 us -> 33.3 us  [call(): pl.pallas_call(kernel, out_shape=outs, in_specs=[smem] * scalars + [vmem]...]
  transfers between devices with their start and end apart: 26 -> 35, of which waited for: 24 -> 29; matrix products, arithmetic and copies ran while one was open for 1% -> 1% of each run, Pallas kernels for 1% -> 1%
where the time goes in v3:
time: 334 us; the launch traced here: 333 us
  blocking collectives  160 us (48%)
  waiting for transfers between devices  71.7 us (21%)
  starting transfers between devices  62 us (19%)
  Pallas kernels  33.3 us (10%)
    all_to_all x10, blocking collectives, exchange(): lax.all_to_all(value, axis, split_axis=0, concat_axis=0, tiled=True, axis...  160 us
    ppermute x15, waiting for transfers between devices, gather(): lax.ppermute(mine, 'rows', x_shift(d))  41.2 us
    pallas_call x16, Pallas kernels, call(): pl.pallas_call(kernel, out_shape=outs, in_specs=[smem] * scalars + [vmem]...  33.3 us
    ppermute x8, waiting for transfers between devices, sum_over_groups(): lax.ppermute(p, 'centers', step)  15.4 us
    ppermute x15, starting transfers between devices, gather(): lax.ppermute(mine, 'rows', x_shift(d))  14.4 us
    all_to_all x1, starting transfers between devices, exchange(): lax.all_to_all(value, axis, split_axis=0, concat_axis=0, tiled=True, axis...  9.33 us
    ppermute x4, starting transfers between devices, sum_over_groups(): return parts + [lax.ppermute(p, 'centers', CORE_SWAP) for p in parts]  8.18 us
    ppermute x2, starting transfers between devices, sum_over_groups(): half = keep + lax.ppermute(send, 'centers', CORE_SWAP)  7.93 us
  transfers between devices with their start and end apart: 35, of which 29 were waited for; matrix products, arithmetic and copies ran while one was open for 1% of the time, Pallas kernels for 1%

profile of v3, /device:TPU:1, one launch (start us, length us, event | category | flops | bytes accessed | tf_op | source)
XLA Modules:
  0.0 333.0 jit_solution(8547952025547522719)
XLA Ops:
  0.6 6.6 %select.3 = (bf16[32,32,256]{2,1,0:T(8,128)(2,1)}, f32[1,2048]{1,0:T(1,128)S(1)}, f32[8,128]{1,0:T(8,128)S(1)}) custom-call(s32[1]{0:T(128)} %constant.13.clone.1.turn_ref, bf16[440,1024]{1,0:T(8,128)(2,1)} %feat_ref.1, s32[1,2048]{1,0:T(1,128)} %index_ref.3), custom_call_target="tpu_custom_call" | custom-call | flops 1073741824 | bytes 4194304 | tf_op jit(solution)/shard_map/select/pallas_call | solution.py:50
  7.3 3.2 collective-permute-start
  11.3 9.3 %all-to-all-start.1 = ((bf16[32,32,256]{2,1,0:T(8,128)(2,1)}), bf16[32,32,256]{2,1,0:T(8,128)(2,1)S(1)}, u32[]{:S(2)}, u32[]{:S(2)}) async-start(bf16[32,32,256]{2,1,0:T(8,128)(2,1)} %get-tuple-element.59), calls=%async_computation.1 | async-start | bytes 1048576 | tf_op jit(solution)/shard_map/all_to_all | solution.py:295
  20.6 2.8 collective-permute-start.3
  28.6 6.2 %all-to-all-done.1.in_ref = bf16[32,32,256]{2,1,0:T(8,128)(2,1)S(1)} async-done(((bf16[32,32,256]{2,1,0:T(8,128)(2,1)}), bf16[32,32,256]{2,1,0:T(8,128)(2,1)S(1)}, u32[]{:S(2)}, u32[]{:S(2)}) %all-to-all-start.1) | async-done | bytes 524320 | tf_op jit(solution)/shard_map/all_to_all | solution.py:295
  36.0 20.2 %all_to_all.60.c_ref = bf16[8,224,128]{2,1,0:T(8,128)(2,1)S(1)} all-to-all(bf16[8,224,128]{2,1,0:T(8,128)(2,1)S(1)} %get-tuple-element.62), channel_id=1, replica_groups={{0,8,16,24,32,40,48,56},{64,72,80,88,96,104,112,120},{128,136,144,152,1..., dimensions={0} | all-to-all | bytes 917504 | tf_op jit(solution)/shard_map/all_to_all | solution.py:295
  62.5 2.8 collective-permute-done.6.c_ref
  69.3 11.9 %collective-permute-done.4.c_ref = bf16[8,224,128]{2,1,0:T(8,128)(2,1)S(1)} collective-permute-done((bf16[8,224,128]{2,1,0:T(8,128)(2,1)S(1)}, bf16[8,224,128]{2,1,0:T(8,128)(2,1)S(1)}, u32[]{:S(2)}, u32[]{:S(2)}) %collective-permute-start.4) | collective-permute-done | bytes 458784 | tf_op jit(solution)/shard_map/ppermute | solution.py:302
  81.1 3.9 %build.1 = (bf16[1024,2048]{1,0:T(8,128)(2,1)S(1)}, f32[160,2048]{1,0:T(8,128)S(1)}, f32[160,1024]{1,0:T(8,128)S(1)}, f32[152,512]{1,0:T(8,128)S(1)}, f32[152,512]{1,0:T(8,128)S(1)}) custom-call(bf16[1024,448]{1,0:T(8,128)(2,1)S(1)} %pad_bitcast_fusion.feat_ref, f32[1024,1]{1,0:T(8,128)S(1)} %copy.11.norm_ref, ...), custom_call_target="tpu_custom_call" | custom-call | flops 1073741824 | bytes 4194304 | tf_op jit(solution)/shard_map/build/pallas_call | solution.py:50
  86.9 2.8 collective-permute-start.10
  89.7 3.8 %collective-permute-done.10 = f32[152,256]{1,0:T(8,128)S(1)} collective-permute-done((f32[152,256]{1,0:T(8,128)S(1)}, f32[152,256]{1,0:T(8,128)S(1)}, u32[]{:S(2)}, u32[]{:S(2)}) %collective-permute-start.10) | collective-permute-done | bytes 155680 | tf_op jit(solution)/shard_map/ppermute | solution.py:368
  98.9 2.8 collective-permute-start.13
  106.0 21.7 %all_to_all.61.in_ref = bf16[32,80,128]{2,1,0:T(8,128)(2,1)S(1)} all-to-all(bf16[32,80,128]{2,1,0:T(8,128)(2,1)S(1)} %get-tuple-element.68), channel_id=1, replica_groups=mesh['rows'=32,'centers'=8] {'rows'}, dimensions={0} | all-to-all | bytes 1310720 | tf_op jit(solution)/shard_map/all_to_all | solution.py:295
  127.9 14.3 %all_to_all.62.g0 = bf16[8,80,128]{2,1,0:T(8,128)(2,1)S(1)} all-to-all(bf16[8,80,128]{2,1,0:T(8,128)(2,1)S(1)} %sum_at_owner.4), channel_id=1, replica_groups={{0,8,16,24,32,40,48,56},{64,72,80,88,96,104,112,120},{128,136,144,152,1..., dimensions={0} | all-to-all | bytes 327680 | tf_op jit(solution)/shard_map/all_to_all | solution.py:295
  146.3 2.9 collective-permute-done.15.g2
  151.4 4.2 %second.2 = (bf16[32,80,128]{2,1,0:T(8,128)(2,1)S(1)}, f32[160,2048]{1,0:T(8,128)S(1)}) custom-call(f32[160,2048]{1,0:T(8,128)S(1)} %get-tuple-element.63.coef_ref, bf16[8,80,128]{2,1,0:T(8,128)(2,1)S(1)} %all_to_all.62.g0, bf16[8,80,128]{2,1,0:T(8,128)(2,1)S(1)} %collective-permute-done.14.g1, bf16[8,80,128]{2,1,0:T(8,128)(2,1)S(1)} %collective-permute-done.15.g2, ...), custom_call_target="tpu_custom_call" | custom-call | flops 1073741824 | bytes 4194304 | tf_op jit(solution)/shard_map/second/pallas_call | solution.py:50
  155.6 16.8 %all_to_all.63.in_ref = bf16[32,80,128]{2,1,0:T(8,128)(2,1)S(1)} all-to-all(bf16[32,80,128]{2,1,0:T(8,128)(2,1)S(1)} %get-tuple-element.71), channel_id=1, replica_groups=mesh['rows'=32,'centers'=8] {'rows'}, dimensions={0} | all-to-all | bytes 1310720 | tf_op jit(solution)/shard_map/all_to_all | solution.py:295
  172.5 13.5 %all_to_all.64.g0 = bf16[8,80,128]{2,1,0:T(8,128)(2,1)S(1)} all-to-all(bf16[8,80,128]{2,1,0:T(8,128)(2,1)S(1)} %sum_at_owner.5), channel_id=1, replica_groups={{0,8,16,24,32,40,48,56},{64,72,80,88,96,104,112,120},{128,136,144,152,1..., dimensions={0} | all-to-all | bytes 327680 | tf_op jit(solution)/shard_map/all_to_all | solution.py:295
  189.2 2.7 collective-permute-done.19.g3
  197.8 7.3 %collective-permute-start.20 = (f32[152,512]{1,0:T(8,128)S(1)}, f32[152,512]{1,0:T(8,128)S(1)}, u32[]{:S(2)}, u32[]{:S(2)}) collective-permute-start(f32[152,512]{1,0:T(8,128)S(1)} %get-tuple-element.74), channel_id=1, source_target_pairs={{0,1},{1,0},{2,3},{3,2},{4,5},{5,4},{6,7},{7,6},{8,9},{9,8},{10,11... | collective-permute-start | bytes 933896 | tf_op jit(solution)/shard_map/ppermute | solution.py:363
  207.6 5.4 %collective-permute-done.23 = f32[152,256]{1,0:T(8,128)S(1)} collective-permute-done((f32[152,256]{1,0:T(8,128)S(1)}, f32[152,256]{1,0:T(8,128)S(1)}, u32[]{:S(2)}, u32[]{:S(2)}) %collective-permute-start.23) | collective-permute-done | bytes 155680 | tf_op jit(solution)/shard_map/ppermute | solution.py:368
  214.6 2.6 collective-permute-done.24
  224.1 19.7 %all_to_all.65.in_ref = bf16[32,80,128]{2,1,0:T(8,128)(2,1)S(1)} all-to-all(bf16[32,80,128]{2,1,0:T(8,128)(2,1)S(1)} %get-tuple-element.76), channel_id=1, replica_groups=mesh['rows'=32,'centers'=8] {'rows'}, dimensions={0} | all-to-all | bytes 1310720 | tf_op jit(solution)/shard_map/all_to_all | solution.py:295
  244.0 14.3 %all_to_all.66.g0 = bf16[8,80,128]{2,1,0:T(8,128)(2,1)S(1)} all-to-all(bf16[8,80,128]{2,1,0:T(8,128)(2,1)S(1)} %sum_at_owner.6), channel_id=1, replica_groups={{0,8,16,24,32,40,48,56},{64,72,80,88,96,104,112,120},{128,136,144,152,1..., dimensions={0} | all-to-all | bytes 327680 | tf_op jit(solution)/shard_map/all_to_all | solution.py:295
  262.4 2.9 collective-permute-done.28.g2
  267.3 4.2 %second.3 = (bf16[32,80,128]{2,1,0:T(8,128)(2,1)S(1)}, f32[160,2048]{1,0:T(8,128)S(1)}) custom-call(f32[160,2048]{1,0:T(8,128)S(1)} %get-tuple-element.72.coef_ref, bf16[8,80,128]{2,1,0:T(8,128)(2,1)S(1)} %all_to_all.66.g0, bf16[8,80,128]{2,1,0:T(8,128)(2,1)S(1)} %collective-permute-done.27.g1, bf16[8,80,128]{2,1,0:T(8,128)(2,1)S(1)} %collective-permute-done.28.g2, ...), custom_call_target="tpu_custom_call" | custom-call | flops 1073741824 | bytes 4194304 | tf_op jit(solution)/shard_map/second/pallas_call | solution.py:50
  271.5 17.1 %all_to_all.67.in_ref = bf16[32,80,128]{2,1,0:T(8,128)(2,1)S(1)} all-to-all(bf16[32,80,128]{2,1,0:T(8,128)(2,1)S(1)} %get-tuple-element.79), channel_id=1, replica_groups=mesh['rows'=32,'centers'=8] {'rows'}, dimensions={0} | all-to-all | bytes 1310720 | tf_op jit(solution)/shard_map/all_to_all | solution.py:295
  288.8 13.3 %all_to_all.68.g0 = bf16[8,80,128]{2,1,0:T(8,128)(2,1)S(1)} all-to-all(bf16[8,80,128]{2,1,0:T(8,128)(2,1)S(1)} %sum_at_owner.7), channel_id=1, replica_groups={{0,8,16,24,32,40,48,56},{64,72,80,88,96,104,112,120},{128,136,144,152,1..., dimensions={0} | all-to-all | bytes 327680 | tf_op jit(solution)/shard_map/all_to_all | solution.py:295
  305.4 2.7 collective-permute-done.32.g3
  311.5 3.1 final.1
  314.6 7.3 %collective-permute-start.33 = (f32[4,152,128]{2,1,0:T(8,128)S(1)}, f32[4,152,128]{2,1,0:T(8,128)S(1)}, u32[]{:S(2)}, u32[]{:S(2)}) collective-permute-start(f32[4,152,128]{2,1,0:T(8,128)S(1)} %get-tuple-element.82), channel_id=1, source_target_pairs={{0,1},{1,0},{2,3},{3,2},{4,5},{5,4},{6,7},{7,6},{8,9},{9,8},{10,11... | collective-permute-start | bytes 933896 | tf_op jit(solution)/shard_map/ppermute | solution.py:422
  323.2 9.2 %all_to_all.69 = f32[4,152,128]{2,1,0:T(8,128)S(1)} all-to-all(f32[4,152,128]{2,1,0:T(8,128)S(1)} %add.51), channel_id=1, replica_groups={{0,2,4,6},{1,3,5,7},{8,10,12,14},{9,11,13,15},{16,18,20,22},{17,19,21,2..., dimensions={0} | all-to-all | bytes 622592 | tf_op jit(solution)/shard_map/all_to_all | solution.py:295
  (92 shorter events, 70.0 us)
Async XLA Ops:
  7.3 4.0 %collective-permute-start = (f32[8,128]{1,0:T(8,128)S(1)}, f32[8,128]{1,0:T(8,128)S(1)}, u32[]{:S(2)}, u32[]{:S(2)}) collective-permute-start(f32[8,128]{1,0:T(8,128)S(1)} %get-tuple-element.58), channel_id=1, source_target_pairs={{0,1},{1,0},{2,3},{3,2},{4,5},{5,4},{6,7},{7,6},{8,9},{9,8},{10,11... | collective-permute-start | bytes 12296 | tf_op jit(solution)/shard_map/ppermute | solution.py:339
  11.3 23.5 %all-to-all-start.1 = ((bf16[32,32,256]{2,1,0:T(8,128)(2,1)}), bf16[32,32,256]{2,1,0:T(8,128)(2,1)S(1)}, u32[]{:S(2)}, u32[]{:S(2)}) async-start(bf16[32,32,256]{2,1,0:T(8,128)(2,1)} %get-tuple-element.59), calls=%async_computation.1 | async-start | bytes 1048576 | tf_op jit(solution)/shard_map/all_to_all | solution.py:295
  20.6 4.5 %collective-permute-start.3 = (f32[8,128]{1,0:T(8,128)S(1)}, f32[8,128]{1,0:T(8,128)S(1)}, u32[]{:S(2)}, u32[]{:S(2)}) collective-permute-start(f32[8,128]{1,0:T(8,128)S(1)} %max.12), channel_id=1, source_target_pairs={{0,6},{1,7},{2,0},{3,1},{4,2},{5,3},{6,4},{7,5},{8,14},{9,15},{10,... | collective-permute-start | bytes 12296 | tf_op jit(solution)/shard_map/ppermute | solution.py:341
  23.4 3.7 %collective-permute-start.2 = (f32[8,128]{1,0:T(8,128)S(1)}, f32[8,128]{1,0:T(8,128)S(1)}, u32[]{:S(2)}, u32[]{:S(2)}) collective-permute-start(f32[8,128]{1,0:T(8,128)S(1)} %max.12), channel_id=1, source_target_pairs={{0,2},{1,3},{2,4},{3,5},{4,6},{5,7},{6,0},{7,1},{8,10},{9,11},{10,... | collective-permute-start | bytes 12296 | tf_op jit(solution)/shard_map/ppermute | solution.py:341
  23.4 4.0 %collective-permute-start.1 = (f32[8,128]{1,0:T(8,128)S(1)}, f32[8,128]{1,0:T(8,128)S(1)}, u32[]{:S(2)}, u32[]{:S(2)}) collective-permute-start(f32[8,128]{1,0:T(8,128)S(1)} %max.12), channel_id=1, source_target_pairs={{0,4},{1,5},{2,6},{3,7},{4,0},{5,1},{6,2},{7,3},{8,12},{9,13},{10,... | collective-permute-start | bytes 12296 | tf_op jit(solution)/shard_map/ppermute | solution.py:341
  56.1 9.1 %collective-permute-start.6 = (bf16[8,224,128]{2,1,0:T(8,128)(2,1)S(1)}, bf16[8,224,128]{2,1,0:T(8,128)(2,1)S(1)}, u32[]{:S(2)}, u32[]{:S(2)}) collective-permute-start(bf16[8,224,128]{2,1,0:T(8,128)(2,1)S(1)} %all_to_all.60.c_ref), channel_id=1, source_target_pairs={{0,192},{8,200},{16,208},{24,216},{32,224},{40,232},{48,240},{56,2... | collective-permute-start | bytes 1376264 | tf_op jit(solution)/shard_map/ppermute | solution.py:302
  57.3 10.5 %collective-permute-start.5 = (bf16[8,224,128]{2,1,0:T(8,128)(2,1)S(1)}, bf16[8,224,128]{2,1,0:T(8,128)(2,1)S(1)}, u32[]{:S(2)}, u32[]{:S(2)}) collective-permute-start(bf16[8,224,128]{2,1,0:T(8,128)(2,1)S(1)} %all_to_all.60.c_ref), channel_id=1, source_target_pairs={{0,128},{8,136},{16,144},{24,152},{32,160},{40,168},{48,176},{56,1... | collective-permute-start | bytes 1376264 | tf_op jit(solution)/shard_map/ppermute | solution.py:302
  58.6 22.6 %collective-permute-start.4 = (bf16[8,224,128]{2,1,0:T(8,128)(2,1)S(1)}, bf16[8,224,128]{2,1,0:T(8,128)(2,1)S(1)}, u32[]{:S(2)}, u32[]{:S(2)}) collective-permute-start(bf16[8,224,128]{2,1,0:T(8,128)(2,1)S(1)} %all_to_all.60.c_ref), channel_id=1, source_target_pairs={{0,64},{8,72},{16,80},{24,88},{32,96},{40,104},{48,112},{56,120},{... | collective-permute-start | bytes 1376264 | tf_op jit(solution)/shard_map/ppermute | solution.py:302
  86.9 6.6 %collective-permute-start.10 = (f32[152,256]{1,0:T(8,128)S(1)}, f32[152,256]{1,0:T(8,128)S(1)}, u32[]{:S(2)}, u32[]{:S(2)}) collective-permute-start(f32[152,256]{1,0:T(8,128)S(1)} %get-tuple-element.99), channel_id=1, source_target_pairs={{0,6},{1,7},{2,4},{3,5},{4,2},{5,3},{6,0},{7,1},{8,14},{9,15},{10,... | collective-permute-start | bytes 466952 | tf_op jit(solution)/shard_map/ppermute | solution.py:368
  89.7 4.9 %collective-permute-start.8 = (f32[152,256]{1,0:T(8,128)S(1)}, f32[152,256]{1,0:T(8,128)S(1)}, u32[]{:S(2)}, u32[]{:S(2)}) collective-permute-start(f32[152,256]{1,0:T(8,128)S(1)} %get-tuple-element.100), channel_id=1, source_target_pairs={{0,2},{1,3},{2,0},{3,1},{4,6},{5,7},{6,4},{7,5},{8,10},{9,11},{10,... | collective-permute-start | bytes 466952 | tf_op jit(solution)/shard_map/ppermute | solution.py:368
  94.7 4.2 %collective-permute-start.11 = (f32[152,256]{1,0:T(8,128)S(1)}, f32[152,256]{1,0:T(8,128)S(1)}, u32[]{:S(2)}, u32[]{:S(2)}) collective-permute-start(f32[152,256]{1,0:T(8,128)S(1)} %get-tuple-element.97), channel_id=1, source_target_pairs={{0,2},{1,3},{2,0},{3,1},{4,6},{5,7},{6,4},{7,5},{8,10},{9,11},{10,... | collective-permute-start | bytes 466952 | tf_op jit(solution)/shard_map/ppermute | solution.py:368
  94.9 6.7 %collective-permute-start.9 = (f32[152,256]{1,0:T(8,128)S(1)}, f32[152,256]{1,0:T(8,128)S(1)}, u32[]{:S(2)}, u32[]{:S(2)}) collective-permute-start(f32[152,256]{1,0:T(8,128)S(1)} %get-tuple-element.98), channel_id=1, source_target_pairs={{0,6},{1,7},{2,4},{3,5},{4,2},{5,3},{6,0},{7,1},{8,14},{9,15},{10,... | collective-permute-start | bytes 466952 | tf_op jit(solution)/shard_map/ppermute | solution.py:368
  98.9 4.2 %collective-permute-start.13 = (f32[152,256]{1,0:T(8,128)S(1)}, f32[152,256]{1,0:T(8,128)S(1)}, u32[]{:S(2)}, u32[]{:S(2)}) collective-permute-start(f32[152,256]{1,0:T(8,128)S(1)} %add.45.m1), channel_id=1, source_target_pairs={{0,1},{1,0},{2,3},{3,2},{4,5},{5,4},{6,7},{7,6},{8,9},{9,8},{10,11... | collective-permute-start | bytes 466952 | tf_op jit(solution)/shard_map/ppermute | solution.py:369
  142.2 4.2 %collective-permute-start.16 = (bf16[8,80,128]{2,1,0:T(8,128)(2,1)S(1)}, bf16[8,80,128]{2,1,0:T(8,128)(2,1)S(1)}, u32[]{:S(2)}, u32[]{:S(2)}) collective-permute-start(bf16[8,80,128]{2,1,0:T(8,128)(2,1)S(1)} %all_to_all.62.g0), channel_id=1, source_target_pairs={{0,192},{8,200},{16,208},{24,216},{32,224},{40,232},{48,240},{56,2... | collective-permute-start | bytes 491528 | tf_op jit(solution)/shard_map/ppermute | solution.py:302
  143.5 5.8 %collective-permute-start.15 = (bf16[8,80,128]{2,1,0:T(8,128)(2,1)S(1)}, bf16[8,80,128]{2,1,0:T(8,128)(2,1)S(1)}, u32[]{:S(2)}, u32[]{:S(2)}) collective-permute-start(bf16[8,80,128]{2,1,0:T(8,128)(2,1)S(1)} %all_to_all.62.g0), channel_id=1, source_target_pairs={{0,128},{8,136},{16,144},{24,152},{32,160},{40,168},{48,176},{56,1... | collective-permute-start | bytes 491528 | tf_op jit(solution)/shard_map/ppermute | solution.py:302
  144.6 6.8 %collective-permute-start.14 = (bf16[8,80,128]{2,1,0:T(8,128)(2,1)S(1)}, bf16[8,80,128]{2,1,0:T(8,128)(2,1)S(1)}, u32[]{:S(2)}, u32[]{:S(2)}) collective-permute-start(bf16[8,80,128]{2,1,0:T(8,128)(2,1)S(1)} %all_to_all.62.g0), channel_id=1, source_target_pairs={{0,64},{8,72},{16,80},{24,88},{32,96},{40,104},{48,112},{56,120},{... | collective-permute-start | bytes 491528 | tf_op jit(solution)/shard_map/ppermute | solution.py:302
  186.0 6.0 %collective-permute-start.19 = (bf16[8,80,128]{2,1,0:T(8,128)(2,1)S(1)}, bf16[8,80,128]{2,1,0:T(8,128)(2,1)S(1)}, u32[]{:S(2)}, u32[]{:S(2)}) collective-permute-start(bf16[8,80,128]{2,1,0:T(8,128)(2,1)S(1)} %all_to_all.64.g0), channel_id=1, source_target_pairs={{0,192},{8,200},{16,208},{24,216},{32,224},{40,232},{48,240},{56,2... | collective-permute-start | bytes 491528 | tf_op jit(solution)/shard_map/ppermute | solution.py:302
  187.9 5.8 %collective-permute-start.18 = (bf16[8,80,128]{2,1,0:T(8,128)(2,1)S(1)}, bf16[8,80,128]{2,1,0:T(8,128)(2,1)S(1)}, u32[]{:S(2)}, u32[]{:S(2)}) collective-permute-start(bf16[8,80,128]{2,1,0:T(8,128)(2,1)S(1)} %all_to_all.64.g0), channel_id=1, source_target_pairs={{0,128},{8,136},{16,144},{24,152},{32,160},{40,168},{48,176},{56,1... | collective-permute-start | bytes 491528 | tf_op jit(solution)/shard_map/ppermute | solution.py:302
  188.9 6.5 %collective-permute-start.17 = (bf16[8,80,128]{2,1,0:T(8,128)(2,1)S(1)}, bf16[8,80,128]{2,1,0:T(8,128)(2,1)S(1)}, u32[]{:S(2)}, u32[]{:S(2)}) collective-permute-start(bf16[8,80,128]{2,1,0:T(8,128)(2,1)S(1)} %all_to_all.64.g0), channel_id=1, source_target_pairs={{0,64},{8,72},{16,80},{24,88},{32,96},{40,104},{48,112},{56,120},{... | collective-permute-start | bytes 491528 | tf_op jit(solution)/shard_map/ppermute | solution.py:302
  197.8 8.6 %collective-permute-start.20 = (f32[152,512]{1,0:T(8,128)S(1)}, f32[152,512]{1,0:T(8,128)S(1)}, u32[]{:S(2)}, u32[]{:S(2)}) collective-permute-start(f32[152,512]{1,0:T(8,128)S(1)} %get-tuple-element.74), channel_id=1, source_target_pairs={{0,1},{1,0},{2,3},{3,2},{4,5},{5,4},{6,7},{7,6},{8,9},{9,8},{10,11... | collective-permute-start | bytes 933896 | tf_op jit(solution)/shard_map/ppermute | solution.py:363
  206.5 6.5 %collective-permute-start.23 = (f32[152,256]{1,0:T(8,128)S(1)}, f32[152,256]{1,0:T(8,128)S(1)}, u32[]{:S(2)}, u32[]{:S(2)}) collective-permute-start(f32[152,256]{1,0:T(8,128)S(1)} %get-tuple-element.95), channel_id=1, source_target_pairs={{0,6},{1,7},{2,4},{3,5},{4,2},{5,3},{6,0},{7,1},{8,14},{9,15},{10,... | collective-permute-start | bytes 466952 | tf_op jit(solution)/shard_map/ppermute | solution.py:368
  207.6 5.4 %collective-permute-start.21 = (f32[152,256]{1,0:T(8,128)S(1)}, f32[152,256]{1,0:T(8,128)S(1)}, u32[]{:S(2)}, u32[]{:S(2)}) collective-permute-start(f32[152,256]{1,0:T(8,128)S(1)} %get-tuple-element.96), channel_id=1, source_target_pairs={{0,2},{1,3},{2,0},{3,1},{4,6},{5,7},{6,4},{7,5},{8,10},{9,11},{10,... | collective-permute-start | bytes 466952 | tf_op jit(solution)/shard_map/ppermute | solution.py:368
  213.1 4.2 %collective-permute-start.24 = (f32[152,256]{1,0:T(8,128)S(1)}, f32[152,256]{1,0:T(8,128)S(1)}, u32[]{:S(2)}, u32[]{:S(2)}) collective-permute-start(f32[152,256]{1,0:T(8,128)S(1)} %get-tuple-element.93), channel_id=1, source_target_pairs={{0,2},{1,3},{2,0},{3,1},{4,6},{5,7},{6,4},{7,5},{8,10},{9,11},{10,... | collective-permute-start | bytes 466952 | tf_op jit(solution)/shard_map/ppermute | solution.py:368
  213.2 6.6 %collective-permute-start.22 = (f32[152,256]{1,0:T(8,128)S(1)}, f32[152,256]{1,0:T(8,128)S(1)}, u32[]{:S(2)}, u32[]{:S(2)}) collective-permute-start(f32[152,256]{1,0:T(8,128)S(1)} %get-tuple-element.94), channel_id=1, source_target_pairs={{0,6},{1,7},{2,4},{3,5},{4,2},{5,3},{6,0},{7,1},{8,14},{9,15},{10,... | collective-permute-start | bytes 466952 | tf_op jit(solution)/shard_map/ppermute | solution.py:368
  217.3 4.0 %collective-permute-start.26 = (f32[152,256]{1,0:T(8,128)S(1)}, f32[152,256]{1,0:T(8,128)S(1)}, u32[]{:S(2)}, u32[]{:S(2)}) collective-permute-start(f32[152,256]{1,0:T(8,128)S(1)} %add.50.m1), channel_id=1, source_target_pairs={{0,1},{1,0},{2,3},{3,2},{4,5},{5,4},{6,7},{7,6},{8,9},{9,8},{10,11... | collective-permute-start | bytes 466952 | tf_op jit(solution)/shard_map/ppermute | solution.py:369
  258.2 4.2 %collective-permute-start.29 = (bf16[8,80,128]{2,1,0:T(8,128)(2,1)S(1)}, bf16[8,80,128]{2,1,0:T(8,128)(2,1)S(1)}, u32[]{:S(2)}, u32[]{:S(2)}) collective-permute-start(bf16[8,80,128]{2,1,0:T(8,128)(2,1)S(1)} %all_to_all.66.g0), channel_id=1, source_target_pairs={{0,192},{8,200},{16,208},{24,216},{32,224},{40,232},{48,240},{56,2... | collective-permute-start | bytes 491528 | tf_op jit(solution)/shard_map/ppermute | solution.py:302
  259.5 5.8 %collective-permute-start.28 = (bf16[8,80,128]{2,1,0:T(8,128)(2,1)S(1)}, bf16[8,80,128]{2,1,0:T(8,128)(2,1)S(1)}, u32[]{:S(2)}, u32[]{:S(2)}) collective-permute-start(bf16[8,80,128]{2,1,0:T(8,128)(2,1)S(1)} %all_to_all.66.g0), channel_id=1, source_target_pairs={{0,128},{8,136},{16,144},{24,152},{32,160},{40,168},{48,176},{56,1... | collective-permute-start | bytes 491528 | tf_op jit(solution)/shard_map/ppermute | solution.py:302
  260.8 6.5 %collective-permute-start.27 = (bf16[8,80,128]{2,1,0:T(8,128)(2,1)S(1)}, bf16[8,80,128]{2,1,0:T(8,128)(2,1)S(1)}, u32[]{:S(2)}, u32[]{:S(2)}) collective-permute-start(bf16[8,80,128]{2,1,0:T(8,128)(2,1)S(1)} %all_to_all.66.g0), channel_id=1, source_target_pairs={{0,64},{8,72},{16,80},{24,88},{32,96},{40,104},{48,112},{56,120},{... | collective-permute-start | bytes 491528 | tf_op jit(solution)/shard_map/ppermute | solution.py:302
  302.1 6.0 %collective-permute-start.32 = (bf16[8,80,128]{2,1,0:T(8,128)(2,1)S(1)}, bf16[8,80,128]{2,1,0:T(8,128)(2,1)S(1)}, u32[]{:S(2)}, u32[]{:S(2)}) collective-permute-start(bf16[8,80,128]{2,1,0:T(8,128)(2,1)S(1)} %all_to_all.68.g0), channel_id=1, source_target_pairs={{0,192},{8,200},{16,208},{24,216},{32,224},{40,232},{48,240},{56,2... | collective-permute-start | bytes 491528 | tf_op jit(solution)/shard_map/ppermute | solution.py:302
  304.0 5.8 %collective-permute-start.31 = (bf16[8,80,128]{2,1,0:T(8,128)(2,1)S(1)}, bf16[8,80,128]{2,1,0:T(8,128)(2,1)S(1)}, u32[]{:S(2)}, u32[]{:S(2)}) collective-permute-start(bf16[8,80,128]{2,1,0:T(8,128)(2,1)S(1)} %all_to_all.68.g0), channel_id=1, source_target_pairs={{0,128},{8,136},{16,144},{24,152},{32,160},{40,168},{48,176},{56,1... | collective-permute-start | bytes 491528 | tf_op jit(solution)/shard_map/ppermute | solution.py:302
  305.1 6.4 %collective-permute-start.30 = (bf16[8,80,128]{2,1,0:T(8,128)(2,1)S(1)}, bf16[8,80,128]{2,1,0:T(8,128)(2,1)S(1)}, u32[]{:S(2)}, u32[]{:S(2)}) collective-permute-start(bf16[8,80,128]{2,1,0:T(8,128)(2,1)S(1)} %all_to_all.68.g0), channel_id=1, source_target_pairs={{0,64},{8,72},{16,80},{24,88},{32,96},{40,104},{48,112},{56,120},{... | collective-permute-start | bytes 491528 | tf_op jit(solution)/shard_map/ppermute | solution.py:302
  314.6 8.6 %collective-permute-start.33 = (f32[4,152,128]{2,1,0:T(8,128)S(1)}, f32[4,152,128]{2,1,0:T(8,128)S(1)}, u32[]{:S(2)}, u32[]{:S(2)}) collective-permute-start(f32[4,152,128]{2,1,0:T(8,128)S(1)} %get-tuple-element.82), channel_id=1, source_target_pairs={{0,1},{1,0},{2,3},{3,2},{4,5},{5,4},{6,7},{7,6},{8,9},{9,8},{10,11... | collective-permute-start | bytes 933896 | tf_op jit(solution)/shard_map/ppermute | solution.py:422
  (7 other events, 73.9 us)

commit v4 on v3

--- a/solution.py
+++ b/solution.py
@@ -43,7 +43,7 @@
     return [(y * CORES + k, (y + d) % Y * CORES + k) for y in range(Y) for k in range(CORES)]
 
 
-def call(kernel, outs, scratch=(), name=None, scalars=0):
+def call(kernel, outs, scratch=(), name=None, scalars=0, last_scalar=False):
     vmem = pl.BlockSpec(memory_space=pltpu.VMEM)
     smem = pl.BlockSpec(memory_space=pltpu.SMEM)
     many = isinstance(outs, (list, tuple))
@@ -51,7 +51,7 @@
         kernel,
         out_shape=outs,
         in_specs=[smem] * scalars + [vmem] * (len(args) - scalars),
-        out_specs=[vmem] * len(outs) if many else vmem,
+        out_specs=([vmem] * (len(outs) - last_scalar) + [smem] * last_scalar) if many else vmem,
         scratch_shapes=list(scratch),
         compiler_params=pltpu.CompilerParams(vmem_limit_bytes=GRANT),
         cost_estimate=pl.CostEstimate(flops=FLOPS, bytes_accessed=2**22, transcendentals=0),
@@ -88,58 +88,54 @@
     return lax.dot_general(a, b, (((1,), (1,)), ((), ())), preferred_element_type=F32)
 
 
-def block_ranks(index_ref, rank_ref, rows):
+def block_ranks(owner):
     before = lax.broadcasted_iota(jnp.int32, (PART, PART), 0) < lax.broadcasted_iota(
         jnp.int32, (PART, PART), 1
     )
     before = jnp.where(before, 1.0, 0.0).astype(BF16)
-    owners = lax.broadcasted_iota(jnp.int32, (X * Z, PART), 0)
-
-    def block(b, top):
-        cols = pl.ds(pl.multiple_of(b * PART, PART), PART)
-        owned = jnp.where(lax.div(index_ref[:, cols], rows) == owners, 1.0, 0.0)
-        rank = jnp.sum(dot(owned.astype(BF16), before) * owned, axis=0, keepdims=True)
-        rank_ref[:, cols] = rank
-        return jnp.maximum(top, rank)
-
-    return lax.fori_loop(0, rank_ref.shape[1] // PART, block, jnp.zeros((1, PART), F32))
+    owned = [jnp.where(owner == device, 1.0, 0.0) for device in range(X * Z)]
+    earlier = dot(jnp.concatenate(owned, axis=0).astype(BF16), before)
+    blocks = owner.shape[0]
+    return sum(
+        one * earlier[device * blocks : (device + 1) * blocks] for device, one in enumerate(owned)
+    )
 
 
 def select_kernel(turn_ref, feat_ref, index_ref, out_ref, rank_ref, top_ref, hot_ref):
     rows = feat_ref.shape[1]
+    blocks = index_ref.shape[0]
     half = FPAD // 2
-    top_ref[...] = jnp.broadcast_to(
-        jnp.max(block_ranks(index_ref, rank_ref, rows), axis=1, keepdims=True), top_ref.shape
-    )
+    rank = block_ranks(lax.div(index_ref[...], rows))
+    rank_ref[...] = rank
+    top_ref[0] = jnp.max(rank).astype(jnp.int32)
     first = lax.axis_index("rows") * rows
     skip = (turn_ref[0] * SLOTS).astype(F32)
     slots = lax.broadcasted_iota(jnp.int32, (SLOTS, PART), 0).astype(F32)
     places = lax.broadcasted_iota(jnp.int32, (SLOTS, rows), 1).astype(F32)
-
-    @pl.loop(0, rank_ref.shape[1] // PART)
-    def _(b):
-        cols = pl.ds(pl.multiple_of(b * PART, PART), PART)
-        local = index_ref[:, cols] - first
+    out_ref[...] = jnp.zeros_like(out_ref)
+
+    def find(b, _):
+        local = index_ref[pl.ds(b, 1), :] - first
         inside = (local >= 0) & (local < rows)
-        chosen = inside & (rank_ref[:, cols] - skip == slots)
-        place = jnp.sum(
-            jnp.where(chosen, (local + 1).astype(F32), 0.0), axis=1, keepdims=True
-        )
-        hot_ref[pl.ds(pl.multiple_of(b * SLOTS, SLOTS), SLOTS), :] = jnp.where(places == place - 1.0, 1.0, 0.0).astype(BF16)
-    out_ref[...] = jnp.zeros_like(out_ref)
+        chosen = inside & (rank_ref[pl.ds(b, 1), :] - skip == slots)
+        place = jnp.sum(jnp.where(chosen, (local + 1).astype(F32), 0.0), axis=1, keepdims=True)
+        hot = jnp.where(places == place - 1.0, 1.0, 0.0).astype(BF16)
+        hot_ref[pl.ds(pl.multiple_of(b * SLOTS, SLOTS), SLOTS), :] = hot
+        return 0
+
+    lax.fori_loop(0, blocks, find, 0, unroll=4)
     for h, stop in ((0, half), (1, FEAT)):
         got = dot_nt(hot_ref[...], feat_ref[h * half : stop, :]).astype(BF16)
-        for b in range(rank_ref.shape[1] // PART):
+        for b in range(blocks):
             to = b // 4 * Z + h * 4 + b % 4
             out_ref[to, :, : stop - h * half] = got[b * SLOTS : (b + 1) * SLOTS]
 
 
 def place_kernel(turn_ref, in_ref, index_ref, rank_ref, out_ref, *, rows):
     me = lax.axis_index("rows")
-    block = lax.div(me, Z) * 4 + lax.rem(me, 4)
-    cols = pl.ds(pl.multiple_of(block * PART, PART), PART)
-    rank = rank_ref[:, cols].astype(jnp.int32) - turn_ref[0] * SLOTS
-    slot = lax.div(index_ref[:, cols], rows) * SLOTS + rank
+    block = pl.ds(lax.div(me, Z) * 4 + lax.rem(me, 4), 1)
+    rank = rank_ref[block, :].astype(jnp.int32) - turn_ref[0] * SLOTS
+    slot = lax.div(index_ref[block, :], rows) * SLOTS + rank
     slot = jnp.where((rank >= 0) & (rank < SLOTS), slot, -1)
     count = in_ref.shape[0] * SLOTS
     hot = lax.broadcasted_iota(jnp.int32, (count, PART), 0) == slot
@@ -310,39 +306,29 @@
 
 def gather_centers(features, center_index):
     rows = features.shape[1]
-    centers = center_index.shape[1]
+    index = center_index.reshape(-1, PART)
 
     def select(turn):
         return call(
             select_kernel,
-            [
-                like((X * Z, SLOTS, 256), BF16),
-                like((1, centers), F32),
-                like((8, LANES), F32),
-            ],
-            [pltpu.VMEM((centers // PART * SLOTS, rows), BF16)],
+            [like((X * Z, SLOTS, 256), BF16), like(index.shape, F32), like((1,), jnp.int32)],
+            [pltpu.VMEM((index.shape[0] * SLOTS, rows), BF16)],
             name="select",
             scalars=1,
-        )(turn, features, center_index)
+            last_scalar=True,
+        )(turn, features, index)
 
     def place(turn, pieces, rank):
-        arrived = exchange(pieces, "rows")
         return call(
             functools.partial(place_kernel, rows=rows),
             like((Z, FPAD // 2, PART), BF16),
             name="place",
             scalars=1,
-        )(turn, arrived, center_index, rank)
+        )(turn, exchange(pieces, "rows"), index, rank)
 
     start = jnp.zeros((1,), jnp.int32)
     pieces, rank, top = select(start)
-    top = jnp.maximum(top, lax.ppermute(top, "centers", CORE_SWAP))
-    pieces, top = lax.optimization_barrier((pieces, top))
-    tops = [lax.ppermute(top, "centers", y_shift(d)) for d in (2, 1, 3)]
     copies = place(start, pieces, rank)
-    for other in tops:
-        top = jnp.maximum(top, other)
-    last = top[0, 0].astype(jnp.int32)
 
     def another(state):
         turn, copies = state
@@ -350,7 +336,7 @@
         return turn + 1, copies + place(turn, pieces, rank)
 
     _, copies = lax.while_loop(
-        lambda state: state[0][0] * SLOTS <= last, another, (start + 1, copies)
+        lambda state: state[0][0] * SLOTS <= top[0], another, (start + 1, copies)
     )
     return gather(copies)
 

time: 334 us -> 330 us (0.988)
  waiting for transfers between devices: 71.7 us -> 77.3 us
  starting transfers between devices: 62 us -> 58 us
    all_to_all x1, waiting for transfers between devices: 6.19 us -> 14.5 us  [exchange(): lax.all_to_all(value, axis, split_axis=0, concat_axis=0, tiled=True, axis...]
    ppermute x4 -> x0, starting transfers between devices: 7.66 us -> none  [the longest x3 4.46 us: gather_centers(): tops = [lax.ppermute(top, 'centers', y_shift(d)) for d in (2, 1, 3)]]
  transfers between devices with their start and end apart: 35 -> 31, of which waited for: 29 -> 25; matrix products, arithmetic and copies ran while one was open for 1% -> 1% of each run, Pallas kernels for 1% -> 1%
where the time goes in v4:
time: 330 us
  blocking collectives  159 us (48%)
  waiting for transfers between devices  77.3 us (23%)
  starting transfers between devices  58 us (18%)
  Pallas kernels  30.3 us (9%)
    all_to_all x10, blocking collectives, exchange(): lax.all_to_all(value, axis, split_axis=0, concat_axis=0, tiled=True, axis...  159 us
    ppermute x15, waiting for transfers between devices, gather(): lax.ppermute(mine, 'rows', x_shift(d))  41.6 us
    pallas_call x16, Pallas kernels, call(): pl.pallas_call(kernel, out_shape=outs, in_specs=[smem] * scalars + [vmem]...  30.3 us
    ppermute x15, starting transfers between devices, gather(): lax.ppermute(mine, 'rows', x_shift(d))  15.6 us
    ppermute x8, waiting for transfers between devices, sum_over_groups(): lax.ppermute(p, 'centers', step)  15.4 us
    all_to_all x1, waiting for transfers between devices, exchange(): lax.all_to_all(value, axis, split_axis=0, concat_axis=0, tiled=True, axis...  14.5 us
    all_to_all x1, starting transfers between devices, exchange(): lax.all_to_all(value, axis, split_axis=0, concat_axis=0, tiled=True, axis...  11.9 us
    ppermute x4, starting transfers between devices, sum_over_groups(): return parts + [lax.ppermute(p, 'centers', CORE_SWAP) for p in parts]  8.15 us
  transfers between devices with their start and end apart: 31, of which 25 were waited for; matrix products, arithmetic and copies ran while one was open for 1% of the time, Pallas kernels for 1%

profile of v4, /device:TPU:1, one launch (start us, length us, event | category | flops | bytes accessed | tf_op | source)
XLA Modules:
  0.0 329.8 jit_solution(10923571100261271636)
XLA Ops:
  0.6 3.6 %select.3 = (bf16[32,32,256]{2,1,0:T(8,128)(2,1)}, f32[16,128]{1,0:T(8,128)S(1)}, s32[1]{0:T(128)}) custom-call(s32[1]{0:T(128)} %constant.13.clone.1.turn_ref, bf16[440,1024]{1,0:T(8,128)(2,1)} %feat_ref.1, s32[16,128]{1,0:T(8,128)} %bitcast.14), custom_call_target="tpu_custom_call" | custom-call | flops 1073741824 | bytes 4194304 | tf_op jit(solution)/shard_map/select/pallas_call | solution.py:50
  4.2 11.9 %all-to-all-start.1 = ((bf16[32,32,256]{2,1,0:T(8,128)(2,1)}), bf16[32,32,256]{2,1,0:T(8,128)(2,1)S(1)}, u32[]{:S(2)}, u32[]{:S(2)}) async-start(bf16[32,32,256]{2,1,0:T(8,128)(2,1)} %get-tuple-element.55), calls=%async_computation.1 | async-start | bytes 1048576 | tf_op jit(solution)/shard_map/all_to_all | solution.py:291
  16.1 14.5 %all-to-all-done.1.in_ref = bf16[32,32,256]{2,1,0:T(8,128)(2,1)S(1)} async-done(((bf16[32,32,256]{2,1,0:T(8,128)(2,1)}), bf16[32,32,256]{2,1,0:T(8,128)(2,1)S(1)}, u32[]{:S(2)}, u32[]{:S(2)}) %all-to-all-start.1) | async-done | bytes 524320 | tf_op jit(solution)/shard_map/all_to_all | solution.py:291
  32.4 18.0 %all_to_all.60.c_ref = bf16[8,224,128]{2,1,0:T(8,128)(2,1)S(1)} all-to-all(bf16[8,224,128]{2,1,0:T(8,128)(2,1)S(1)} %get-tuple-element.58), channel_id=1, replica_groups={{0,8,16,24,32,40,48,56},{64,72,80,88,96,104,112,120},{128,136,144,152,1..., dimensions={0} | all-to-all | bytes 917504 | tf_op jit(solution)/shard_map/all_to_all | solution.py:291
  50.4 2.9 collective-permute-start.2
  58.0 4.5 %collective-permute-done.2.c_ref = bf16[8,224,128]{2,1,0:T(8,128)(2,1)S(1)} collective-permute-done((bf16[8,224,128]{2,1,0:T(8,128)(2,1)S(1)}, bf16[8,224,128]{2,1,0:T(8,128)(2,1)S(1)}, u32[]{:S(2)}, u32[]{:S(2)}) %collective-permute-start.2) | collective-permute-done | bytes 458784 | tf_op jit(solution)/shard_map/ppermute | solution.py:298
  65.4 11.6 %collective-permute-done.c_ref = bf16[8,224,128]{2,1,0:T(8,128)(2,1)S(1)} collective-permute-done((bf16[8,224,128]{2,1,0:T(8,128)(2,1)S(1)}, bf16[8,224,128]{2,1,0:T(8,128)(2,1)S(1)}, u32[]{:S(2)}, u32[]{:S(2)}) %collective-permute-start) | collective-permute-done | bytes 458784 | tf_op jit(solution)/shard_map/ppermute | solution.py:298
  77.0 3.9 %build.1 = (bf16[1024,2048]{1,0:T(8,128)(2,1)S(1)}, f32[160,2048]{1,0:T(8,128)S(1)}, f32[160,1024]{1,0:T(8,128)S(1)}, f32[152,512]{1,0:T(8,128)S(1)}, f32[152,512]{1,0:T(8,128)S(1)}) custom-call(bf16[1024,448]{1,0:T(8,128)(2,1)S(1)} %pad_bitcast_fusion.feat_ref, f32[1024,1]{1,0:T(8,128)S(1)} %copy.11.norm_ref, ...), custom_call_target="tpu_custom_call" | custom-call | flops 1073741824 | bytes 4194304 | tf_op jit(solution)/shard_map/build/pallas_call | solution.py:50
  82.8 2.8 collective-permute-start.6
  85.6 3.8 %collective-permute-done.6 = f32[152,256]{1,0:T(8,128)S(1)} collective-permute-done((f32[152,256]{1,0:T(8,128)S(1)}, f32[152,256]{1,0:T(8,128)S(1)}, u32[]{:S(2)}, u32[]{:S(2)}) %collective-permute-start.6) | collective-permute-done | bytes 155680 | tf_op jit(solution)/shard_map/ppermute | solution.py:354
  94.8 2.8 collective-permute-start.9
  102.1 22.3 %all_to_all.61.in_ref = bf16[32,80,128]{2,1,0:T(8,128)(2,1)S(1)} all-to-all(bf16[32,80,128]{2,1,0:T(8,128)(2,1)S(1)} %get-tuple-element.64), channel_id=1, replica_groups=mesh['rows'=32,'centers'=8] {'rows'}, dimensions={0} | all-to-all | bytes 1310720 | tf_op jit(solution)/shard_map/all_to_all | solution.py:291
  124.5 14.3 %all_to_all.62.g0 = bf16[8,80,128]{2,1,0:T(8,128)(2,1)S(1)} all-to-all(bf16[8,80,128]{2,1,0:T(8,128)(2,1)S(1)} %sum_at_owner.4), channel_id=1, replica_groups={{0,8,16,24,32,40,48,56},{64,72,80,88,96,104,112,120},{128,136,144,152,1..., dimensions={0} | all-to-all | bytes 327680 | tf_op jit(solution)/shard_map/all_to_all | solution.py:291
  142.9 2.9 collective-permute-done.11.g2
  148.0 4.2 %second.2 = (bf16[32,80,128]{2,1,0:T(8,128)(2,1)S(1)}, f32[160,2048]{1,0:T(8,128)S(1)}) custom-call(f32[160,2048]{1,0:T(8,128)S(1)} %get-tuple-element.59.coef_ref, bf16[8,80,128]{2,1,0:T(8,128)(2,1)S(1)} %all_to_all.62.g0, bf16[8,80,128]{2,1,0:T(8,128)(2,1)S(1)} %collective-permute-done.10.g1, bf16[8,80,128]{2,1,0:T(8,128)(2,1)S(1)} %collective-permute-done.11.g2, ...), custom_call_target="tpu_custom_call" | custom-call | flops 1073741824 | bytes 4194304 | tf_op jit(solution)/shard_map/second/pallas_call | solution.py:50
  152.2 16.8 %all_to_all.63.in_ref = bf16[32,80,128]{2,1,0:T(8,128)(2,1)S(1)} all-to-all(bf16[32,80,128]{2,1,0:T(8,128)(2,1)S(1)} %get-tuple-element.67), channel_id=1, replica_groups=mesh['rows'=32,'centers'=8] {'rows'}, dimensions={0} | all-to-all | bytes 1310720 | tf_op jit(solution)/shard_map/all_to_all | solution.py:291
  169.1 13.5 %all_to_all.64.g0 = bf16[8,80,128]{2,1,0:T(8,128)(2,1)S(1)} all-to-all(bf16[8,80,128]{2,1,0:T(8,128)(2,1)S(1)} %sum_at_owner.5), channel_id=1, replica_groups={{0,8,16,24,32,40,48,56},{64,72,80,88,96,104,112,120},{128,136,144,152,1..., dimensions={0} | all-to-all | bytes 327680 | tf_op jit(solution)/shard_map/all_to_all | solution.py:291
  185.8 2.7 collective-permute-done.15.g3
  192.0 2.5 scores.1
  194.5 7.3 %collective-permute-start.16 = (f32[152,512]{1,0:T(8,128)S(1)}, f32[152,512]{1,0:T(8,128)S(1)}, u32[]{:S(2)}, u32[]{:S(2)}) collective-permute-start(f32[152,512]{1,0:T(8,128)S(1)} %get-tuple-element.70), channel_id=1, source_target_pairs={{0,1},{1,0},{2,3},{3,2},{4,5},{5,4},{6,7},{7,6},{8,9},{9,8},{10,11... | collective-permute-start | bytes 933896 | tf_op jit(solution)/shard_map/ppermute | solution.py:349
  204.2 5.4 %collective-permute-done.19 = f32[152,256]{1,0:T(8,128)S(1)} collective-permute-done((f32[152,256]{1,0:T(8,128)S(1)}, f32[152,256]{1,0:T(8,128)S(1)}, u32[]{:S(2)}, u32[]{:S(2)}) %collective-permute-start.19) | collective-permute-done | bytes 155680 | tf_op jit(solution)/shard_map/ppermute | solution.py:354
  211.2 2.6 collective-permute-done.20
  220.5 19.7 %all_to_all.65.in_ref = bf16[32,80,128]{2,1,0:T(8,128)(2,1)S(1)} all-to-all(bf16[32,80,128]{2,1,0:T(8,128)(2,1)S(1)} %get-tuple-element.72), channel_id=1, replica_groups=mesh['rows'=32,'centers'=8] {'rows'}, dimensions={0} | all-to-all | bytes 1310720 | tf_op jit(solution)/shard_map/all_to_all | solution.py:291
  240.4 14.5 %all_to_all.66.g0 = bf16[8,80,128]{2,1,0:T(8,128)(2,1)S(1)} all-to-all(bf16[8,80,128]{2,1,0:T(8,128)(2,1)S(1)} %sum_at_owner.6), channel_id=1, replica_groups={{0,8,16,24,32,40,48,56},{64,72,80,88,96,104,112,120},{128,136,144,152,1..., dimensions={0} | all-to-all | bytes 327680 | tf_op jit(solution)/shard_map/all_to_all | solution.py:291
  259.0 2.9 collective-permute-done.24.g2
  263.9 4.2 %second.3 = (bf16[32,80,128]{2,1,0:T(8,128)(2,1)S(1)}, f32[160,2048]{1,0:T(8,128)S(1)}) custom-call(f32[160,2048]{1,0:T(8,128)S(1)} %get-tuple-element.68.coef_ref, bf16[8,80,128]{2,1,0:T(8,128)(2,1)S(1)} %all_to_all.66.g0, bf16[8,80,128]{2,1,0:T(8,128)(2,1)S(1)} %collective-permute-done.23.g1, bf16[8,80,128]{2,1,0:T(8,128)(2,1)S(1)} %collective-permute-done.24.g2, ...), custom_call_target="tpu_custom_call" | custom-call | flops 1073741824 | bytes 4194304 | tf_op jit(solution)/shard_map/second/pallas_call | solution.py:50
  268.2 17.1 %all_to_all.67.in_ref = bf16[32,80,128]{2,1,0:T(8,128)(2,1)S(1)} all-to-all(bf16[32,80,128]{2,1,0:T(8,128)(2,1)S(1)} %get-tuple-element.75), channel_id=1, replica_groups=mesh['rows'=32,'centers'=8] {'rows'}, dimensions={0} | all-to-all | bytes 1310720 | tf_op jit(solution)/shard_map/all_to_all | solution.py:291
  285.4 13.3 %all_to_all.68.g0 = bf16[8,80,128]{2,1,0:T(8,128)(2,1)S(1)} all-to-all(bf16[8,80,128]{2,1,0:T(8,128)(2,1)S(1)} %sum_at_owner.7), channel_id=1, replica_groups={{0,8,16,24,32,40,48,56},{64,72,80,88,96,104,112,120},{128,136,144,152,1..., dimensions={0} | all-to-all | bytes 327680 | tf_op jit(solution)/shard_map/all_to_all | solution.py:291
  302.0 2.7 collective-permute-done.28.g3
  308.1 3.1 final.1
  311.2 7.3 %collective-permute-start.29 = (f32[4,152,128]{2,1,0:T(8,128)S(1)}, f32[4,152,128]{2,1,0:T(8,128)S(1)}, u32[]{:S(2)}, u32[]{:S(2)}) collective-permute-start(f32[4,152,128]{2,1,0:T(8,128)S(1)} %get-tuple-element.78), channel_id=1, source_target_pairs={{0,1},{1,0},{2,3},{3,2},{4,5},{5,4},{6,7},{7,6},{8,9},{9,8},{10,11... | collective-permute-start | bytes 933896 | tf_op jit(solution)/shard_map/ppermute | solution.py:408
  319.8 9.3 %all_to_all.69 = f32[4,152,128]{2,1,0:T(8,128)S(1)} all-to-all(f32[4,152,128]{2,1,0:T(8,128)S(1)} %add.51), channel_id=1, replica_groups={{0,2,4,6},{1,3,5,7},{8,10,12,14},{9,11,13,15},{16,18,20,22},{17,19,21,2..., dimensions={0} | all-to-all | bytes 622592 | tf_op jit(solution)/shard_map/all_to_all | solution.py:291
  (81 shorter events, 60.0 us)
Async XLA Ops:
  0.6 30.0 %copy-start.3 = (s32[1,2048]{1,0:T(1,128)S(1)}, s32[1,2048]{1,0:T(1,128)}, u32[]{:S(2)}) copy-start(s32[1,2048]{1,0:T(1,128)} %param.8) | copy-start | bytes 24580
  4.2 26.4 %all-to-all-start.1 = ((bf16[32,32,256]{2,1,0:T(8,128)(2,1)}), bf16[32,32,256]{2,1,0:T(8,128)(2,1)S(1)}, u32[]{:S(2)}, u32[]{:S(2)}) async-start(bf16[32,32,256]{2,1,0:T(8,128)(2,1)} %get-tuple-element.55), calls=%async_computation.1 | async-start | bytes 1048576 | tf_op jit(solution)/shard_map/all_to_all | solution.py:291
  50.4 12.1 %collective-permute-start.2 = (bf16[8,224,128]{2,1,0:T(8,128)(2,1)S(1)}, bf16[8,224,128]{2,1,0:T(8,128)(2,1)S(1)}, u32[]{:S(2)}, u32[]{:S(2)}) collective-permute-start(bf16[8,224,128]{2,1,0:T(8,128)(2,1)S(1)} %all_to_all.60.c_ref), channel_id=1, source_target_pairs={{0,192},{8,200},{16,208},{24,216},{32,224},{40,232},{48,240},{56,2... | collective-permute-start | bytes 1376264 | tf_op jit(solution)/shard_map/ppermute | solution.py:298
  53.2 10.7 %collective-permute-start.1 = (bf16[8,224,128]{2,1,0:T(8,128)(2,1)S(1)}, bf16[8,224,128]{2,1,0:T(8,128)(2,1)S(1)}, u32[]{:S(2)}, u32[]{:S(2)}) collective-permute-start(bf16[8,224,128]{2,1,0:T(8,128)(2,1)S(1)} %all_to_all.60.c_ref), channel_id=1, source_target_pairs={{0,128},{8,136},{16,144},{24,152},{32,160},{40,168},{48,176},{56,1... | collective-permute-start | bytes 1376264 | tf_op jit(solution)/shard_map/ppermute | solution.py:298
  53.7 23.3 %collective-permute-start = (bf16[8,224,128]{2,1,0:T(8,128)(2,1)S(1)}, bf16[8,224,128]{2,1,0:T(8,128)(2,1)S(1)}, u32[]{:S(2)}, u32[]{:S(2)}) collective-permute-start(bf16[8,224,128]{2,1,0:T(8,128)(2,1)S(1)} %all_to_all.60.c_ref), channel_id=1, source_target_pairs={{0,64},{8,72},{16,80},{24,88},{32,96},{40,104},{48,112},{56,120},{... | collective-permute-start | bytes 1376264 | tf_op jit(solution)/shard_map/ppermute | solution.py:298
  80.9 1.8 collective-permute-start.3
  82.8 6.6 %collective-permute-start.6 = (f32[152,256]{1,0:T(8,128)S(1)}, f32[152,256]{1,0:T(8,128)S(1)}, u32[]{:S(2)}, u32[]{:S(2)}) collective-permute-start(f32[152,256]{1,0:T(8,128)S(1)} %get-tuple-element.95), channel_id=1, source_target_pairs={{0,6},{1,7},{2,4},{3,5},{4,2},{5,3},{6,0},{7,1},{8,14},{9,15},{10,... | collective-permute-start | bytes 466952 | tf_op jit(solution)/shard_map/ppermute | solution.py:354
  85.6 4.9 %collective-permute-start.4 = (f32[152,256]{1,0:T(8,128)S(1)}, f32[152,256]{1,0:T(8,128)S(1)}, u32[]{:S(2)}, u32[]{:S(2)}) collective-permute-start(f32[152,256]{1,0:T(8,128)S(1)} %get-tuple-element.96), channel_id=1, source_target_pairs={{0,2},{1,3},{2,0},{3,1},{4,6},{5,7},{6,4},{7,5},{8,10},{9,11},{10,... | collective-permute-start | bytes 466952 | tf_op jit(solution)/shard_map/ppermute | solution.py:354
  90.6 4.2 %collective-permute-start.7 = (f32[152,256]{1,0:T(8,128)S(1)}, f32[152,256]{1,0:T(8,128)S(1)}, u32[]{:S(2)}, u32[]{:S(2)}) collective-permute-start(f32[152,256]{1,0:T(8,128)S(1)} %get-tuple-element.93), channel_id=1, source_target_pairs={{0,2},{1,3},{2,0},{3,1},{4,6},{5,7},{6,4},{7,5},{8,10},{9,11},{10,... | collective-permute-start | bytes 466952 | tf_op jit(solution)/shard_map/ppermute | solution.py:354
  90.8 6.7 %collective-permute-start.5 = (f32[152,256]{1,0:T(8,128)S(1)}, f32[152,256]{1,0:T(8,128)S(1)}, u32[]{:S(2)}, u32[]{:S(2)}) collective-permute-start(f32[152,256]{1,0:T(8,128)S(1)} %get-tuple-element.94), channel_id=1, source_target_pairs={{0,6},{1,7},{2,4},{3,5},{4,2},{5,3},{6,0},{7,1},{8,14},{9,15},{10,... | collective-permute-start | bytes 466952 | tf_op jit(solution)/shard_map/ppermute | solution.py:354
  94.8 4.4 %collective-permute-start.9 = (f32[152,256]{1,0:T(8,128)S(1)}, f32[152,256]{1,0:T(8,128)S(1)}, u32[]{:S(2)}, u32[]{:S(2)}) collective-permute-start(f32[152,256]{1,0:T(8,128)S(1)} %add.45.m1), channel_id=1, source_target_pairs={{0,1},{1,0},{2,3},{3,2},{4,5},{5,4},{6,7},{7,6},{8,9},{9,8},{10,11... | collective-permute-start | bytes 466952 | tf_op jit(solution)/shard_map/ppermute | solution.py:355
  97.5 2.7 collective-permute-start.8
  138.8 4.2 %collective-permute-start.12 = (bf16[8,80,128]{2,1,0:T(8,128)(2,1)S(1)}, bf16[8,80,128]{2,1,0:T(8,128)(2,1)S(1)}, u32[]{:S(2)}, u32[]{:S(2)}) collective-permute-start(bf16[8,80,128]{2,1,0:T(8,128)(2,1)S(1)} %all_to_all.62.g0), channel_id=1, source_target_pairs={{0,192},{8,200},{16,208},{24,216},{32,224},{40,232},{48,240},{56,2... | collective-permute-start | bytes 491528 | tf_op jit(solution)/shard_map/ppermute | solution.py:298
  140.1 5.8 %collective-permute-start.11 = (bf16[8,80,128]{2,1,0:T(8,128)(2,1)S(1)}, bf16[8,80,128]{2,1,0:T(8,128)(2,1)S(1)}, u32[]{:S(2)}, u32[]{:S(2)}) collective-permute-start(bf16[8,80,128]{2,1,0:T(8,128)(2,1)S(1)} %all_to_all.62.g0), channel_id=1, source_target_pairs={{0,128},{8,136},{16,144},{24,152},{32,160},{40,168},{48,176},{56,1... | collective-permute-start | bytes 491528 | tf_op jit(solution)/shard_map/ppermute | solution.py:298
  141.2 6.8 %collective-permute-start.10 = (bf16[8,80,128]{2,1,0:T(8,128)(2,1)S(1)}, bf16[8,80,128]{2,1,0:T(8,128)(2,1)S(1)}, u32[]{:S(2)}, u32[]{:S(2)}) collective-permute-start(bf16[8,80,128]{2,1,0:T(8,128)(2,1)S(1)} %all_to_all.62.g0), channel_id=1, source_target_pairs={{0,64},{8,72},{16,80},{24,88},{32,96},{40,104},{48,112},{56,120},{... | collective-permute-start | bytes 491528 | tf_op jit(solution)/shard_map/ppermute | solution.py:298
  182.6 6.0 %collective-permute-start.15 = (bf16[8,80,128]{2,1,0:T(8,128)(2,1)S(1)}, bf16[8,80,128]{2,1,0:T(8,128)(2,1)S(1)}, u32[]{:S(2)}, u32[]{:S(2)}) collective-permute-start(bf16[8,80,128]{2,1,0:T(8,128)(2,1)S(1)} %all_to_all.64.g0), channel_id=1, source_target_pairs={{0,192},{8,200},{16,208},{24,216},{32,224},{40,232},{48,240},{56,2... | collective-permute-start | bytes 491528 | tf_op jit(solution)/shard_map/ppermute | solution.py:298
  184.5 5.8 %collective-permute-start.14 = (bf16[8,80,128]{2,1,0:T(8,128)(2,1)S(1)}, bf16[8,80,128]{2,1,0:T(8,128)(2,1)S(1)}, u32[]{:S(2)}, u32[]{:S(2)}) collective-permute-start(bf16[8,80,128]{2,1,0:T(8,128)(2,1)S(1)} %all_to_all.64.g0), channel_id=1, source_target_pairs={{0,128},{8,136},{16,144},{24,152},{32,160},{40,168},{48,176},{56,1... | collective-permute-start | bytes 491528 | tf_op jit(solution)/shard_map/ppermute | solution.py:298
  185.5 6.5 %collective-permute-start.13 = (bf16[8,80,128]{2,1,0:T(8,128)(2,1)S(1)}, bf16[8,80,128]{2,1,0:T(8,128)(2,1)S(1)}, u32[]{:S(2)}, u32[]{:S(2)}) collective-permute-start(bf16[8,80,128]{2,1,0:T(8,128)(2,1)S(1)} %all_to_all.64.g0), channel_id=1, source_target_pairs={{0,64},{8,72},{16,80},{24,88},{32,96},{40,104},{48,112},{56,120},{... | collective-permute-start | bytes 491528 | tf_op jit(solution)/shard_map/ppermute | solution.py:298
  194.5 8.6 %collective-permute-start.16 = (f32[152,512]{1,0:T(8,128)S(1)}, f32[152,512]{1,0:T(8,128)S(1)}, u32[]{:S(2)}, u32[]{:S(2)}) collective-permute-start(f32[152,512]{1,0:T(8,128)S(1)} %get-tuple-element.70), channel_id=1, source_target_pairs={{0,1},{1,0},{2,3},{3,2},{4,5},{5,4},{6,7},{7,6},{8,9},{9,8},{10,11... | collective-permute-start | bytes 933896 | tf_op jit(solution)/shard_map/ppermute | solution.py:349
  203.1 6.5 %collective-permute-start.19 = (f32[152,256]{1,0:T(8,128)S(1)}, f32[152,256]{1,0:T(8,128)S(1)}, u32[]{:S(2)}, u32[]{:S(2)}) collective-permute-start(f32[152,256]{1,0:T(8,128)S(1)} %get-tuple-element.91), channel_id=1, source_target_pairs={{0,6},{1,7},{2,4},{3,5},{4,2},{5,3},{6,0},{7,1},{8,14},{9,15},{10,... | collective-permute-start | bytes 466952 | tf_op jit(solution)/shard_map/ppermute | solution.py:354
  204.2 5.4 %collective-permute-start.17 = (f32[152,256]{1,0:T(8,128)S(1)}, f32[152,256]{1,0:T(8,128)S(1)}, u32[]{:S(2)}, u32[]{:S(2)}) collective-permute-start(f32[152,256]{1,0:T(8,128)S(1)} %get-tuple-element.92), channel_id=1, source_target_pairs={{0,2},{1,3},{2,0},{3,1},{4,6},{5,7},{6,4},{7,5},{8,10},{9,11},{10,... | collective-permute-start | bytes 466952 | tf_op jit(solution)/shard_map/ppermute | solution.py:354
  209.7 4.2 %collective-permute-start.20 = (f32[152,256]{1,0:T(8,128)S(1)}, f32[152,256]{1,0:T(8,128)S(1)}, u32[]{:S(2)}, u32[]{:S(2)}) collective-permute-start(f32[152,256]{1,0:T(8,128)S(1)} %get-tuple-element.89), channel_id=1, source_target_pairs={{0,2},{1,3},{2,0},{3,1},{4,6},{5,7},{6,4},{7,5},{8,10},{9,11},{10,... | collective-permute-start | bytes 466952 | tf_op jit(solution)/shard_map/ppermute | solution.py:354
  209.8 6.6 %collective-permute-start.18 = (f32[152,256]{1,0:T(8,128)S(1)}, f32[152,256]{1,0:T(8,128)S(1)}, u32[]{:S(2)}, u32[]{:S(2)}) collective-permute-start(f32[152,256]{1,0:T(8,128)S(1)} %get-tuple-element.90), channel_id=1, source_target_pairs={{0,6},{1,7},{2,4},{3,5},{4,2},{5,3},{6,0},{7,1},{8,14},{9,15},{10,... | collective-permute-start | bytes 466952 | tf_op jit(solution)/shard_map/ppermute | solution.py:354
  213.9 3.8 %collective-permute-start.22 = (f32[152,256]{1,0:T(8,128)S(1)}, f32[152,256]{1,0:T(8,128)S(1)}, u32[]{:S(2)}, u32[]{:S(2)}) collective-permute-start(f32[152,256]{1,0:T(8,128)S(1)} %add.50.m1), channel_id=1, source_target_pairs={{0,1},{1,0},{2,3},{3,2},{4,5},{5,4},{6,7},{7,6},{8,9},{9,8},{10,11... | collective-permute-start | bytes 466952 | tf_op jit(solution)/shard_map/ppermute | solution.py:355
  216.4 2.3 collective-permute-start.21
  254.9 4.2 %collective-permute-start.25 = (bf16[8,80,128]{2,1,0:T(8,128)(2,1)S(1)}, bf16[8,80,128]{2,1,0:T(8,128)(2,1)S(1)}, u32[]{:S(2)}, u32[]{:S(2)}) collective-permute-start(bf16[8,80,128]{2,1,0:T(8,128)(2,1)S(1)} %all_to_all.66.g0), channel_id=1, source_target_pairs={{0,192},{8,200},{16,208},{24,216},{32,224},{40,232},{48,240},{56,2... | collective-permute-start | bytes 491528 | tf_op jit(solution)/shard_map/ppermute | solution.py:298
  256.1 5.8 %collective-permute-start.24 = (bf16[8,80,128]{2,1,0:T(8,128)(2,1)S(1)}, bf16[8,80,128]{2,1,0:T(8,128)(2,1)S(1)}, u32[]{:S(2)}, u32[]{:S(2)}) collective-permute-start(bf16[8,80,128]{2,1,0:T(8,128)(2,1)S(1)} %all_to_all.66.g0), channel_id=1, source_target_pairs={{0,128},{8,136},{16,144},{24,152},{32,160},{40,168},{48,176},{56,1... | collective-permute-start | bytes 491528 | tf_op jit(solution)/shard_map/ppermute | solution.py:298
  257.4 6.5 %collective-permute-start.23 = (bf16[8,80,128]{2,1,0:T(8,128)(2,1)S(1)}, bf16[8,80,128]{2,1,0:T(8,128)(2,1)S(1)}, u32[]{:S(2)}, u32[]{:S(2)}) collective-permute-start(bf16[8,80,128]{2,1,0:T(8,128)(2,1)S(1)} %all_to_all.66.g0), channel_id=1, source_target_pairs={{0,64},{8,72},{16,80},{24,88},{32,96},{40,104},{48,112},{56,120},{... | collective-permute-start | bytes 491528 | tf_op jit(solution)/shard_map/ppermute | solution.py:298
  298.7 6.0 %collective-permute-start.28 = (bf16[8,80,128]{2,1,0:T(8,128)(2,1)S(1)}, bf16[8,80,128]{2,1,0:T(8,128)(2,1)S(1)}, u32[]{:S(2)}, u32[]{:S(2)}) collective-permute-start(bf16[8,80,128]{2,1,0:T(8,128)(2,1)S(1)} %all_to_all.68.g0), channel_id=1, source_target_pairs={{0,192},{8,200},{16,208},{24,216},{32,224},{40,232},{48,240},{56,2... | collective-permute-start | bytes 491528 | tf_op jit(solution)/shard_map/ppermute | solution.py:298
  300.6 5.8 %collective-permute-start.27 = (bf16[8,80,128]{2,1,0:T(8,128)(2,1)S(1)}, bf16[8,80,128]{2,1,0:T(8,128)(2,1)S(1)}, u32[]{:S(2)}, u32[]{:S(2)}) collective-permute-start(bf16[8,80,128]{2,1,0:T(8,128)(2,1)S(1)} %all_to_all.68.g0), channel_id=1, source_target_pairs={{0,128},{8,136},{16,144},{24,152},{32,160},{40,168},{48,176},{56,1... | collective-permute-start | bytes 491528 | tf_op jit(solution)/shard_map/ppermute | solution.py:298
  301.7 6.4 %collective-permute-start.26 = (bf16[8,80,128]{2,1,0:T(8,128)(2,1)S(1)}, bf16[8,80,128]{2,1,0:T(8,128)(2,1)S(1)}, u32[]{:S(2)}, u32[]{:S(2)}) collective-permute-start(bf16[8,80,128]{2,1,0:T(8,128)(2,1)S(1)} %all_to_all.68.g0), channel_id=1, source_target_pairs={{0,64},{8,72},{16,80},{24,88},{32,96},{40,104},{48,112},{56,120},{... | collective-permute-start | bytes 491528 | tf_op jit(solution)/shard_map/ppermute | solution.py:298
  311.2 8.6 %collective-permute-start.29 = (f32[4,152,128]{2,1,0:T(8,128)S(1)}, f32[4,152,128]{2,1,0:T(8,128)S(1)}, u32[]{:S(2)}, u32[]{:S(2)}) collective-permute-start(f32[4,152,128]{2,1,0:T(8,128)S(1)} %get-tuple-element.78), channel_id=1, source_target_pairs={{0,1},{1,0},{2,3},{3,2},{4,5},{5,4},{6,7},{7,6},{8,9},{9,8},{10,11... | collective-permute-start | bytes 933896 | tf_op jit(solution)/shard_map/ppermute | solution.py:408
  (3 other events, 31.7 us)

commit v5 on v4

--- a/solution.py
+++ b/solution.py
@@ -21,7 +21,7 @@
 CHUNK = X * LANES
 PART = CHUNK // 4
 BLOCK = 256
-SLOTS = 32
+SLOTS = 16
 GRANT = 20 * 2**20
 FLOPS = 2**30
 
@@ -29,9 +29,7 @@
 BF16 = jnp.bfloat16
 LOG2E = 1.4426950408889634
 
-X_GROUPS = [[x * Z + z for x in range(X)] for z in range(Z)]
 Z_GROUPS = [[x * Z + z for z in range(Z)] for x in range(X)]
-Y_GROUPS = [[y * CORES + k for y in range(Y)] for k in range(CORES)]
 CORE_SWAP = [(y * CORES + k, y * CORES + 1 - k) for y in range(Y) for k in range(CORES)]
 
 
@@ -208,6 +206,29 @@
     split_halves(own_ref, keep_ref, send_ref)
 
 
+def encode_kernel(keep_ref, partner_ref, pair_ref, code_ref):
+    pair = keep_ref[...] + partner_ref[...]
+    pair_ref[...] = pair
+    largest = jnp.max(jnp.abs(pair), axis=0, keepdims=True)
+    exponent = jnp.clip(jnp.ceil(jnp.log2(jnp.maximum(largest, 1e-30))), -100.0, 120.0)
+    scaled = jnp.floor(pair * jnp.exp2(14.0 - exponent) + 0.5)
+    rest = jnp.broadcast_to(exponent, (PAD - WIRE, pair.shape[1]))
+    code_ref[...] = jnp.concatenate([scaled, rest], axis=0).astype(jnp.int32).astype(jnp.int16)
+
+
+def decode_kernel(pair_ref, c0, c1, c2, half_ref):
+    total = pair_ref[...]
+    for ref in (c0, c1, c2):
+        code = ref[...].astype(jnp.int32).astype(F32)
+        total = total + code[:WIRE] * jnp.exp2(code[WIRE : WIRE + 1] - 14.0)
+    half_ref[...] = total
+
+
+def add_kernel(keep_ref, partner_ref, *out_refs):
+    for d, ref in enumerate(out_refs):
+        ref[...] = keep_ref[d] + partner_ref[d]
+
+
 def residual_of(logits, labels):
     classes = lax.broadcasted_iota(jnp.int32, logits.shape, 0)
     logits = jnp.where(classes < CLASSES, logits, -1e30)
@@ -228,13 +249,13 @@
             out_ref[chunk_of(d) * Z + z] = grad[height, left : left + PART]
 
 
-def first_kernel(m0, m1, t0, t1, own_ref, kern_ref, label_ref, out_ref, base_ref, res_ref, sum_ref):
+def first_kernel(
+    mine_ref, theirs_ref, own_ref, kern_ref, label_ref, out_ref, base_ref, res_ref, sum_ref
+):
     core = my_core()
-    width = m0.shape[1]
-    for side, refs in ((core, (m0, m1)), (1 - core, (t0, t1))):
-        for i, ref in enumerate(refs):
-            to = pl.multiple_of((side * 2 + i) * width, width)
-            sum_ref[:WIRE, pl.ds(to, width)] = ref[...]
+    width = mine_ref.shape[1]
+    for side, ref in ((core, mine_ref), (1 - core, theirs_ref)):
+        sum_ref[:WIRE, pl.ds(pl.multiple_of(side * width, width), width)] = ref[...]
     for n in range(sum_ref.shape[1] // BLOCK):
         at = slice(n * BLOCK, (n + 1) * BLOCK)
         res_ref[:, at] = residual_of(sum_ref[:, at], label_ref[:, at])
@@ -282,9 +303,10 @@
         coef_out_ref[:, to] = new_ref[:CLASSES, cols]
     own_scores(low_ref, kern_ref, own_ref)
     core = my_core()
-    for y in range(Y):
+    for d in range(Y):
+        y = lax.rem(lax.div(lax.axis_index("centers"), CORES) + d, Y)
         for ref, k in ((keep_ref, core), (send_ref, 1 - core)):
-            ref[y] = own_ref[:WIRE, pl.ds(pl.multiple_of((y * CORES + k) * LANES, LANES), LANES)]
+            ref[d] = own_ref[:WIRE, pl.ds(pl.multiple_of((y * CORES + k) * LANES, LANES), LANES)]
 
 
 def exchange(value, axis, groups=None):
@@ -341,18 +363,15 @@
     return gather(copies)
 
 
-def pairwise(axis_map):
-    return [(y * CORES + k, axis_map(y) * CORES + k) for y in range(Y) for k in range(CORES)]
-
-
 def sum_over_groups(keep, send):
-    half = keep + lax.ppermute(send, "centers", CORE_SWAP)
-    width = half.shape[1] // 2
-    steps = (pairwise(lambda y: y ^ 1), pairwise(lambda y: Y - 1 - y))
-    parts = [half[:, :width], half[:, width:]]
-    for order in (steps, steps[::-1]):
-        parts = [p + lax.ppermute(p, "centers", step) for p, step in zip(parts, order)]
-    return parts + [lax.ppermute(p, "centers", CORE_SWAP) for p in parts]
+    partner = lax.ppermute(send, "centers", CORE_SWAP)
+    code_type = like((PAD, keep.shape[1]), jnp.int16)
+    pair, code = call(encode_kernel, [like(keep.shape, F32), code_type], name="encode")(
+        keep, partner
+    )
+    codes = [lax.ppermute(code, "centers", y_shift(d)) for d in (2, 1, 3)]
+    half = call(decode_kernel, like(keep.shape, F32), name="decode")(pair, *codes)
+    return half, lax.ppermute(half, "centers", CORE_SWAP)
 
 
 def body(features, labels, center_index, warm_coef):
@@ -405,8 +424,10 @@
         [coef_scratch, low, score],
         name="final",
     )(coef, *grads, kern)
-    part = keep + lax.ppermute(send, "centers", CORE_SWAP)
-    logits_out = exchange(part, "centers", Y_GROUPS).sum(axis=0)[:CLASSES]
+    partner = lax.ppermute(send, "centers", CORE_SWAP)
+    parts = call(add_kernel, [like((WIRE, LANES), F32)] * Y, name="pair")(keep, partner)
+    arrived = [lax.ppermute(parts[d], "centers", y_shift(d)) for d in (2, 1, 3)]
+    logits_out = (parts[0] + arrived[0] + (arrived[1] + arrived[2]))[:CLASSES]
     return coef_out, logits_out
 
 

time: 330 us -> 317 us (0.961)
  blocking collectives: 159 us -> 149 us
  waiting for transfers between devices: 77.3 us -> 73.5 us
    all_to_all x10 -> x9, blocking collectives: 159 us -> 149 us  [exchange(): lax.all_to_all(value, axis, split_axis=0, concat_axis=0, tiled=True, axis...]
    all_to_all x1, waiting for transfers between devices: 14.5 us -> 9.68 us  [exchange(): lax.all_to_all(value, axis, split_axis=0, concat_axis=0, tiled=True, axis...]
    ppermute x15 -> x14, waiting for transfers between devices: 21.1 us -> 23.7 us  [the longest x6 14.7 us: sum_over_groups(): codes = [lax.ppermute(code, 'centers', y_shift(d)) for d in (2, 1, 3)]]
    ppermute x15 -> x14, starting transfers between devices: 30.6 us -> 31.1 us  [the longest x2 8.16 us: sum_over_groups(): partner = lax.ppermute(send, 'centers', CORE_SWAP)]
    pallas_call x16 -> x21, Pallas kernels: 30.3 us -> 30.8 us  [call(): pl.pallas_call(kernel, out_shape=outs, in_specs=[smem] * scalars + [vmem]...]
  transfers between devices with their start and end apart: 31 -> 30, of which waited for: 25 -> 29; matrix products, arithmetic and copies ran while one was open for 1% -> 1% of each run, Pallas kernels for 1% -> 1%
where the time goes in v5:
time: 317 us; the launch traced here: 316 us
  blocking collectives  149 us (47%)
  waiting for transfers between devices  73.5 us (23%)
  starting transfers between devices  57.9 us (18%)
  Pallas kernels  30.8 us (10%)
    all_to_all x9, blocking collectives, exchange(): lax.all_to_all(value, axis, split_axis=0, concat_axis=0, tiled=True, axis...  149 us
    ppermute x15, waiting for transfers between devices, gather(): lax.ppermute(mine, 'rows', x_shift(d))  40.1 us
    pallas_call x21, Pallas kernels, call(): pl.pallas_call(kernel, out_shape=outs, in_specs=[smem] * scalars + [vmem]...  30.8 us
    ppermute x15, starting transfers between devices, gather(): lax.ppermute(mine, 'rows', x_shift(d))  14.9 us
    ppermute x6, waiting for transfers between devices, sum_over_groups(): codes = [lax.ppermute(code, 'centers', y_shift(d)) for d in (2, 1, 3)]  14.7 us
    all_to_all x1, starting transfers between devices, exchange(): lax.all_to_all(value, axis, split_axis=0, concat_axis=0, tiled=True, axis...  11.9 us
    all_to_all x1, waiting for transfers between devices, exchange(): lax.all_to_all(value, axis, split_axis=0, concat_axis=0, tiled=True, axis...  9.68 us
    ppermute x2, starting transfers between devices, sum_over_groups(): partner = lax.ppermute(send, 'centers', CORE_SWAP)  8.16 us
  transfers between devices with their start and end apart: 30, of which 29 were waited for; matrix products, arithmetic and copies ran while one was open for 1% of the time, Pallas kernels for 1%

profile of v5, /device:TPU:1, one launch (start us, length us, event | category | flops | bytes accessed | tf_op | source)
XLA Modules:
  0.0 315.9 jit_solution(13393278670405917476)
XLA Ops:
  0.6 3.1 select.3
  3.8 11.9 %all-to-all-start.1 = ((bf16[32,16,256]{2,1,0:T(8,128)(2,1)}), bf16[32,16,256]{2,1,0:T(8,128)(2,1)S(1)}, u32[]{:S(2)}, u32[]{:S(2)}) async-start(bf16[32,16,256]{2,1,0:T(8,128)(2,1)} %get-tuple-element.63), calls=%async_computation.1 | async-start | bytes 524288 | tf_op jit(solution)/shard_map/all_to_all | solution.py:313
  15.6 9.7 %all-to-all-done.1.in_ref = bf16[32,16,256]{2,1,0:T(8,128)(2,1)S(1)} async-done(((bf16[32,16,256]{2,1,0:T(8,128)(2,1)}), bf16[32,16,256]{2,1,0:T(8,128)(2,1)S(1)}, u32[]{:S(2)}, u32[]{:S(2)}) %all-to-all-start.1) | async-done | bytes 262176 | tf_op jit(solution)/shard_map/all_to_all | solution.py:313
  27.1 17.6 %all_to_all.55.c_ref = bf16[8,224,128]{2,1,0:T(8,128)(2,1)S(1)} all-to-all(bf16[8,224,128]{2,1,0:T(8,128)(2,1)S(1)} %get-tuple-element.66), channel_id=1, replica_groups={{0,8,16,24,32,40,48,56},{64,72,80,88,96,104,112,120},{128,136,144,152,1..., dimensions={0} | all-to-all | bytes 917504 | tf_op jit(solution)/shard_map/all_to_all | solution.py:313
  56.5 12.6 %collective-permute-done.c_ref = bf16[8,224,128]{2,1,0:T(8,128)(2,1)S(1)} collective-permute-done((bf16[8,224,128]{2,1,0:T(8,128)(2,1)S(1)}, bf16[8,224,128]{2,1,0:T(8,128)(2,1)S(1)}, u32[]{:S(2)}, u32[]{:S(2)}) %collective-permute-start) | collective-permute-done | bytes 458784 | tf_op jit(solution)/shard_map/ppermute | solution.py:320
  69.2 3.9 %build.1 = (bf16[1024,2048]{1,0:T(8,128)(2,1)S(1)}, f32[160,2048]{1,0:T(8,128)S(1)}, f32[160,1024]{1,0:T(8,128)S(1)}, f32[152,512]{1,0:T(8,128)S(1)}, f32[152,512]{1,0:T(8,128)S(1)}) custom-call(bf16[1024,448]{1,0:T(8,128)(2,1)S(1)} %pad_bitcast_fusion.feat_ref, f32[1024,1]{1,0:T(8,128)S(1)} %copy.11.norm_ref, ...), custom_call_target="tpu_custom_call" | custom-call | flops 1073741824 | bytes 4194304 | tf_op jit(solution)/shard_map/build/pallas_call | solution.py:48
  75.2 2.8 collective-permute-start.6
  81.2 4.1 %collective-permute-done.5.c1 = s16[160,512]{1,0:T(8,128)(2,1)S(1)} collective-permute-done((s16[160,512]{1,0:T(8,128)(2,1)S(1)}, s16[160,512]{1,0:T(8,128)(2,1)S(1)}, u32[]{:S(2)}, u32[]{:S(2)}) %collective-permute-start.5) | collective-permute-done | bytes 163872 | tf_op jit(solution)/shard_map/ppermute | solution.py:372
  87.0 2.6 collective-permute-start.7
  92.7 22.0 %all_to_all.56.in_ref = bf16[32,80,128]{2,1,0:T(8,128)(2,1)S(1)} all-to-all(bf16[32,80,128]{2,1,0:T(8,128)(2,1)S(1)} %get-tuple-element.74), channel_id=1, replica_groups=mesh['rows'=32,'centers'=8] {'rows'}, dimensions={0} | all-to-all | bytes 1310720 | tf_op jit(solution)/shard_map/all_to_all | solution.py:313
  114.8 14.3 %all_to_all.57.g0 = bf16[8,80,128]{2,1,0:T(8,128)(2,1)S(1)} all-to-all(bf16[8,80,128]{2,1,0:T(8,128)(2,1)S(1)} %sum_at_owner.4), channel_id=1, replica_groups={{0,8,16,24,32,40,48,56},{64,72,80,88,96,104,112,120},{128,136,144,152,1..., dimensions={0} | all-to-all | bytes 327680 | tf_op jit(solution)/shard_map/all_to_all | solution.py:313
  133.3 2.8 collective-permute-done.9.g2
  136.2 2.1 collective-permute-done.8.g1
  138.3 4.2 %second.2 = (bf16[32,80,128]{2,1,0:T(8,128)(2,1)S(1)}, f32[160,2048]{1,0:T(8,128)S(1)}) custom-call(f32[160,2048]{1,0:T(8,128)S(1)} %get-tuple-element.67.coef_ref, bf16[8,80,128]{2,1,0:T(8,128)(2,1)S(1)} %all_to_all.57.g0, bf16[8,80,128]{2,1,0:T(8,128)(2,1)S(1)} %collective-permute-done.8.g1, bf16[8,80,128]{2,1,0:T(8,128)(2,1)S(1)} %collective-permute-done.9.g2, ...), custom_call_target="tpu_custom_call" | custom-call | flops 1073741824 | bytes 4194304 | tf_op jit(solution)/shard_map/second/pallas_call | solution.py:48
  142.5 16.8 %all_to_all.58.in_ref = bf16[32,80,128]{2,1,0:T(8,128)(2,1)S(1)} all-to-all(bf16[32,80,128]{2,1,0:T(8,128)(2,1)S(1)} %get-tuple-element.77), channel_id=1, replica_groups=mesh['rows'=32,'centers'=8] {'rows'}, dimensions={0} | all-to-all | bytes 1310720 | tf_op jit(solution)/shard_map/all_to_all | solution.py:313
  159.4 13.5 %all_to_all.59.g0 = bf16[8,80,128]{2,1,0:T(8,128)(2,1)S(1)} all-to-all(bf16[8,80,128]{2,1,0:T(8,128)(2,1)S(1)} %sum_at_owner.5), channel_id=1, replica_groups={{0,8,16,24,32,40,48,56},{64,72,80,88,96,104,112,120},{128,136,144,152,1..., dimensions={0} | all-to-all | bytes 327680 | tf_op jit(solution)/shard_map/all_to_all | solution.py:313
  176.1 2.7 collective-permute-done.13.g3
  182.3 2.5 scores.1
  184.8 7.3 %collective-permute-start.14 = (f32[152,512]{1,0:T(8,128)S(1)}, f32[152,512]{1,0:T(8,128)S(1)}, u32[]{:S(2)}, u32[]{:S(2)}) collective-permute-start(f32[152,512]{1,0:T(8,128)S(1)} %get-tuple-element.80), channel_id=1, source_target_pairs={{0,1},{1,0},{2,3},{3,2},{4,5},{5,4},{6,7},{7,6},{8,9},{9,8},{10,11... | collective-permute-start | bytes 933896 | tf_op jit(solution)/shard_map/ppermute | solution.py:367
  195.3 3.6 %collective-permute-done.17.c2 = s16[160,512]{1,0:T(8,128)(2,1)S(1)} collective-permute-done((s16[160,512]{1,0:T(8,128)(2,1)S(1)}, s16[160,512]{1,0:T(8,128)(2,1)S(1)}, u32[]{:S(2)}, u32[]{:S(2)}) %collective-permute-start.17) | collective-permute-done | bytes 163872 | tf_op jit(solution)/shard_map/ppermute | solution.py:372
  202.9 2.3 collective-permute-start.18
  208.3 19.7 %all_to_all.60.in_ref = bf16[32,80,128]{2,1,0:T(8,128)(2,1)S(1)} all-to-all(bf16[32,80,128]{2,1,0:T(8,128)(2,1)S(1)} %get-tuple-element.84), channel_id=1, replica_groups=mesh['rows'=32,'centers'=8] {'rows'}, dimensions={0} | all-to-all | bytes 1310720 | tf_op jit(solution)/shard_map/all_to_all | solution.py:313
  228.1 14.3 %all_to_all.61.g0 = bf16[8,80,128]{2,1,0:T(8,128)(2,1)S(1)} all-to-all(bf16[8,80,128]{2,1,0:T(8,128)(2,1)S(1)} %sum_at_owner.6), channel_id=1, replica_groups={{0,8,16,24,32,40,48,56},{64,72,80,88,96,104,112,120},{128,136,144,152,1..., dimensions={0} | all-to-all | bytes 327680 | tf_op jit(solution)/shard_map/all_to_all | solution.py:313
  246.6 2.9 collective-permute-done.20.g2
  251.5 4.2 %second.3 = (bf16[32,80,128]{2,1,0:T(8,128)(2,1)S(1)}, f32[160,2048]{1,0:T(8,128)S(1)}) custom-call(f32[160,2048]{1,0:T(8,128)S(1)} %get-tuple-element.78.coef_ref, bf16[8,80,128]{2,1,0:T(8,128)(2,1)S(1)} %all_to_all.61.g0, bf16[8,80,128]{2,1,0:T(8,128)(2,1)S(1)} %collective-permute-done.19.g1, bf16[8,80,128]{2,1,0:T(8,128)(2,1)S(1)} %collective-permute-done.20.g2, ...), custom_call_target="tpu_custom_call" | custom-call | flops 1073741824 | bytes 4194304 | tf_op jit(solution)/shard_map/second/pallas_call | solution.py:48
  255.7 17.2 %all_to_all.62.in_ref = bf16[32,80,128]{2,1,0:T(8,128)(2,1)S(1)} all-to-all(bf16[32,80,128]{2,1,0:T(8,128)(2,1)S(1)} %get-tuple-element.87), channel_id=1, replica_groups=mesh['rows'=32,'centers'=8] {'rows'}, dimensions={0} | all-to-all | bytes 1310720 | tf_op jit(solution)/shard_map/all_to_all | solution.py:313
  273.0 13.3 %all_to_all.63.g0 = bf16[8,80,128]{2,1,0:T(8,128)(2,1)S(1)} all-to-all(bf16[8,80,128]{2,1,0:T(8,128)(2,1)S(1)} %sum_at_owner.7), channel_id=1, replica_groups={{0,8,16,24,32,40,48,56},{64,72,80,88,96,104,112,120},{128,136,144,152,1..., dimensions={0} | all-to-all | bytes 327680 | tf_op jit(solution)/shard_map/all_to_all | solution.py:313
  289.5 2.7 collective-permute-done.24.g3
  295.6 3.7 %final.1 = (f32[147,2048]{1,0:T(8,128)}, f32[4,152,128]{2,1,0:T(8,128)S(1)}, f32[4,152,128]{2,1,0:T(8,128)S(1)}) custom-call(f32[160,2048]{1,0:T(8,128)S(1)} %get-tuple-element.86.coef_ref, bf16[8,80,128]{2,1,0:T(8,128)(2,1)S(1)} %all_to_all.63.g0, bf16[8,80,128]{2,1,0:T(8,128)(2,1)S(1)} %collective-permute-done.22.g1, ...), custom_call_target="tpu_custom_call" | custom-call | flops 1073741824 | bytes 4194304 | tf_op jit(solution)/shard_map/final/pallas_call | solution.py:48
  299.3 7.4 %collective-permute-start.25 = (f32[4,152,128]{2,1,0:T(8,128)S(1)}, f32[4,152,128]{2,1,0:T(8,128)S(1)}, u32[]{:S(2)}, u32[]{:S(2)}) collective-permute-start(f32[4,152,128]{2,1,0:T(8,128)S(1)} %get-tuple-element.90), channel_id=1, source_target_pairs={{0,1},{1,0},{2,3},{3,2},{4,5},{5,4},{6,7},{7,6},{8,9},{9,8},{10,11... | collective-permute-start | bytes 933896 | tf_op jit(solution)/shard_map/ppermute | solution.py:427
  309.7 2.7 collective-permute-start.28
  312.8 2.5 collective-permute-done.27
  (72 shorter events, 62.1 us)
Async XLA Ops:
  0.6 24.7 %copy-start.3 = (s32[1,2048]{1,0:T(1,128)S(1)}, s32[1,2048]{1,0:T(1,128)}, u32[]{:S(2)}) copy-start(s32[1,2048]{1,0:T(1,128)} %param.8) | copy-start | bytes 24580
  3.8 21.6 %all-to-all-start.1 = ((bf16[32,16,256]{2,1,0:T(8,128)(2,1)}), bf16[32,16,256]{2,1,0:T(8,128)(2,1)S(1)}, u32[]{:S(2)}, u32[]{:S(2)}) async-start(bf16[32,16,256]{2,1,0:T(8,128)(2,1)} %get-tuple-element.63), calls=%async_computation.1 | async-start | bytes 524288 | tf_op jit(solution)/shard_map/all_to_all | solution.py:313
  44.7 8.1 %collective-permute-start.2 = (bf16[8,224,128]{2,1,0:T(8,128)(2,1)S(1)}, bf16[8,224,128]{2,1,0:T(8,128)(2,1)S(1)}, u32[]{:S(2)}, u32[]{:S(2)}) collective-permute-start(bf16[8,224,128]{2,1,0:T(8,128)(2,1)S(1)} %all_to_all.55.c_ref), channel_id=1, source_target_pairs={{0,192},{8,200},{16,208},{24,216},{32,224},{40,232},{48,240},{56,2... | collective-permute-start | bytes 1376264 | tf_op jit(solution)/shard_map/ppermute | solution.py:320
  45.7 9.4 %collective-permute-start.1 = (bf16[8,224,128]{2,1,0:T(8,128)(2,1)S(1)}, bf16[8,224,128]{2,1,0:T(8,128)(2,1)S(1)}, u32[]{:S(2)}, u32[]{:S(2)}) collective-permute-start(bf16[8,224,128]{2,1,0:T(8,128)(2,1)S(1)} %all_to_all.55.c_ref), channel_id=1, source_target_pairs={{0,128},{8,136},{16,144},{24,152},{32,160},{40,168},{48,176},{56,1... | collective-permute-start | bytes 1376264 | tf_op jit(solution)/shard_map/ppermute | solution.py:320
  47.3 21.9 %collective-permute-start = (bf16[8,224,128]{2,1,0:T(8,128)(2,1)S(1)}, bf16[8,224,128]{2,1,0:T(8,128)(2,1)S(1)}, u32[]{:S(2)}, u32[]{:S(2)}) collective-permute-start(bf16[8,224,128]{2,1,0:T(8,128)(2,1)S(1)} %all_to_all.55.c_ref), channel_id=1, source_target_pairs={{0,64},{8,72},{16,80},{24,88},{32,96},{40,104},{48,112},{56,120},{... | collective-permute-start | bytes 1376264 | tf_op jit(solution)/shard_map/ppermute | solution.py:320
  54.3 14.9 %copy-start = (f32[147,2048]{1,0:T(8,128)S(1)}, f32[147,2048]{1,0:T(8,128)}, u32[]{:S(2)}) copy-start(f32[147,2048]{1,0:T(8,128)} %warm_ref.1) | copy-start | bytes 3612676
  73.1 2.1 collective-permute-start.3
  75.2 6.0 %collective-permute-start.6 = (s16[160,512]{1,0:T(8,128)(2,1)S(1)}, s16[160,512]{1,0:T(8,128)(2,1)S(1)}, u32[]{:S(2)}, u32[]{:S(2)}) collective-permute-start(s16[160,512]{1,0:T(8,128)(2,1)S(1)} %get-tuple-element.71), channel_id=1, source_target_pairs={{0,6},{1,7},{2,0},{3,1},{4,2},{5,3},{6,4},{7,5},{8,14},{9,15},{10,... | collective-permute-start | bytes 491528 | tf_op jit(solution)/shard_map/ppermute | solution.py:372
  78.0 7.3 %collective-permute-start.5 = (s16[160,512]{1,0:T(8,128)(2,1)S(1)}, s16[160,512]{1,0:T(8,128)(2,1)S(1)}, u32[]{:S(2)}, u32[]{:S(2)}) collective-permute-start(s16[160,512]{1,0:T(8,128)(2,1)S(1)} %get-tuple-element.71), channel_id=1, source_target_pairs={{0,2},{1,3},{2,4},{3,5},{4,6},{5,7},{6,0},{7,1},{8,10},{9,11},{10,... | collective-permute-start | bytes 491528 | tf_op jit(solution)/shard_map/ppermute | solution.py:372
  78.0 8.8 %collective-permute-start.4 = (s16[160,512]{1,0:T(8,128)(2,1)S(1)}, s16[160,512]{1,0:T(8,128)(2,1)S(1)}, u32[]{:S(2)}, u32[]{:S(2)}) collective-permute-start(s16[160,512]{1,0:T(8,128)(2,1)S(1)} %get-tuple-element.71), channel_id=1, source_target_pairs={{0,4},{1,5},{2,6},{3,7},{4,0},{5,1},{6,2},{7,3},{8,12},{9,13},{10,... | collective-permute-start | bytes 491528 | tf_op jit(solution)/shard_map/ppermute | solution.py:372
  87.0 3.8 %collective-permute-start.7 = (f32[152,512]{1,0:T(8,128)S(1)}, f32[152,512]{1,0:T(8,128)S(1)}, u32[]{:S(2)}, u32[]{:S(2)}) collective-permute-start(f32[152,512]{1,0:T(8,128)S(1)} %decode.2.mine_ref), channel_id=1, source_target_pairs={{0,1},{1,0},{2,3},{3,2},{4,5},{5,4},{6,7},{7,6},{8,9},{9,8},{10,11... | collective-permute-start | bytes 933896 | tf_op jit(solution)/shard_map/ppermute | solution.py:374
  129.1 4.2 %collective-permute-start.10 = (bf16[8,80,128]{2,1,0:T(8,128)(2,1)S(1)}, bf16[8,80,128]{2,1,0:T(8,128)(2,1)S(1)}, u32[]{:S(2)}, u32[]{:S(2)}) collective-permute-start(bf16[8,80,128]{2,1,0:T(8,128)(2,1)S(1)} %all_to_all.57.g0), channel_id=1, source_target_pairs={{0,192},{8,200},{16,208},{24,216},{32,224},{40,232},{48,240},{56,2... | collective-permute-start | bytes 491528 | tf_op jit(solution)/shard_map/ppermute | solution.py:320
  130.4 5.8 %collective-permute-start.9 = (bf16[8,80,128]{2,1,0:T(8,128)(2,1)S(1)}, bf16[8,80,128]{2,1,0:T(8,128)(2,1)S(1)}, u32[]{:S(2)}, u32[]{:S(2)}) collective-permute-start(bf16[8,80,128]{2,1,0:T(8,128)(2,1)S(1)} %all_to_all.57.g0), channel_id=1, source_target_pairs={{0,128},{8,136},{16,144},{24,152},{32,160},{40,168},{48,176},{56,1... | collective-permute-start | bytes 491528 | tf_op jit(solution)/shard_map/ppermute | solution.py:320
  131.5 6.8 %collective-permute-start.8 = (bf16[8,80,128]{2,1,0:T(8,128)(2,1)S(1)}, bf16[8,80,128]{2,1,0:T(8,128)(2,1)S(1)}, u32[]{:S(2)}, u32[]{:S(2)}) collective-permute-start(bf16[8,80,128]{2,1,0:T(8,128)(2,1)S(1)} %all_to_all.57.g0), channel_id=1, source_target_pairs={{0,64},{8,72},{16,80},{24,88},{32,96},{40,104},{48,112},{56,120},{... | collective-permute-start | bytes 491528 | tf_op jit(solution)/shard_map/ppermute | solution.py:320
  172.9 6.0 %collective-permute-start.13 = (bf16[8,80,128]{2,1,0:T(8,128)(2,1)S(1)}, bf16[8,80,128]{2,1,0:T(8,128)(2,1)S(1)}, u32[]{:S(2)}, u32[]{:S(2)}) collective-permute-start(bf16[8,80,128]{2,1,0:T(8,128)(2,1)S(1)} %all_to_all.59.g0), channel_id=1, source_target_pairs={{0,192},{8,200},{16,208},{24,216},{32,224},{40,232},{48,240},{56,2... | collective-permute-start | bytes 491528 | tf_op jit(solution)/shard_map/ppermute | solution.py:320
  174.8 5.8 %collective-permute-start.12 = (bf16[8,80,128]{2,1,0:T(8,128)(2,1)S(1)}, bf16[8,80,128]{2,1,0:T(8,128)(2,1)S(1)}, u32[]{:S(2)}, u32[]{:S(2)}) collective-permute-start(bf16[8,80,128]{2,1,0:T(8,128)(2,1)S(1)} %all_to_all.59.g0), channel_id=1, source_target_pairs={{0,128},{8,136},{16,144},{24,152},{32,160},{40,168},{48,176},{56,1... | collective-permute-start | bytes 491528 | tf_op jit(solution)/shard_map/ppermute | solution.py:320
  175.8 6.5 %collective-permute-start.11 = (bf16[8,80,128]{2,1,0:T(8,128)(2,1)S(1)}, bf16[8,80,128]{2,1,0:T(8,128)(2,1)S(1)}, u32[]{:S(2)}, u32[]{:S(2)}) collective-permute-start(bf16[8,80,128]{2,1,0:T(8,128)(2,1)S(1)} %all_to_all.59.g0), channel_id=1, source_target_pairs={{0,64},{8,72},{16,80},{24,88},{32,96},{40,104},{48,112},{56,120},{... | collective-permute-start | bytes 491528 | tf_op jit(solution)/shard_map/ppermute | solution.py:320
  184.8 8.6 %collective-permute-start.14 = (f32[152,512]{1,0:T(8,128)S(1)}, f32[152,512]{1,0:T(8,128)S(1)}, u32[]{:S(2)}, u32[]{:S(2)}) collective-permute-start(f32[152,512]{1,0:T(8,128)S(1)} %get-tuple-element.80), channel_id=1, source_target_pairs={{0,1},{1,0},{2,3},{3,2},{4,5},{5,4},{6,7},{7,6},{8,9},{9,8},{10,11... | collective-permute-start | bytes 933896 | tf_op jit(solution)/shard_map/ppermute | solution.py:367
  193.5 5.5 %collective-permute-start.17 = (s16[160,512]{1,0:T(8,128)(2,1)S(1)}, s16[160,512]{1,0:T(8,128)(2,1)S(1)}, u32[]{:S(2)}, u32[]{:S(2)}) collective-permute-start(s16[160,512]{1,0:T(8,128)(2,1)S(1)} %get-tuple-element.82), channel_id=1, source_target_pairs={{0,6},{1,7},{2,0},{3,1},{4,2},{5,3},{6,4},{7,5},{8,14},{9,15},{10,... | collective-permute-start | bytes 491528 | tf_op jit(solution)/shard_map/ppermute | solution.py:372
  193.5 7.3 %collective-permute-start.16 = (s16[160,512]{1,0:T(8,128)(2,1)S(1)}, s16[160,512]{1,0:T(8,128)(2,1)S(1)}, u32[]{:S(2)}, u32[]{:S(2)}) collective-permute-start(s16[160,512]{1,0:T(8,128)(2,1)S(1)} %get-tuple-element.82), channel_id=1, source_target_pairs={{0,2},{1,3},{2,4},{3,5},{4,6},{5,7},{6,0},{7,1},{8,10},{9,11},{10,... | collective-permute-start | bytes 491528 | tf_op jit(solution)/shard_map/ppermute | solution.py:372
  195.0 7.8 %collective-permute-start.15 = (s16[160,512]{1,0:T(8,128)(2,1)S(1)}, s16[160,512]{1,0:T(8,128)(2,1)S(1)}, u32[]{:S(2)}, u32[]{:S(2)}) collective-permute-start(s16[160,512]{1,0:T(8,128)(2,1)S(1)} %get-tuple-element.82), channel_id=1, source_target_pairs={{0,4},{1,5},{2,6},{3,7},{4,0},{5,1},{6,2},{7,3},{8,12},{9,13},{10,... | collective-permute-start | bytes 491528 | tf_op jit(solution)/shard_map/ppermute | solution.py:372
  202.9 3.5 %collective-permute-start.18 = (f32[152,512]{1,0:T(8,128)S(1)}, f32[152,512]{1,0:T(8,128)S(1)}, u32[]{:S(2)}, u32[]{:S(2)}) collective-permute-start(f32[152,512]{1,0:T(8,128)S(1)} %decode.3.mine_ref), channel_id=1, source_target_pairs={{0,1},{1,0},{2,3},{3,2},{4,5},{5,4},{6,7},{7,6},{8,9},{9,8},{10,11... | collective-permute-start | bytes 933896 | tf_op jit(solution)/shard_map/ppermute | solution.py:374
  242.4 4.2 %collective-permute-start.21 = (bf16[8,80,128]{2,1,0:T(8,128)(2,1)S(1)}, bf16[8,80,128]{2,1,0:T(8,128)(2,1)S(1)}, u32[]{:S(2)}, u32[]{:S(2)}) collective-permute-start(bf16[8,80,128]{2,1,0:T(8,128)(2,1)S(1)} %all_to_all.61.g0), channel_id=1, source_target_pairs={{0,192},{8,200},{16,208},{24,216},{32,224},{40,232},{48,240},{56,2... | collective-permute-start | bytes 491528 | tf_op jit(solution)/shard_map/ppermute | solution.py:320
  243.7 5.8 %collective-permute-start.20 = (bf16[8,80,128]{2,1,0:T(8,128)(2,1)S(1)}, bf16[8,80,128]{2,1,0:T(8,128)(2,1)S(1)}, u32[]{:S(2)}, u32[]{:S(2)}) collective-permute-start(bf16[8,80,128]{2,1,0:T(8,128)(2,1)S(1)} %all_to_all.61.g0), channel_id=1, source_target_pairs={{0,128},{8,136},{16,144},{24,152},{32,160},{40,168},{48,176},{56,1... | collective-permute-start | bytes 491528 | tf_op jit(solution)/shard_map/ppermute | solution.py:320
  245.0 6.5 %collective-permute-start.19 = (bf16[8,80,128]{2,1,0:T(8,128)(2,1)S(1)}, bf16[8,80,128]{2,1,0:T(8,128)(2,1)S(1)}, u32[]{:S(2)}, u32[]{:S(2)}) collective-permute-start(bf16[8,80,128]{2,1,0:T(8,128)(2,1)S(1)} %all_to_all.61.g0), channel_id=1, source_target_pairs={{0,64},{8,72},{16,80},{24,88},{32,96},{40,104},{48,112},{56,120},{... | collective-permute-start | bytes 491528 | tf_op jit(solution)/shard_map/ppermute | solution.py:320
  286.3 5.9 %collective-permute-start.24 = (bf16[8,80,128]{2,1,0:T(8,128)(2,1)S(1)}, bf16[8,80,128]{2,1,0:T(8,128)(2,1)S(1)}, u32[]{:S(2)}, u32[]{:S(2)}) collective-permute-start(bf16[8,80,128]{2,1,0:T(8,128)(2,1)S(1)} %all_to_all.63.g0), channel_id=1, source_target_pairs={{0,192},{8,200},{16,208},{24,216},{32,224},{40,232},{48,240},{56,2... | collective-permute-start | bytes 491528 | tf_op jit(solution)/shard_map/ppermute | solution.py:320
  288.2 5.8 %collective-permute-start.23 = (bf16[8,80,128]{2,1,0:T(8,128)(2,1)S(1)}, bf16[8,80,128]{2,1,0:T(8,128)(2,1)S(1)}, u32[]{:S(2)}, u32[]{:S(2)}) collective-permute-start(bf16[8,80,128]{2,1,0:T(8,128)(2,1)S(1)} %all_to_all.63.g0), channel_id=1, source_target_pairs={{0,128},{8,136},{16,144},{24,152},{32,160},{40,168},{48,176},{56,1... | collective-permute-start | bytes 491528 | tf_op jit(solution)/shard_map/ppermute | solution.py:320
  289.2 6.4 %collective-permute-start.22 = (bf16[8,80,128]{2,1,0:T(8,128)(2,1)S(1)}, bf16[8,80,128]{2,1,0:T(8,128)(2,1)S(1)}, u32[]{:S(2)}, u32[]{:S(2)}) collective-permute-start(bf16[8,80,128]{2,1,0:T(8,128)(2,1)S(1)} %all_to_all.63.g0), channel_id=1, source_target_pairs={{0,64},{8,72},{16,80},{24,88},{32,96},{40,104},{48,112},{56,120},{... | collective-permute-start | bytes 491528 | tf_op jit(solution)/shard_map/ppermute | solution.py:320
  299.3 8.6 %collective-permute-start.25 = (f32[4,152,128]{2,1,0:T(8,128)S(1)}, f32[4,152,128]{2,1,0:T(8,128)S(1)}, u32[]{:S(2)}, u32[]{:S(2)}) collective-permute-start(f32[4,152,128]{2,1,0:T(8,128)S(1)} %get-tuple-element.90), channel_id=1, source_target_pairs={{0,1},{1,0},{2,3},{3,2},{4,5},{5,4},{6,7},{7,6},{8,9},{9,8},{10,11... | collective-permute-start | bytes 933896 | tf_op jit(solution)/shard_map/ppermute | solution.py:427
  307.9 4.8 %collective-permute-start.26 = (f32[152,128]{1,0:T(8,128)S(1)}, f32[152,128]{1,0:T(8,128)S(1)}, u32[]{:S(2)}, u32[]{:S(2)}) collective-permute-start(f32[152,128]{1,0:T(8,128)S(1)} %get-tuple-element.92), channel_id=1, source_target_pairs={{0,4},{1,5},{2,6},{3,7},{4,0},{5,1},{6,2},{7,3},{8,12},{9,13},{10,... | collective-permute-start | bytes 233480 | tf_op jit(solution)/shard_map/ppermute | solution.py:429
  309.7 5.6 %collective-permute-start.27 = (f32[152,128]{1,0:T(8,128)S(1)}, f32[152,128]{1,0:T(8,128)S(1)}, u32[]{:S(2)}, u32[]{:S(2)}) collective-permute-start(f32[152,128]{1,0:T(8,128)S(1)} %get-tuple-element.93), channel_id=1, source_target_pairs={{0,2},{1,3},{2,4},{3,5},{4,6},{5,7},{6,0},{7,1},{8,10},{9,11},{10,... | collective-permute-start | bytes 233480 | tf_op jit(solution)/shard_map/ppermute | solution.py:429
  309.7 5.6 %collective-permute-start.28 = (f32[152,128]{1,0:T(8,128)S(1)}, f32[152,128]{1,0:T(8,128)S(1)}, u32[]{:S(2)}, u32[]{:S(2)}) collective-permute-start(f32[152,128]{1,0:T(8,128)S(1)} %get-tuple-element.94), channel_id=1, source_target_pairs={{0,6},{1,7},{2,0},{3,1},{4,2},{5,3},{6,4},{7,5},{8,14},{9,15},{10,... | collective-permute-start | bytes 233480 | tf_op jit(solution)/shard_map/ppermute | solution.py:429
  (2 other events, 5.1 us)

commit v6 on v5

--- a/solution.py
+++ b/solution.py
@@ -22,6 +22,7 @@
 PART = CHUNK // 4
 BLOCK = 256
 SLOTS = 16
+EARLY = (0, 3, 2)
 GRANT = 20 * 2**20
 FLOPS = 2**30
 
@@ -163,11 +164,19 @@
     send_ref[...] = own_ref[:WIRE, pl.ds(pl.multiple_of((1 - core) * width, width), width)]
 
 
-def own_scores(low_ref, kern_ref, own_ref):
+def add_scores(low_ref, kern_ref, left, before_ref, total_ref):
     @pl.loop(0, kern_ref.shape[0] // BLOCK)
     def _(n):
         at = pl.ds(pl.multiple_of(n * BLOCK, BLOCK), BLOCK)
-        own_ref[:, at] = dot_nt(low_ref[...], kern_ref[at, :])
+        scores = dot_nt(low_ref[...], kern_ref[at, left : left + CHUNK])
+        total_ref[:, at] = scores if before_ref is None else before_ref[:, at] + scores
+
+
+def warm_chunk(warm_ref, d, coef_ref, low_ref):
+    warm = warm_ref[:, pl.ds(pl.multiple_of(chunk_of(d) * CHUNK, CHUNK), CHUNK)]
+    warm = jnp.concatenate([warm, jnp.zeros((PAD - CLASSES, CHUNK), F32)], axis=0)
+    coef_ref[...] = warm
+    low_ref[...] = warm.astype(BF16)
 
 
 def kernel_columns(feat_ref, norm_ref, c_ref, cent_ref, kern_ref, left):
@@ -185,24 +194,23 @@
         kern_ref[at, left : left + CHUNK] = jnp.exp2(power).astype(BF16)
 
 
-def chunk_kernel(feat_ref, norm_ref, c_ref, kern_ref, cent_ref):
+def chunk_kernel(feat_ref, norm_ref, c_ref, warm_ref, *refs, d):
+    before = refs[0] if len(refs) == 6 else None
+    kern_ref, coef_ref, total_ref, cent_ref, low_ref = refs[-5:]
     kernel_columns(feat_ref, norm_ref, c_ref, cent_ref, kern_ref, 0)
+    warm_chunk(warm_ref, d, coef_ref, low_ref)
+    add_scores(low_ref, kern_ref, 0, before, total_ref)
 
 
 def build_kernel(
-    feat_ref, norm_ref, c_ref, k0, k2, k3, warm_ref,
+    feat_ref, norm_ref, c_ref, warm_ref, before_ref, k0, k2, k3,
     kern_ref, coef_ref, own_ref, keep_ref, send_ref, cent_ref, low_ref,
 ):
     for d, k_ref in ((0, k0), (2, k2), (3, k3)):
         kern_ref[:, d * CHUNK : (d + 1) * CHUNK] = k_ref[...]
-    for d in range(X):
-        cols = slice(d * CHUNK, (d + 1) * CHUNK)
-        warm = warm_ref[:, pl.ds(pl.multiple_of(chunk_of(d) * CHUNK, CHUNK), CHUNK)]
-        warm = jnp.concatenate([warm, jnp.zeros((PAD - CLASSES, CHUNK), F32)], axis=0)
-        coef_ref[:, cols] = warm
-        low_ref[:, cols] = warm.astype(BF16)
     kernel_columns(feat_ref, norm_ref, c_ref, cent_ref, kern_ref, CHUNK)
-    own_scores(low_ref, kern_ref, own_ref)
+    warm_chunk(warm_ref, 1, coef_ref, low_ref)
+    add_scores(low_ref, kern_ref, CHUNK, before_ref, own_ref)
     split_halves(own_ref, keep_ref, send_ref)
 
 
@@ -263,45 +271,57 @@
     gradient_pieces(res_ref, kern_ref, out_ref)
 
 
-def update(coef_ref, grads, new_ref, low_ref):
+def update(coef_ref, g_ref, new_ref, low_ref):
     half = PAD // 2
 
     @pl.loop(0, Z)
     def _(z):
         height = pl.ds(pl.multiple_of(lax.div(z, 4) * half, half), half)
-        for d, g_ref in enumerate(grads):
-            left = pl.multiple_of(d * CHUNK + lax.rem(z, 4) * PART, PART)
-            cols = pl.ds(left, PART)
-            fresh = coef_ref[height, cols] - STEP * g_ref[z].astype(F32)
-            new_ref[height, cols] = fresh
-            low_ref[height, cols] = fresh.astype(BF16)
-
-
-def second_kernel(coef_ref, g0, g1, g2, g3, base_ref, kern_ref, label_ref, out_ref, new_ref, res_ref, low_ref):
-    update(coef_ref, (g0, g1, g2, g3), new_ref, low_ref)
+        cols = pl.ds(pl.multiple_of(lax.rem(z, 4) * PART, PART), PART)
+        fresh = coef_ref[height, cols] - STEP * g_ref[z].astype(F32)
+        new_ref[height, cols] = fresh
+        low_ref[height, cols] = fresh.astype(BF16)
+
+
+def step_kernel(coef_ref, g_ref, kern_ref, *refs, d):
+    before = refs[0] if len(refs) == 4 else None
+    new_ref, total_ref, low_ref = refs[-3:]
+    update(coef_ref, g_ref, new_ref, low_ref)
+    add_scores(low_ref, kern_ref, d * CHUNK, before, total_ref)
+
+
+def second_kernel(
+    coef_ref, g_ref, before_ref, base_ref, kern_ref, label_ref, out_ref, new_ref, res_ref, low_ref
+):
+    update(coef_ref, g_ref, new_ref, low_ref)
 
     @pl.loop(0, kern_ref.shape[0] // BLOCK)
     def _(n):
         at = pl.ds(pl.multiple_of(n * BLOCK, BLOCK), BLOCK)
-        logits = base_ref[:, at] + dot_nt(low_ref[...], kern_ref[at, :])
+        last = dot_nt(low_ref[...], kern_ref[at, CHUNK : 2 * CHUNK])
+        logits = base_ref[:, at] + (before_ref[:, at] + last)
         res_ref[:, at] = residual_of(logits, label_ref[:, at])
 
     gradient_pieces(res_ref, kern_ref, out_ref)
 
 
-def score_kernel(coef_ref, g0, g1, g2, g3, kern_ref, new_ref, own_ref, keep_ref, send_ref, low_ref):
-    update(coef_ref, (g0, g1, g2, g3), new_ref, low_ref)
-    own_scores(low_ref, kern_ref, own_ref)
+def score_kernel(
+    coef_ref, g_ref, before_ref, kern_ref, new_ref, own_ref, keep_ref, send_ref, low_ref
+):
+    update(coef_ref, g_ref, new_ref, low_ref)
+    add_scores(low_ref, kern_ref, CHUNK, before_ref, own_ref)
     split_halves(own_ref, keep_ref, send_ref)
 
 
-def final_kernel(coef_ref, g0, g1, g2, g3, kern_ref, coef_out_ref, keep_ref, send_ref, new_ref, low_ref, own_ref):
-    update(coef_ref, (g0, g1, g2, g3), new_ref, low_ref)
-    for d in range(X):
-        cols = slice(d * CHUNK, (d + 1) * CHUNK)
+def final_kernel(
+    c0, c2, c3, coef_ref, g_ref, before_ref, kern_ref,
+    coef_out_ref, keep_ref, send_ref, new_ref, low_ref, own_ref,
+):
+    update(coef_ref, g_ref, new_ref, low_ref)
+    for d, ref in enumerate((c0, new_ref, c2, c3)):
         to = pl.ds(pl.multiple_of(chunk_of(d) * CHUNK, CHUNK), CHUNK)
-        coef_out_ref[:, to] = new_ref[:CLASSES, cols]
-    own_scores(low_ref, kern_ref, own_ref)
+        coef_out_ref[:, to] = ref[:CLASSES, :]
+    add_scores(low_ref, kern_ref, CHUNK, before_ref, own_ref)
     core = my_core()
     for d in range(Y):
         y = lax.rem(lax.div(lax.axis_index("centers"), CORES) + d, Y)
@@ -379,51 +399,67 @@
     centers = center_index.shape[1]
     labels = labels.reshape(1, rows)
     kern_type = like((rows, centers), BF16)
-    coef_type = like((PAD, centers), F32)
+    coef_type = like((PAD, CHUNK), F32)
     own_type = like((PAD, rows), F32)
     half_type = like((WIRE, rows // CORES), F32)
     last_type = like((Y, WIRE, LANES), F32)
     grad_type = like((X * Z, PAD // 2, PART), BF16)
-    low = pltpu.VMEM((PAD, centers), BF16)
+    low = pltpu.VMEM((PAD, CHUNK), BF16)
     res = pltpu.VMEM((PAD, rows), BF16)
     score = pltpu.VMEM((PAD, rows), F32)
-    coef_scratch = pltpu.VMEM((PAD, centers), F32)
+    cent = pltpu.VMEM((FPAD, CHUNK), BF16)
 
     row_norms = jnp.sum(jnp.square(features.astype(F32)), axis=0).reshape(rows, 1)
     feat_rows = jnp.pad(features, ((0, FPAD - FEAT), (0, 0))).T
     cents = gather_centers(features, center_index)
-    build_chunk = call(
-        chunk_kernel, like((rows, CHUNK), BF16), [pltpu.VMEM((FPAD, CHUNK), BF16)], name="chunk"
-    )
-    chunks = [build_chunk(feat_rows, row_norms, cents[d]) for d in (0, 2, 3)]
-    kern, coef, own, keep, send = call(
+    before, chunks, coefs = [], {}, {}
+    for d in EARLY:
+        chunks[d], coefs[d], total = call(
+            functools.partial(chunk_kernel, d=d),
+            [like((rows, CHUNK), BF16), coef_type, own_type],
+            [cent, low],
+            name="chunk",
+        )(feat_rows, row_norms, cents[d], warm_coef, *before)
+        before = [total]
+    kern, coefs[1], own, keep, send = call(
         build_kernel,
         [kern_type, coef_type, own_type, half_type, half_type],
-        [pltpu.VMEM((FPAD, CHUNK), BF16), low],
+        [cent, low],
         name="build",
-    )(feat_rows, row_norms, cents[1], *chunks, warm_coef)
+    )(feat_rows, row_norms, cents[1], warm_coef, *before, chunks[0], chunks[2], chunks[3])
+
+    def early_steps(coefs, grads):
+        coefs, before = dict(coefs), []
+        for d in EARLY:
+            coefs[d], total = call(
+                functools.partial(step_kernel, d=d), [coef_type, own_type], [low], name="step"
+            )(coefs[d], grads[d], kern, *before)
+            before = [total]
+        return coefs, before[0]
 
     for round_idx in range(ROUNDS):
-        sums = sum_over_groups(keep, send)
+        mine, theirs = sum_over_groups(keep, send)
         pieces, base = call(first_kernel, [grad_type, own_type], [res, score], name="first")(
-            *sums, own, kern, labels
+            mine, theirs, own, kern, labels
         )
         for _ in range(1, PASSES):
             grads = sum_and_gather(pieces)
-            pieces, coef = call(second_kernel, [grad_type, coef_type], [res, low], name="second")(
-                coef, *grads, base, kern, labels
-            )
+            coefs, total = early_steps(coefs, grads)
+            pieces, coefs[1] = call(
+                second_kernel, [grad_type, coef_type], [res, low], name="second"
+            )(coefs[1], grads[1], total, base, kern, labels)
         grads = sum_and_gather(pieces)
+        coefs, total = early_steps(coefs, grads)
         if round_idx < ROUNDS - 1:
-            coef, own, keep, send = call(
+            coefs[1], own, keep, send = call(
                 score_kernel, [coef_type, own_type, half_type, half_type], [low], name="scores"
-            )(coef, *grads, kern)
+            )(coefs[1], grads[1], total, kern)
     coef_out, keep, send = call(
         final_kernel,
         [like((CLASSES, centers), F32), last_type, last_type],
-        [coef_scratch, low, score],
+        [pltpu.VMEM((PAD, CHUNK), F32), low, score],
         name="final",
-    )(coef, *grads, kern)
+    )(coefs[0], coefs[2], coefs[3], coefs[1], grads[1], total, kern)
     partner = lax.ppermute(send, "centers", CORE_SWAP)
     parts = call(add_kernel, [like((WIRE, LANES), F32)] * Y, name="pair")(keep, partner)
     arrived = [lax.ppermute(parts[d], "centers", y_shift(d)) for d in (2, 1, 3)]

time: 317 us -> 313 us (0.987)
  waiting for transfers between devices: 73.5 us -> 54.2 us
  Pallas kernels: 30.8 us -> 40.6 us
    ppermute x15, waiting for transfers between devices: 40.1 us -> 20.8 us  [gather(): lax.ppermute(mine, 'rows', x_shift(d))]
    pallas_call x21 -> x33, Pallas kernels: 30.8 us -> 40.6 us  [call(): pl.pallas_call(kernel, out_shape=outs, in_specs=[smem] * scalars + [vmem]...]
  transfers between devices with their start and end apart: 30 -> 30, of which waited for: 29 -> 25; matrix products, arithmetic and copies ran while one was open for 1% -> 1% of each run, Pallas kernels for 1% -> 7%
where the time goes in v6:
time: 313 us; the launch traced here: 312 us
  blocking collectives  151 us (48%)
  starting transfers between devices  58.6 us (19%)
  waiting for transfers between devices  54.2 us (17%)
  Pallas kernels  40.6 us (13%)
  local copies, waits for them, and re-layouts  4.84 us (2%)
    all_to_all x9, blocking collectives, exchange(): lax.all_to_all(value, axis, split_axis=0, concat_axis=0, tiled=True, axis...  151 us
    pallas_call x33, Pallas kernels, call(): pl.pallas_call(kernel, out_shape=outs, in_specs=[smem] * scalars + [vmem]...  40.6 us
    ppermute x15, waiting for transfers between devices, gather(): lax.ppermute(mine, 'rows', x_shift(d))  20.8 us
    ppermute x15, starting transfers between devices, gather(): lax.ppermute(mine, 'rows', x_shift(d))  15.4 us
    ppermute x6, waiting for transfers between devices, sum_over_groups(): codes = [lax.ppermute(code, 'centers', y_shift(d)) for d in (2, 1, 3)]  14.7 us
    all_to_all x1, starting transfers between devices, exchange(): lax.all_to_all(value, axis, split_axis=0, concat_axis=0, tiled=True, axis...  11.9 us
    all_to_all x1, waiting for transfers between devices, exchange(): lax.all_to_all(value, axis, split_axis=0, concat_axis=0, tiled=True, axis...  9.68 us
    ppermute x2, starting transfers between devices, sum_over_groups(): partner = lax.ppermute(send, 'centers', CORE_SWAP)  8.32 us
  transfers between devices with their start and end apart: 30, of which 25 were waited for; matrix products, arithmetic and copies ran while one was open for 1% of the time, Pallas kernels for 7%

profile of v6, /device:TPU:1, one launch (start us, length us, event | category | flops | bytes accessed | tf_op | source)
XLA Modules:
  0.0 311.8 jit_solution(4002958426163526131)
XLA Ops:
  0.6 3.1 %select.3 = (bf16[32,16,256]{2,1,0:T(8,128)(2,1)}, f32[16,128]{1,0:T(8,128)S(1)}, s32[1]{0:T(128)}) custom-call(s32[1]{0:T(128)} %constant.13.clone.1.turn_ref, bf16[440,1024]{1,0:T(8,128)(2,1)} %feat_ref.1, s32[16,128]{1,0:T(8,128)} %bitcast.12), custom_call_target="tpu_custom_call" | custom-call | flops 1073741824 | bytes 4194304 | tf_op jit(solution)/shard_map/select/pallas_call | solution.py:49
  3.8 11.9 %all-to-all-start.1 = ((bf16[32,16,256]{2,1,0:T(8,128)(2,1)}), bf16[32,16,256]{2,1,0:T(8,128)(2,1)S(1)}, u32[]{:S(2)}, u32[]{:S(2)}) async-start(bf16[32,16,256]{2,1,0:T(8,128)(2,1)} %get-tuple-element.96), calls=%async_computation.1 | async-start | bytes 524288 | tf_op jit(solution)/shard_map/all_to_all | solution.py:333
  15.6 9.7 %all-to-all-done.1.in_ref = bf16[32,16,256]{2,1,0:T(8,128)(2,1)S(1)} async-done(((bf16[32,16,256]{2,1,0:T(8,128)(2,1)}), bf16[32,16,256]{2,1,0:T(8,128)(2,1)S(1)}, u32[]{:S(2)}, u32[]{:S(2)}) %all-to-all-start.1) | async-done | bytes 262176 | tf_op jit(solution)/shard_map/all_to_all | solution.py:333
  27.2 17.6 %all_to_all.55.c_ref = bf16[8,224,128]{2,1,0:T(8,128)(2,1)S(1)} all-to-all(bf16[8,224,128]{2,1,0:T(8,128)(2,1)S(1)} %get-tuple-element.99), channel_id=1, replica_groups={{0,8,16,24,32,40,48,56},{64,72,80,88,96,104,112,120},{128,136,144,152,1..., dimensions={0} | all-to-all | bytes 917504 | tf_op jit(solution)/shard_map/all_to_all | solution.py:333
  48.5 2.3 copy.7
  52.4 2.4 chunk.3
  54.8 3.4 %chunk.4 = (bf16[1024,512]{1,0:T(8,128)(2,1)S(1)}, f32[160,512]{1,0:T(8,128)S(1)}, f32[160,1024]{1,0:T(8,128)S(1)}) custom-call(bf16[1024,448]{1,0:T(8,128)(2,1)S(1)} %pad_bitcast_fusion.feat_ref, f32[1024,1]{1,0:T(8,128)S(1)} %copy.8.norm_ref, bf16[8,224,128]{2,1,0:T(8,128)(2,1)} %collective-permute-done.2.c_ref, f32[147,2048]{1,0:T(8,128)S(1)} %copy-done, ...), custom_call_target="tpu_custom_call" | custom-call | flops 1073741824 | bytes 4194304 | tf_op jit(solution)/shard_map/chunk/pallas_call | solution.py:49
  58.3 2.4 chunk.5
  60.7 8.5 %collective-permute-done.c_ref = bf16[8,224,128]{2,1,0:T(8,128)(2,1)S(1)} collective-permute-done((bf16[8,224,128]{2,1,0:T(8,128)(2,1)S(1)}, bf16[8,224,128]{2,1,0:T(8,128)(2,1)S(1)}, u32[]{:S(2)}, u32[]{:S(2)}) %collective-permute-start) | collective-permute-done | bytes 458784 | tf_op jit(solution)/shard_map/ppermute | solution.py:340
  69.2 2.7 build.1
  74.2 2.8 collective-permute-start.6
  80.2 4.1 %collective-permute-done.5.c1 = s16[160,512]{1,0:T(8,128)(2,1)S(1)} collective-permute-done((s16[160,512]{1,0:T(8,128)(2,1)S(1)}, s16[160,512]{1,0:T(8,128)(2,1)S(1)}, u32[]{:S(2)}, u32[]{:S(2)}) %collective-permute-start.5) | collective-permute-done | bytes 163872 | tf_op jit(solution)/shard_map/ppermute | solution.py:392
  85.9 2.6 collective-permute-start.7
  91.6 23.0 %all_to_all.56.in_ref = bf16[32,80,128]{2,1,0:T(8,128)(2,1)S(1)} all-to-all(bf16[32,80,128]{2,1,0:T(8,128)(2,1)S(1)} %get-tuple-element.113), channel_id=1, replica_groups=mesh['rows'=32,'centers'=8] {'rows'}, dimensions={0} | all-to-all | bytes 1310720 | tf_op jit(solution)/shard_map/all_to_all | solution.py:333
  114.7 14.3 %all_to_all.57.g_ref = bf16[8,80,128]{2,1,0:T(8,128)(2,1)S(1)} all-to-all(bf16[8,80,128]{2,1,0:T(8,128)(2,1)S(1)} %sum_at_owner.4), channel_id=1, replica_groups={{0,8,16,24,32,40,48,56},{64,72,80,88,96,104,112,120},{128,136,144,152,1..., dimensions={0} | all-to-all | bytes 327680 | tf_op jit(solution)/shard_map/all_to_all | solution.py:333
  138.2 2.8 second.2
  141.0 17.4 %all_to_all.58.in_ref = bf16[32,80,128]{2,1,0:T(8,128)(2,1)S(1)} all-to-all(bf16[32,80,128]{2,1,0:T(8,128)(2,1)S(1)} %get-tuple-element.122), channel_id=1, replica_groups=mesh['rows'=32,'centers'=8] {'rows'}, dimensions={0} | all-to-all | bytes 1310720 | tf_op jit(solution)/shard_map/all_to_all | solution.py:333
  158.5 13.5 %all_to_all.59.g_ref = bf16[8,80,128]{2,1,0:T(8,128)(2,1)S(1)} all-to-all(bf16[8,80,128]{2,1,0:T(8,128)(2,1)S(1)} %sum_at_owner.5), channel_id=1, replica_groups={{0,8,16,24,32,40,48,56},{64,72,80,88,96,104,112,120},{128,136,144,152,1..., dimensions={0} | all-to-all | bytes 327680 | tf_op jit(solution)/shard_map/all_to_all | solution.py:333
  182.3 7.5 %collective-permute-start.14 = (f32[152,512]{1,0:T(8,128)S(1)}, f32[152,512]{1,0:T(8,128)S(1)}, u32[]{:S(2)}, u32[]{:S(2)}) collective-permute-start(f32[152,512]{1,0:T(8,128)S(1)} %get-tuple-element.131), channel_id=1, source_target_pairs={{0,1},{1,0},{2,3},{3,2},{4,5},{5,4},{6,7},{7,6},{8,9},{9,8},{10,11... | collective-permute-start | bytes 933896 | tf_op jit(solution)/shard_map/ppermute | solution.py:387
  193.0 3.6 %collective-permute-done.17.c2 = s16[160,512]{1,0:T(8,128)(2,1)S(1)} collective-permute-done((s16[160,512]{1,0:T(8,128)(2,1)S(1)}, s16[160,512]{1,0:T(8,128)(2,1)S(1)}, u32[]{:S(2)}, u32[]{:S(2)}) %collective-permute-start.17) | collective-permute-done | bytes 163872 | tf_op jit(solution)/shard_map/ppermute | solution.py:392
  200.6 2.3 collective-permute-start.18
  205.9 19.8 %all_to_all.60.in_ref = bf16[32,80,128]{2,1,0:T(8,128)(2,1)S(1)} all-to-all(bf16[32,80,128]{2,1,0:T(8,128)(2,1)S(1)} %get-tuple-element.135), channel_id=1, replica_groups=mesh['rows'=32,'centers'=8] {'rows'}, dimensions={0} | all-to-all | bytes 1310720 | tf_op jit(solution)/shard_map/all_to_all | solution.py:333
  225.8 14.2 %all_to_all.61.g_ref = bf16[8,80,128]{2,1,0:T(8,128)(2,1)S(1)} all-to-all(bf16[8,80,128]{2,1,0:T(8,128)(2,1)S(1)} %sum_at_owner.6), channel_id=1, replica_groups={{0,8,16,24,32,40,48,56},{64,72,80,88,96,104,112,120},{128,136,144,152,1..., dimensions={0} | all-to-all | bytes 327680 | tf_op jit(solution)/shard_map/all_to_all | solution.py:333
  249.1 2.8 second.3
  251.9 17.8 %all_to_all.62.in_ref = bf16[32,80,128]{2,1,0:T(8,128)(2,1)S(1)} all-to-all(bf16[32,80,128]{2,1,0:T(8,128)(2,1)S(1)} %get-tuple-element.144), channel_id=1, replica_groups=mesh['rows'=32,'centers'=8] {'rows'}, dimensions={0} | all-to-all | bytes 1310720 | tf_op jit(solution)/shard_map/all_to_all | solution.py:333
  269.8 13.5 %all_to_all.63.g_ref = bf16[8,80,128]{2,1,0:T(8,128)(2,1)S(1)} all-to-all(bf16[8,80,128]{2,1,0:T(8,128)(2,1)S(1)} %sum_at_owner.7), channel_id=1, replica_groups={{0,8,16,24,32,40,48,56},{64,72,80,88,96,104,112,120},{128,136,144,152,1..., dimensions={0} | all-to-all | bytes 327680 | tf_op jit(solution)/shard_map/all_to_all | solution.py:333
  283.3 1.9 collective-permute-start.23
  289.3 2.4 collective-permute-done.22.g_ref
  292.8 2.3 final.1
  295.1 7.5 %collective-permute-start.25 = (f32[4,152,128]{2,1,0:T(8,128)S(1)}, f32[4,152,128]{2,1,0:T(8,128)S(1)}, u32[]{:S(2)}, u32[]{:S(2)}) collective-permute-start(f32[4,152,128]{2,1,0:T(8,128)S(1)} %get-tuple-element.156), channel_id=1, source_target_pairs={{0,1},{1,0},{2,3},{3,2},{4,5},{5,4},{6,7},{7,6},{8,9},{9,8},{10,11... | collective-permute-start | bytes 933896 | tf_op jit(solution)/shard_map/ppermute | solution.py:463
  305.6 2.7 collective-permute-start.28
  308.7 2.5 collective-permute-done.27
  (84 shorter events, 65.5 us)
Async XLA Ops:
  0.6 24.7 %copy-start.3 = (s32[1,2048]{1,0:T(1,128)S(1)}, s32[1,2048]{1,0:T(1,128)}, u32[]{:S(2)}) copy-start(s32[1,2048]{1,0:T(1,128)} %param.8) | copy-start | bytes 24580
  3.8 21.6 %all-to-all-start.1 = ((bf16[32,16,256]{2,1,0:T(8,128)(2,1)}), bf16[32,16,256]{2,1,0:T(8,128)(2,1)S(1)}, u32[]{:S(2)}, u32[]{:S(2)}) async-start(bf16[32,16,256]{2,1,0:T(8,128)(2,1)} %get-tuple-element.96), calls=%async_computation.1 | async-start | bytes 524288 | tf_op jit(solution)/shard_map/all_to_all | solution.py:333
  44.8 10.0 %collective-permute-start.2 = (bf16[8,224,128]{2,1,0:T(8,128)(2,1)S(1)}, bf16[8,224,128]{2,1,0:T(8,128)(2,1)}, u32[]{:S(2)}, u32[]{:S(2)}) collective-permute-start(bf16[8,224,128]{2,1,0:T(8,128)(2,1)S(1)} %all_to_all.55.c_ref), channel_id=1, source_target_pairs={{0,192},{8,200},{16,208},{24,216},{32,224},{40,232},{48,240},{56,2... | collective-permute-start | bytes 1376264 | tf_op jit(solution)/shard_map/ppermute | solution.py:340
  45.7 12.6 %collective-permute-start.1 = (bf16[8,224,128]{2,1,0:T(8,128)(2,1)S(1)}, bf16[8,224,128]{2,1,0:T(8,128)(2,1)S(1)}, u32[]{:S(2)}, u32[]{:S(2)}) collective-permute-start(bf16[8,224,128]{2,1,0:T(8,128)(2,1)S(1)} %all_to_all.55.c_ref), channel_id=1, source_target_pairs={{0,128},{8,136},{16,144},{24,152},{32,160},{40,168},{48,176},{56,1... | collective-permute-start | bytes 1376264 | tf_op jit(solution)/shard_map/ppermute | solution.py:340
  47.4 21.9 %collective-permute-start = (bf16[8,224,128]{2,1,0:T(8,128)(2,1)S(1)}, bf16[8,224,128]{2,1,0:T(8,128)(2,1)S(1)}, u32[]{:S(2)}, u32[]{:S(2)}) collective-permute-start(bf16[8,224,128]{2,1,0:T(8,128)(2,1)S(1)} %all_to_all.55.c_ref), channel_id=1, source_target_pairs={{0,64},{8,72},{16,80},{24,88},{32,96},{40,104},{48,112},{56,120},{... | collective-permute-start | bytes 1376264 | tf_op jit(solution)/shard_map/ppermute | solution.py:340
  71.9 2.1 collective-permute-start.3
  74.2 6.0 %collective-permute-start.6 = (s16[160,512]{1,0:T(8,128)(2,1)S(1)}, s16[160,512]{1,0:T(8,128)(2,1)S(1)}, u32[]{:S(2)}, u32[]{:S(2)}) collective-permute-start(s16[160,512]{1,0:T(8,128)(2,1)S(1)} %get-tuple-element.110), channel_id=1, source_target_pairs={{0,6},{1,7},{2,0},{3,1},{4,2},{5,3},{6,4},{7,5},{8,14},{9,15},{10,... | collective-permute-start | bytes 491528 | tf_op jit(solution)/shard_map/ppermute | solution.py:392
  77.0 7.3 %collective-permute-start.5 = (s16[160,512]{1,0:T(8,128)(2,1)S(1)}, s16[160,512]{1,0:T(8,128)(2,1)S(1)}, u32[]{:S(2)}, u32[]{:S(2)}) collective-permute-start(s16[160,512]{1,0:T(8,128)(2,1)S(1)} %get-tuple-element.110), channel_id=1, source_target_pairs={{0,2},{1,3},{2,4},{3,5},{4,6},{5,7},{6,0},{7,1},{8,10},{9,11},{10,... | collective-permute-start | bytes 491528 | tf_op jit(solution)/shard_map/ppermute | solution.py:392
  77.0 8.8 %collective-permute-start.4 = (s16[160,512]{1,0:T(8,128)(2,1)S(1)}, s16[160,512]{1,0:T(8,128)(2,1)S(1)}, u32[]{:S(2)}, u32[]{:S(2)}) collective-permute-start(s16[160,512]{1,0:T(8,128)(2,1)S(1)} %get-tuple-element.110), channel_id=1, source_target_pairs={{0,4},{1,5},{2,6},{3,7},{4,0},{5,1},{6,2},{7,3},{8,12},{9,13},{10,... | collective-permute-start | bytes 491528 | tf_op jit(solution)/shard_map/ppermute | solution.py:392
  85.8 4.0 %copy-start.1 = (s32[1024]{0:T(1024)S(1)}, s32[1024]{0:T(1024)}, u32[]{:S(2)}) copy-start(s32[1024]{0:T(1024)} %param.7) | copy-start | bytes 12292
  85.9 3.8 %collective-permute-start.7 = (f32[152,512]{1,0:T(8,128)S(1)}, f32[152,512]{1,0:T(8,128)S(1)}, u32[]{:S(2)}, u32[]{:S(2)}) collective-permute-start(f32[152,512]{1,0:T(8,128)S(1)} %decode.2.mine_ref), channel_id=1, source_target_pairs={{0,1},{1,0},{2,3},{3,2},{4,5},{5,4},{6,7},{7,6},{8,9},{9,8},{10,11... | collective-permute-start | bytes 933896 | tf_op jit(solution)/shard_map/ppermute | solution.py:394
  129.0 4.2 %collective-permute-start.10 = (bf16[8,80,128]{2,1,0:T(8,128)(2,1)S(1)}, bf16[8,80,128]{2,1,0:T(8,128)(2,1)S(1)}, u32[]{:S(2)}, u32[]{:S(2)}) collective-permute-start(bf16[8,80,128]{2,1,0:T(8,128)(2,1)S(1)} %all_to_all.57.g_ref), channel_id=1, source_target_pairs={{0,192},{8,200},{16,208},{24,216},{32,224},{40,232},{48,240},{56,2... | collective-permute-start | bytes 491528 | tf_op jit(solution)/shard_map/ppermute | solution.py:340
  130.3 5.8 %collective-permute-start.9 = (bf16[8,80,128]{2,1,0:T(8,128)(2,1)S(1)}, bf16[8,80,128]{2,1,0:T(8,128)(2,1)S(1)}, u32[]{:S(2)}, u32[]{:S(2)}) collective-permute-start(bf16[8,80,128]{2,1,0:T(8,128)(2,1)S(1)} %all_to_all.57.g_ref), channel_id=1, source_target_pairs={{0,128},{8,136},{16,144},{24,152},{32,160},{40,168},{48,176},{56,1... | collective-permute-start | bytes 491528 | tf_op jit(solution)/shard_map/ppermute | solution.py:340
  131.4 6.8 %collective-permute-start.8 = (bf16[8,80,128]{2,1,0:T(8,128)(2,1)S(1)}, bf16[8,80,128]{2,1,0:T(8,128)(2,1)S(1)}, u32[]{:S(2)}, u32[]{:S(2)}) collective-permute-start(bf16[8,80,128]{2,1,0:T(8,128)(2,1)S(1)} %all_to_all.57.g_ref), channel_id=1, source_target_pairs={{0,64},{8,72},{16,80},{24,88},{32,96},{40,104},{48,112},{56,120},{... | collective-permute-start | bytes 491528 | tf_op jit(solution)/shard_map/ppermute | solution.py:340
  172.0 5.7 %collective-permute-start.13 = (bf16[8,80,128]{2,1,0:T(8,128)(2,1)S(1)}, bf16[8,80,128]{2,1,0:T(8,128)(2,1)S(1)}, u32[]{:S(2)}, u32[]{:S(2)}) collective-permute-start(bf16[8,80,128]{2,1,0:T(8,128)(2,1)S(1)} %all_to_all.59.g_ref), channel_id=1, source_target_pairs={{0,192},{8,200},{16,208},{24,216},{32,224},{40,232},{48,240},{56,2... | collective-permute-start | bytes 491528 | tf_op jit(solution)/shard_map/ppermute | solution.py:340
  173.8 5.8 %collective-permute-start.12 = (bf16[8,80,128]{2,1,0:T(8,128)(2,1)S(1)}, bf16[8,80,128]{2,1,0:T(8,128)(2,1)S(1)}, u32[]{:S(2)}, u32[]{:S(2)}) collective-permute-start(bf16[8,80,128]{2,1,0:T(8,128)(2,1)S(1)} %all_to_all.59.g_ref), channel_id=1, source_target_pairs={{0,128},{8,136},{16,144},{24,152},{32,160},{40,168},{48,176},{56,1... | collective-permute-start | bytes 491528 | tf_op jit(solution)/shard_map/ppermute | solution.py:340
  174.8 6.4 %collective-permute-start.11 = (bf16[8,80,128]{2,1,0:T(8,128)(2,1)S(1)}, bf16[8,80,128]{2,1,0:T(8,128)(2,1)S(1)}, u32[]{:S(2)}, u32[]{:S(2)}) collective-permute-start(bf16[8,80,128]{2,1,0:T(8,128)(2,1)S(1)} %all_to_all.59.g_ref), channel_id=1, source_target_pairs={{0,64},{8,72},{16,80},{24,88},{32,96},{40,104},{48,112},{56,120},{... | collective-permute-start | bytes 491528 | tf_op jit(solution)/shard_map/ppermute | solution.py:340
  182.3 8.7 %collective-permute-start.14 = (f32[152,512]{1,0:T(8,128)S(1)}, f32[152,512]{1,0:T(8,128)S(1)}, u32[]{:S(2)}, u32[]{:S(2)}) collective-permute-start(f32[152,512]{1,0:T(8,128)S(1)} %get-tuple-element.131), channel_id=1, source_target_pairs={{0,1},{1,0},{2,3},{3,2},{4,5},{5,4},{6,7},{7,6},{8,9},{9,8},{10,11... | collective-permute-start | bytes 933896 | tf_op jit(solution)/shard_map/ppermute | solution.py:387
  191.1 5.5 %collective-permute-start.17 = (s16[160,512]{1,0:T(8,128)(2,1)S(1)}, s16[160,512]{1,0:T(8,128)(2,1)S(1)}, u32[]{:S(2)}, u32[]{:S(2)}) collective-permute-start(s16[160,512]{1,0:T(8,128)(2,1)S(1)} %get-tuple-element.133), channel_id=1, source_target_pairs={{0,6},{1,7},{2,0},{3,1},{4,2},{5,3},{6,4},{7,5},{8,14},{9,15},{10,... | collective-permute-start | bytes 491528 | tf_op jit(solution)/shard_map/ppermute | solution.py:392
  191.2 7.3 %collective-permute-start.16 = (s16[160,512]{1,0:T(8,128)(2,1)S(1)}, s16[160,512]{1,0:T(8,128)(2,1)S(1)}, u32[]{:S(2)}, u32[]{:S(2)}) collective-permute-start(s16[160,512]{1,0:T(8,128)(2,1)S(1)} %get-tuple-element.133), channel_id=1, source_target_pairs={{0,2},{1,3},{2,4},{3,5},{4,6},{5,7},{6,0},{7,1},{8,10},{9,11},{10,... | collective-permute-start | bytes 491528 | tf_op jit(solution)/shard_map/ppermute | solution.py:392
  192.7 7.8 %collective-permute-start.15 = (s16[160,512]{1,0:T(8,128)(2,1)S(1)}, s16[160,512]{1,0:T(8,128)(2,1)S(1)}, u32[]{:S(2)}, u32[]{:S(2)}) collective-permute-start(s16[160,512]{1,0:T(8,128)(2,1)S(1)} %get-tuple-element.133), channel_id=1, source_target_pairs={{0,4},{1,5},{2,6},{3,7},{4,0},{5,1},{6,2},{7,3},{8,12},{9,13},{10,... | collective-permute-start | bytes 491528 | tf_op jit(solution)/shard_map/ppermute | solution.py:392
  200.6 3.5 %collective-permute-start.18 = (f32[152,512]{1,0:T(8,128)S(1)}, f32[152,512]{1,0:T(8,128)S(1)}, u32[]{:S(2)}, u32[]{:S(2)}) collective-permute-start(f32[152,512]{1,0:T(8,128)S(1)} %decode.3.mine_ref), channel_id=1, source_target_pairs={{0,1},{1,0},{2,3},{3,2},{4,5},{5,4},{6,7},{7,6},{8,9},{9,8},{10,11... | collective-permute-start | bytes 933896 | tf_op jit(solution)/shard_map/ppermute | solution.py:394
  240.1 4.2 %collective-permute-start.21 = (bf16[8,80,128]{2,1,0:T(8,128)(2,1)S(1)}, bf16[8,80,128]{2,1,0:T(8,128)(2,1)S(1)}, u32[]{:S(2)}, u32[]{:S(2)}) collective-permute-start(bf16[8,80,128]{2,1,0:T(8,128)(2,1)S(1)} %all_to_all.61.g_ref), channel_id=1, source_target_pairs={{0,192},{8,200},{16,208},{24,216},{32,224},{40,232},{48,240},{56,2... | collective-permute-start | bytes 491528 | tf_op jit(solution)/shard_map/ppermute | solution.py:340
  241.3 5.8 %collective-permute-start.20 = (bf16[8,80,128]{2,1,0:T(8,128)(2,1)S(1)}, bf16[8,80,128]{2,1,0:T(8,128)(2,1)S(1)}, u32[]{:S(2)}, u32[]{:S(2)}) collective-permute-start(bf16[8,80,128]{2,1,0:T(8,128)(2,1)S(1)} %all_to_all.61.g_ref), channel_id=1, source_target_pairs={{0,128},{8,136},{16,144},{24,152},{32,160},{40,168},{48,176},{56,1... | collective-permute-start | bytes 491528 | tf_op jit(solution)/shard_map/ppermute | solution.py:340
  242.6 6.5 %collective-permute-start.19 = (bf16[8,80,128]{2,1,0:T(8,128)(2,1)S(1)}, bf16[8,80,128]{2,1,0:T(8,128)(2,1)S(1)}, u32[]{:S(2)}, u32[]{:S(2)}) collective-permute-start(bf16[8,80,128]{2,1,0:T(8,128)(2,1)S(1)} %all_to_all.61.g_ref), channel_id=1, source_target_pairs={{0,64},{8,72},{16,80},{24,88},{32,96},{40,104},{48,112},{56,120},{... | collective-permute-start | bytes 491528 | tf_op jit(solution)/shard_map/ppermute | solution.py:340
  283.3 4.9 %collective-permute-start.23 = (bf16[8,80,128]{2,1,0:T(8,128)(2,1)S(1)}, bf16[8,80,128]{2,1,0:T(8,128)(2,1)S(1)}, u32[]{:S(2)}, u32[]{:S(2)}) collective-permute-start(bf16[8,80,128]{2,1,0:T(8,128)(2,1)S(1)} %all_to_all.63.g_ref), channel_id=1, source_target_pairs={{0,192},{8,200},{16,208},{24,216},{32,224},{40,232},{48,240},{56,2... | collective-permute-start | bytes 491528 | tf_op jit(solution)/shard_map/ppermute | solution.py:340
  285.2 7.5 %collective-permute-start.24 = (bf16[8,80,128]{2,1,0:T(8,128)(2,1)S(1)}, bf16[8,80,128]{2,1,0:T(8,128)(2,1)S(1)}, u32[]{:S(2)}, u32[]{:S(2)}) collective-permute-start(bf16[8,80,128]{2,1,0:T(8,128)(2,1)S(1)} %all_to_all.63.g_ref), channel_id=1, source_target_pairs={{0,64},{8,72},{16,80},{24,88},{32,96},{40,104},{48,112},{56,120},{... | collective-permute-start | bytes 491528 | tf_op jit(solution)/shard_map/ppermute | solution.py:340
  285.3 6.4 %collective-permute-start.22 = (bf16[8,80,128]{2,1,0:T(8,128)(2,1)S(1)}, bf16[8,80,128]{2,1,0:T(8,128)(2,1)S(1)}, u32[]{:S(2)}, u32[]{:S(2)}) collective-permute-start(bf16[8,80,128]{2,1,0:T(8,128)(2,1)S(1)} %all_to_all.63.g_ref), channel_id=1, source_target_pairs={{0,128},{8,136},{16,144},{24,152},{32,160},{40,168},{48,176},{56,1... | collective-permute-start | bytes 491528 | tf_op jit(solution)/shard_map/ppermute | solution.py:340
  295.1 8.7 %collective-permute-start.25 = (f32[4,152,128]{2,1,0:T(8,128)S(1)}, f32[4,152,128]{2,1,0:T(8,128)S(1)}, u32[]{:S(2)}, u32[]{:S(2)}) collective-permute-start(f32[4,152,128]{2,1,0:T(8,128)S(1)} %get-tuple-element.156), channel_id=1, source_target_pairs={{0,1},{1,0},{2,3},{3,2},{4,5},{5,4},{6,7},{7,6},{8,9},{9,8},{10,11... | collective-permute-start | bytes 933896 | tf_op jit(solution)/shard_map/ppermute | solution.py:463
  303.8 4.8 %collective-permute-start.26 = (f32[152,128]{1,0:T(8,128)S(1)}, f32[152,128]{1,0:T(8,128)S(1)}, u32[]{:S(2)}, u32[]{:S(2)}) collective-permute-start(f32[152,128]{1,0:T(8,128)S(1)} %get-tuple-element.158), channel_id=1, source_target_pairs={{0,4},{1,5},{2,6},{3,7},{4,0},{5,1},{6,2},{7,3},{8,12},{9,13},{10,... | collective-permute-start | bytes 233480 | tf_op jit(solution)/shard_map/ppermute | solution.py:465
  305.6 5.6 %collective-permute-start.27 = (f32[152,128]{1,0:T(8,128)S(1)}, f32[152,128]{1,0:T(8,128)S(1)}, u32[]{:S(2)}, u32[]{:S(2)}) collective-permute-start(f32[152,128]{1,0:T(8,128)S(1)} %get-tuple-element.159), channel_id=1, source_target_pairs={{0,2},{1,3},{2,4},{3,5},{4,6},{5,7},{6,0},{7,1},{8,10},{9,11},{10,... | collective-permute-start | bytes 233480 | tf_op jit(solution)/shard_map/ppermute | solution.py:465
  305.6 5.6 %collective-permute-start.28 = (f32[152,128]{1,0:T(8,128)S(1)}, f32[152,128]{1,0:T(8,128)S(1)}, u32[]{:S(2)}, u32[]{:S(2)}) collective-permute-start(f32[152,128]{1,0:T(8,128)S(1)} %get-tuple-element.160), channel_id=1, source_target_pairs={{0,6},{1,7},{2,0},{3,1},{4,2},{5,3},{6,4},{7,5},{8,14},{9,15},{10,... | collective-permute-start | bytes 233480 | tf_op jit(solution)/shard_map/ppermute | solution.py:465
  (2 other events, 5.1 us)

commit v7 on v6

--- a/solution.py
+++ b/solution.py
@@ -42,14 +42,16 @@
     return [(y * CORES + k, (y + d) % Y * CORES + k) for y in range(Y) for k in range(CORES)]
 
 
-def call(kernel, outs, scratch=(), name=None, scalars=0, last_scalar=False):
+def call(kernel, outs, scratch=(), name=None, scalars=0, far=0, last_scalar=False):
     vmem = pl.BlockSpec(memory_space=pltpu.VMEM)
     smem = pl.BlockSpec(memory_space=pltpu.SMEM)
     many = isinstance(outs, (list, tuple))
     return lambda *args: pl.pallas_call(
         kernel,
         out_shape=outs,
-        in_specs=[smem] * scalars + [vmem] * (len(args) - scalars),
+        in_specs=[smem] * scalars
+        + [vmem] * (len(args) - scalars - far)
+        + [pl.BlockSpec(memory_space=pltpu.HBM)] * far,
         out_specs=([vmem] * (len(outs) - last_scalar) + [smem] * last_scalar) if many else vmem,
         scratch_shapes=list(scratch),
         compiler_params=pltpu.CompilerParams(vmem_limit_bytes=GRANT),
@@ -100,7 +102,11 @@
     )
 
 
-def select_kernel(turn_ref, feat_ref, index_ref, out_ref, rank_ref, top_ref, hot_ref):
+def select_kernel(
+    turn_ref, index_ref, far_ref, out_ref, rank_ref, top_ref, hot_ref, feat_ref, copied
+):
+    copy = pltpu.make_async_copy(far_ref, feat_ref, copied)
+    copy.start()
     rows = feat_ref.shape[1]
     blocks = index_ref.shape[0]
     half = FPAD // 2
@@ -123,6 +129,7 @@
         return 0
 
     lax.fori_loop(0, blocks, find, 0, unroll=4)
+    copy.wait()
     for h, stop in ((0, half), (1, FEAT)):
         got = dot_nt(hot_ref[...], feat_ref[h * half : stop, :]).astype(BF16)
         for b in range(blocks):
@@ -314,13 +321,9 @@
 
 
 def final_kernel(
-    c0, c2, c3, coef_ref, g_ref, before_ref, kern_ref,
-    coef_out_ref, keep_ref, send_ref, new_ref, low_ref, own_ref,
+    coef_ref, g_ref, before_ref, kern_ref, new_ref, keep_ref, send_ref, low_ref, own_ref
 ):
     update(coef_ref, g_ref, new_ref, low_ref)
-    for d, ref in enumerate((c0, new_ref, c2, c3)):
-        to = pl.ds(pl.multiple_of(chunk_of(d) * CHUNK, CHUNK), CHUNK)
-        coef_out_ref[:, to] = ref[:CLASSES, :]
     add_scores(low_ref, kern_ref, CHUNK, before_ref, own_ref)
     core = my_core()
     for d in range(Y):
@@ -329,6 +332,12 @@
             ref[d] = own_ref[:WIRE, pl.ds(pl.multiple_of((y * CORES + k) * LANES, LANES), LANES)]
 
 
+def order_kernel(c0, c1, c2, c3, coef_out_ref):
+    for d, ref in enumerate((c0, c1, c2, c3)):
+        to = pl.ds(pl.multiple_of(chunk_of(d) * CHUNK, CHUNK), CHUNK)
+        coef_out_ref[:, to] = ref[:CLASSES, :]
+
+
 def exchange(value, axis, groups=None):
     return lax.all_to_all(
         value, axis, split_axis=0, concat_axis=0, tiled=True, axis_index_groups=groups
@@ -346,7 +355,7 @@
     return gather(copies)
 
 
-def gather_centers(features, center_index):
+def gather_centers(features, center_index, beside):
     rows = features.shape[1]
     index = center_index.reshape(-1, PART)
 
@@ -354,11 +363,16 @@
         return call(
             select_kernel,
             [like((X * Z, SLOTS, 256), BF16), like(index.shape, F32), like((1,), jnp.int32)],
-            [pltpu.VMEM((index.shape[0] * SLOTS, rows), BF16)],
+            [
+                pltpu.VMEM((index.shape[0] * SLOTS, rows), BF16),
+                pltpu.VMEM(features.shape, BF16),
+                pltpu.SemaphoreType.DMA,
+            ],
             name="select",
             scalars=1,
+            far=1,
             last_scalar=True,
-        )(turn, features, index)
+        )(turn, index, features)
 
     def place(turn, pieces, rank):
         return call(
@@ -371,6 +385,7 @@
     start = jnp.zeros((1,), jnp.int32)
     pieces, rank, top = select(start)
     copies = place(start, pieces, rank)
+    copies, beside = lax.optimization_barrier((copies, beside))
 
     def another(state):
         turn, copies = state
@@ -380,7 +395,7 @@
     _, copies = lax.while_loop(
         lambda state: state[0][0] * SLOTS <= top[0], another, (start + 1, copies)
     )
-    return gather(copies)
+    return gather(copies), beside
 
 
 def sum_over_groups(keep, send):
@@ -411,7 +426,9 @@
 
     row_norms = jnp.sum(jnp.square(features.astype(F32)), axis=0).reshape(rows, 1)
     feat_rows = jnp.pad(features, ((0, FPAD - FEAT), (0, 0))).T
-    cents = gather_centers(features, center_index)
+    cents, (feat_rows, row_norms) = gather_centers(
+        features, center_index, (feat_rows, row_norms)
+    )
     before, chunks, coefs = [], {}, {}
     for d in EARLY:
         chunks[d], coefs[d], total = call(
@@ -454,12 +471,12 @@
             coefs[1], own, keep, send = call(
                 score_kernel, [coef_type, own_type, half_type, half_type], [low], name="scores"
             )(coefs[1], grads[1], total, kern)
-    coef_out, keep, send = call(
-        final_kernel,
-        [like((CLASSES, centers), F32), last_type, last_type],
-        [pltpu.VMEM((PAD, CHUNK), F32), low, score],
-        name="final",
-    )(coefs[0], coefs[2], coefs[3], coefs[1], grads[1], total, kern)
+    coefs[1], keep, send = call(
+        final_kernel, [coef_type, last_type, last_type], [low, score], name="final"
+    )(coefs[1], grads[1], total, kern)
+    coef_out = call(order_kernel, like((CLASSES, centers), F32), name="order")(
+        *(coefs[d] for d in range(X))
+    )
     partner = lax.ppermute(send, "centers", CORE_SWAP)
     parts = call(add_kernel, [like((WIRE, LANES), F32)] * Y, name="pair")(keep, partner)
     arrived = [lax.ppermute(parts[d], "centers", y_shift(d)) for d in (2, 1, 3)]

time: 313 us -> 312 us (level)
    pallas_call x33 -> x34, Pallas kernels: 40.6 us -> 42.7 us  [call(): pl.pallas_call(kernel, out_shape=outs, in_specs=[smem] * scalars + [vmem]...]
  transfers between devices with their start and end apart: 30 -> 30, of which waited for: 25 -> 27; matrix products, arithmetic and copies ran while one was open for 1% -> 1% of each run, Pallas kernels for 7% -> 8%
where the time goes in v7:
time: 312 us; the launch traced here: 311 us
  blocking collectives  152 us (49%)
  starting transfers between devices  57.6 us (18%)
  waiting for transfers between devices  52.8 us (17%)
  Pallas kernels  42.7 us (14%)
    all_to_all x9, blocking collectives, exchange(): lax.all_to_all(value, axis, split_axis=0, concat_axis=0, tiled=True, axis...  152 us
    pallas_call x34, Pallas kernels, call(): pl.pallas_call(kernel, out_shape=outs, in_specs=[smem] * scalars + [vmem]...  42.7 us
    ppermute x15, waiting for transfers between devices, gather(): lax.ppermute(mine, 'rows', x_shift(d))  23.6 us
    ppermute x6, waiting for transfers between devices, sum_over_groups(): codes = [lax.ppermute(code, 'centers', y_shift(d)) for d in (2, 1, 3)]  14.7 us
    ppermute x15, starting transfers between devices, gather(): lax.ppermute(mine, 'rows', x_shift(d))  14.5 us
    all_to_all x1, starting transfers between devices, exchange(): lax.all_to_all(value, axis, split_axis=0, concat_axis=0, tiled=True, axis...  11.9 us
    ppermute x2, starting transfers between devices, sum_over_groups(): partner = lax.ppermute(send, 'centers', CORE_SWAP)  8.27 us
    ppermute x1, starting transfers between devices, body(): partner = lax.ppermute(send, 'centers', CORE_SWAP)  7.35 us
  transfers between devices with their start and end apart: 30, of which 27 were waited for; matrix products, arithmetic and copies ran while one was open for 1% of the time, Pallas kernels for 8%

profile of v7, /device:TPU:1, one launch (start us, length us, event | category | flops | bytes accessed | tf_op | source)
XLA Modules:
  0.0 310.9 jit_solution(9799751726688658212)
XLA Ops:
  0.6 3.1 select.3
  3.7 11.9 %all-to-all-start.1 = ((bf16[32,16,256]{2,1,0:T(8,128)(2,1)}), bf16[32,16,256]{2,1,0:T(8,128)(2,1)S(1)}, u32[]{:S(2)}, u32[]{:S(2)}) async-start(bf16[32,16,256]{2,1,0:T(8,128)(2,1)} %get-tuple-element.99), calls=%async_computation.1 | async-start | bytes 524288 | tf_op jit(solution)/shard_map/all_to_all | solution.py:342
  18.6 6.7 %all-to-all-done.1.in_ref = bf16[32,16,256]{2,1,0:T(8,128)(2,1)S(1)} async-done(((bf16[32,16,256]{2,1,0:T(8,128)(2,1)}), bf16[32,16,256]{2,1,0:T(8,128)(2,1)S(1)}, u32[]{:S(2)}, u32[]{:S(2)}) %all-to-all-start.1) | async-done | bytes 262176 | tf_op jit(solution)/shard_map/all_to_all | solution.py:342
  26.2 17.7 %all_to_all.55.c_ref = bf16[8,224,128]{2,1,0:T(8,128)(2,1)} all-to-all(bf16[8,224,128]{2,1,0:T(8,128)(2,1)S(1)} %get-tuple-element.105), channel_id=1, replica_groups={{0,8,16,24,32,40,48,56},{64,72,80,88,96,104,112,120},{128,136,144,152,1..., dimensions={0} | all-to-all | bytes 917504 | tf_op jit(solution)/shard_map/all_to_all | solution.py:342
  47.4 3.4 %chunk.3 = (bf16[1024,512]{1,0:T(8,128)(2,1)S(1)}, f32[160,512]{1,0:T(8,128)S(1)}, f32[160,1024]{1,0:T(8,128)S(1)}) custom-call(bf16[1024,448]{1,0:T(8,128)(2,1)S(1)} %pad_bitcast_fusion.feat_ref, f32[1024,1]{1,0:T(8,128)S(1)} %copy.8.norm_ref, bf16[8,224,128]{2,1,0:T(8,128)(2,1)} %all_to_all.55.c_ref, f32[147,2048]{1,0:T(8,128)S(1)} %copy-done), custom_call_target="tpu_custom_call" | custom-call | flops 1073741824 | bytes 4194304 | tf_op jit(solution)/shard_map/chunk/pallas_call | solution.py:49
  52.3 3.4 %chunk.4 = (bf16[1024,512]{1,0:T(8,128)(2,1)S(1)}, f32[160,512]{1,0:T(8,128)S(1)}, f32[160,1024]{1,0:T(8,128)S(1)}) custom-call(bf16[1024,448]{1,0:T(8,128)(2,1)S(1)} %pad_bitcast_fusion.feat_ref, f32[1024,1]{1,0:T(8,128)S(1)} %copy.8.norm_ref, bf16[8,224,128]{2,1,0:T(8,128)(2,1)} %collective-permute-done.2.c_ref, f32[147,2048]{1,0:T(8,128)S(1)} %copy-done, ...), custom_call_target="tpu_custom_call" | custom-call | flops 1073741824 | bytes 4194304 | tf_op jit(solution)/shard_map/chunk/pallas_call | solution.py:49
  55.8 3.4 %chunk.5 = (bf16[1024,512]{1,0:T(8,128)(2,1)S(1)}, f32[160,512]{1,0:T(8,128)S(1)}, f32[160,1024]{1,0:T(8,128)S(1)}) custom-call(bf16[1024,448]{1,0:T(8,128)(2,1)S(1)} %pad_bitcast_fusion.feat_ref, f32[1024,1]{1,0:T(8,128)S(1)} %copy.8.norm_ref, bf16[8,224,128]{2,1,0:T(8,128)(2,1)} %collective-permute-done.1.c_ref, f32[147,2048]{1,0:T(8,128)S(1)} %copy-done, ...), custom_call_target="tpu_custom_call" | custom-call | flops 1073741824 | bytes 4194304 | tf_op jit(solution)/shard_map/chunk/pallas_call | solution.py:49
  59.2 9.3 %collective-permute-done.c_ref = bf16[8,224,128]{2,1,0:T(8,128)(2,1)S(1)} collective-permute-done((bf16[8,224,128]{2,1,0:T(8,128)(2,1)}, bf16[8,224,128]{2,1,0:T(8,128)(2,1)S(1)}, u32[]{:S(2)}, u32[]{:S(2)}) %collective-permute-start) | collective-permute-done | bytes 458784 | tf_op jit(solution)/shard_map/ppermute | solution.py:349
  68.6 2.7 build.1
  73.5 2.8 collective-permute-start.6
  79.5 4.1 %collective-permute-done.5.c1 = s16[160,512]{1,0:T(8,128)(2,1)S(1)} collective-permute-done((s16[160,512]{1,0:T(8,128)(2,1)S(1)}, s16[160,512]{1,0:T(8,128)(2,1)S(1)}, u32[]{:S(2)}, u32[]{:S(2)}) %collective-permute-start.5) | collective-permute-done | bytes 163872 | tf_op jit(solution)/shard_map/ppermute | solution.py:407
  85.3 2.6 collective-permute-start.7
  89.1 1.8 first.2
  90.9 24.1 %all_to_all.56.in_ref = bf16[32,80,128]{2,1,0:T(8,128)(2,1)S(1)} all-to-all(bf16[32,80,128]{2,1,0:T(8,128)(2,1)S(1)} %get-tuple-element.119), channel_id=1, replica_groups=mesh['rows'=32,'centers'=8] {'rows'}, dimensions={0} | all-to-all | bytes 1310720 | tf_op jit(solution)/shard_map/all_to_all | solution.py:342
  115.2 14.3 %all_to_all.57.g_ref = bf16[8,80,128]{2,1,0:T(8,128)(2,1)S(1)} all-to-all(bf16[8,80,128]{2,1,0:T(8,128)(2,1)S(1)} %sum_at_owner.4), channel_id=1, replica_groups={{0,8,16,24,32,40,48,56},{64,72,80,88,96,104,112,120},{128,136,144,152,1..., dimensions={0} | all-to-all | bytes 327680 | tf_op jit(solution)/shard_map/all_to_all | solution.py:342
  138.7 2.8 second.2
  141.5 17.4 %all_to_all.58.in_ref = bf16[32,80,128]{2,1,0:T(8,128)(2,1)S(1)} all-to-all(bf16[32,80,128]{2,1,0:T(8,128)(2,1)S(1)} %get-tuple-element.128), channel_id=1, replica_groups=mesh['rows'=32,'centers'=8] {'rows'}, dimensions={0} | all-to-all | bytes 1310720 | tf_op jit(solution)/shard_map/all_to_all | solution.py:342
  159.0 13.5 %all_to_all.59.g_ref = bf16[8,80,128]{2,1,0:T(8,128)(2,1)S(1)} all-to-all(bf16[8,80,128]{2,1,0:T(8,128)(2,1)S(1)} %sum_at_owner.5), channel_id=1, replica_groups={{0,8,16,24,32,40,48,56},{64,72,80,88,96,104,112,120},{128,136,144,152,1..., dimensions={0} | all-to-all | bytes 327680 | tf_op jit(solution)/shard_map/all_to_all | solution.py:342
  182.8 7.5 %collective-permute-start.14 = (f32[152,512]{1,0:T(8,128)S(1)}, f32[152,512]{1,0:T(8,128)S(1)}, u32[]{:S(2)}, u32[]{:S(2)}) collective-permute-start(f32[152,512]{1,0:T(8,128)S(1)} %get-tuple-element.137), channel_id=1, source_target_pairs={{0,1},{1,0},{2,3},{3,2},{4,5},{5,4},{6,7},{7,6},{8,9},{9,8},{10,11... | collective-permute-start | bytes 933896 | tf_op jit(solution)/shard_map/ppermute | solution.py:402
  193.4 3.6 %collective-permute-done.17.c2 = s16[160,512]{1,0:T(8,128)(2,1)S(1)} collective-permute-done((s16[160,512]{1,0:T(8,128)(2,1)S(1)}, s16[160,512]{1,0:T(8,128)(2,1)S(1)}, u32[]{:S(2)}, u32[]{:S(2)}) %collective-permute-start.17) | collective-permute-done | bytes 163872 | tf_op jit(solution)/shard_map/ppermute | solution.py:407
  197.0 1.9 collective-permute-done.16.c1
  198.9 2.0 collective-permute-done.15.c0
  201.0 2.3 collective-permute-start.18
  204.5 1.8 first.3
  206.4 19.8 %all_to_all.60.in_ref = bf16[32,80,128]{2,1,0:T(8,128)(2,1)S(1)} all-to-all(bf16[32,80,128]{2,1,0:T(8,128)(2,1)S(1)} %get-tuple-element.141), channel_id=1, replica_groups=mesh['rows'=32,'centers'=8] {'rows'}, dimensions={0} | all-to-all | bytes 1310720 | tf_op jit(solution)/shard_map/all_to_all | solution.py:342
  226.3 14.2 %all_to_all.61.g_ref = bf16[8,80,128]{2,1,0:T(8,128)(2,1)S(1)} all-to-all(bf16[8,80,128]{2,1,0:T(8,128)(2,1)S(1)} %sum_at_owner.6), channel_id=1, replica_groups={{0,8,16,24,32,40,48,56},{64,72,80,88,96,104,112,120},{128,136,144,152,1..., dimensions={0} | all-to-all | bytes 327680 | tf_op jit(solution)/shard_map/all_to_all | solution.py:342
  249.6 2.8 second.3
  252.4 17.8 %all_to_all.62.in_ref = bf16[32,80,128]{2,1,0:T(8,128)(2,1)S(1)} all-to-all(bf16[32,80,128]{2,1,0:T(8,128)(2,1)S(1)} %get-tuple-element.150), channel_id=1, replica_groups=mesh['rows'=32,'centers'=8] {'rows'}, dimensions={0} | all-to-all | bytes 1310720 | tf_op jit(solution)/shard_map/all_to_all | solution.py:342
  270.3 13.5 %all_to_all.63.g_ref = bf16[8,80,128]{2,1,0:T(8,128)(2,1)S(1)} all-to-all(bf16[8,80,128]{2,1,0:T(8,128)(2,1)S(1)} %sum_at_owner.7), channel_id=1, replica_groups={{0,8,16,24,32,40,48,56},{64,72,80,88,96,104,112,120},{128,136,144,152,1..., dimensions={0} | all-to-all | bytes 327680 | tf_op jit(solution)/shard_map/all_to_all | solution.py:342
  283.8 1.9 collective-permute-start.24
  294.3 7.4 %collective-permute-start.25 = (f32[4,152,128]{2,1,0:T(8,128)S(1)}, f32[4,152,128]{2,1,0:T(8,128)S(1)}, u32[]{:S(2)}, u32[]{:S(2)}) collective-permute-start(f32[4,152,128]{2,1,0:T(8,128)S(1)} %get-tuple-element.162), channel_id=1, source_target_pairs={{0,1},{1,0},{2,3},{3,2},{4,5},{5,4},{6,7},{7,6},{8,9},{9,8},{10,11... | collective-permute-start | bytes 933896 | tf_op jit(solution)/shard_map/ppermute | solution.py:480
  304.7 2.7 collective-permute-start.28
  (83 shorter events, 65.7 us)
Async XLA Ops:
  3.7 21.6 %all-to-all-start.1 = ((bf16[32,16,256]{2,1,0:T(8,128)(2,1)}), bf16[32,16,256]{2,1,0:T(8,128)(2,1)S(1)}, u32[]{:S(2)}, u32[]{:S(2)}) async-start(bf16[32,16,256]{2,1,0:T(8,128)(2,1)} %get-tuple-element.99), calls=%async_computation.1 | async-start | bytes 524288 | tf_op jit(solution)/shard_map/all_to_all | solution.py:342
  17.0 8.2 %copy-start.2 = (s32[1,2048]{1,0:T(1,128)S(1)}, s32[1,2048]{1,0:T(1,128)}, u32[]{:S(2)}) copy-start(s32[1,2048]{1,0:T(1,128)} %param.8) | copy-start | bytes 24580
  25.5 21.8 %copy-start = (f32[147,2048]{1,0:T(8,128)S(1)}, f32[147,2048]{1,0:T(8,128)}, u32[]{:S(2)}) copy-start(f32[147,2048]{1,0:T(8,128)} %warm_ref.7) | copy-start | bytes 3612676
  43.9 8.4 %collective-permute-start.2 = (bf16[8,224,128]{2,1,0:T(8,128)(2,1)}, bf16[8,224,128]{2,1,0:T(8,128)(2,1)}, u32[]{:S(2)}, u32[]{:S(2)}) collective-permute-start(bf16[8,224,128]{2,1,0:T(8,128)(2,1)} %all_to_all.55.c_ref), channel_id=1, source_target_pairs={{0,192},{8,200},{16,208},{24,216},{32,224},{40,232},{48,240},{56,2... | collective-permute-start | bytes 1376264 | tf_op jit(solution)/shard_map/ppermute | solution.py:349
  44.8 11.0 %collective-permute-start.1 = (bf16[8,224,128]{2,1,0:T(8,128)(2,1)}, bf16[8,224,128]{2,1,0:T(8,128)(2,1)}, u32[]{:S(2)}, u32[]{:S(2)}) collective-permute-start(bf16[8,224,128]{2,1,0:T(8,128)(2,1)} %all_to_all.55.c_ref), channel_id=1, source_target_pairs={{0,128},{8,136},{16,144},{24,152},{32,160},{40,168},{48,176},{56,1... | collective-permute-start | bytes 1376264 | tf_op jit(solution)/shard_map/ppermute | solution.py:349
  46.3 22.3 %collective-permute-start = (bf16[8,224,128]{2,1,0:T(8,128)(2,1)}, bf16[8,224,128]{2,1,0:T(8,128)(2,1)S(1)}, u32[]{:S(2)}, u32[]{:S(2)}) collective-permute-start(bf16[8,224,128]{2,1,0:T(8,128)(2,1)} %all_to_all.55.c_ref), channel_id=1, source_target_pairs={{0,64},{8,72},{16,80},{24,88},{32,96},{40,104},{48,112},{56,120},{... | collective-permute-start | bytes 1376264 | tf_op jit(solution)/shard_map/ppermute | solution.py:349
  71.3 2.0 collective-permute-start.3
  73.5 6.0 %collective-permute-start.6 = (s16[160,512]{1,0:T(8,128)(2,1)S(1)}, s16[160,512]{1,0:T(8,128)(2,1)S(1)}, u32[]{:S(2)}, u32[]{:S(2)}) collective-permute-start(s16[160,512]{1,0:T(8,128)(2,1)S(1)} %get-tuple-element.116), channel_id=1, source_target_pairs={{0,6},{1,7},{2,0},{3,1},{4,2},{5,3},{6,4},{7,5},{8,14},{9,15},{10,... | collective-permute-start | bytes 491528 | tf_op jit(solution)/shard_map/ppermute | solution.py:407
  76.3 7.3 %collective-permute-start.5 = (s16[160,512]{1,0:T(8,128)(2,1)S(1)}, s16[160,512]{1,0:T(8,128)(2,1)S(1)}, u32[]{:S(2)}, u32[]{:S(2)}) collective-permute-start(s16[160,512]{1,0:T(8,128)(2,1)S(1)} %get-tuple-element.116), channel_id=1, source_target_pairs={{0,2},{1,3},{2,4},{3,5},{4,6},{5,7},{6,0},{7,1},{8,10},{9,11},{10,... | collective-permute-start | bytes 491528 | tf_op jit(solution)/shard_map/ppermute | solution.py:407
  76.3 8.8 %collective-permute-start.4 = (s16[160,512]{1,0:T(8,128)(2,1)S(1)}, s16[160,512]{1,0:T(8,128)(2,1)S(1)}, u32[]{:S(2)}, u32[]{:S(2)}) collective-permute-start(s16[160,512]{1,0:T(8,128)(2,1)S(1)} %get-tuple-element.116), channel_id=1, source_target_pairs={{0,4},{1,5},{2,6},{3,7},{4,0},{5,1},{6,2},{7,3},{8,12},{9,13},{10,... | collective-permute-start | bytes 491528 | tf_op jit(solution)/shard_map/ppermute | solution.py:407
  85.3 3.8 %collective-permute-start.7 = (f32[152,512]{1,0:T(8,128)S(1)}, f32[152,512]{1,0:T(8,128)S(1)}, u32[]{:S(2)}, u32[]{:S(2)}) collective-permute-start(f32[152,512]{1,0:T(8,128)S(1)} %decode.2.mine_ref), channel_id=1, source_target_pairs={{0,1},{1,0},{2,3},{3,2},{4,5},{5,4},{6,7},{7,6},{8,9},{9,8},{10,11... | collective-permute-start | bytes 933896 | tf_op jit(solution)/shard_map/ppermute | solution.py:409
  129.5 4.2 %collective-permute-start.10 = (bf16[8,80,128]{2,1,0:T(8,128)(2,1)S(1)}, bf16[8,80,128]{2,1,0:T(8,128)(2,1)S(1)}, u32[]{:S(2)}, u32[]{:S(2)}) collective-permute-start(bf16[8,80,128]{2,1,0:T(8,128)(2,1)S(1)} %all_to_all.57.g_ref), channel_id=1, source_target_pairs={{0,192},{8,200},{16,208},{24,216},{32,224},{40,232},{48,240},{56,2... | collective-permute-start | bytes 491528 | tf_op jit(solution)/shard_map/ppermute | solution.py:349
  130.8 5.8 %collective-permute-start.9 = (bf16[8,80,128]{2,1,0:T(8,128)(2,1)S(1)}, bf16[8,80,128]{2,1,0:T(8,128)(2,1)S(1)}, u32[]{:S(2)}, u32[]{:S(2)}) collective-permute-start(bf16[8,80,128]{2,1,0:T(8,128)(2,1)S(1)} %all_to_all.57.g_ref), channel_id=1, source_target_pairs={{0,128},{8,136},{16,144},{24,152},{32,160},{40,168},{48,176},{56,1... | collective-permute-start | bytes 491528 | tf_op jit(solution)/shard_map/ppermute | solution.py:349
  131.9 6.8 %collective-permute-start.8 = (bf16[8,80,128]{2,1,0:T(8,128)(2,1)S(1)}, bf16[8,80,128]{2,1,0:T(8,128)(2,1)S(1)}, u32[]{:S(2)}, u32[]{:S(2)}) collective-permute-start(bf16[8,80,128]{2,1,0:T(8,128)(2,1)S(1)} %all_to_all.57.g_ref), channel_id=1, source_target_pairs={{0,64},{8,72},{16,80},{24,88},{32,96},{40,104},{48,112},{56,120},{... | collective-permute-start | bytes 491528 | tf_op jit(solution)/shard_map/ppermute | solution.py:349
  172.5 5.7 %collective-permute-start.13 = (bf16[8,80,128]{2,1,0:T(8,128)(2,1)S(1)}, bf16[8,80,128]{2,1,0:T(8,128)(2,1)S(1)}, u32[]{:S(2)}, u32[]{:S(2)}) collective-permute-start(bf16[8,80,128]{2,1,0:T(8,128)(2,1)S(1)} %all_to_all.59.g_ref), channel_id=1, source_target_pairs={{0,192},{8,200},{16,208},{24,216},{32,224},{40,232},{48,240},{56,2... | collective-permute-start | bytes 491528 | tf_op jit(solution)/shard_map/ppermute | solution.py:349
  174.2 5.8 %collective-permute-start.12 = (bf16[8,80,128]{2,1,0:T(8,128)(2,1)S(1)}, bf16[8,80,128]{2,1,0:T(8,128)(2,1)S(1)}, u32[]{:S(2)}, u32[]{:S(2)}) collective-permute-start(bf16[8,80,128]{2,1,0:T(8,128)(2,1)S(1)} %all_to_all.59.g_ref), channel_id=1, source_target_pairs={{0,128},{8,136},{16,144},{24,152},{32,160},{40,168},{48,176},{56,1... | collective-permute-start | bytes 491528 | tf_op jit(solution)/shard_map/ppermute | solution.py:349
  175.3 6.4 %collective-permute-start.11 = (bf16[8,80,128]{2,1,0:T(8,128)(2,1)S(1)}, bf16[8,80,128]{2,1,0:T(8,128)(2,1)S(1)}, u32[]{:S(2)}, u32[]{:S(2)}) collective-permute-start(bf16[8,80,128]{2,1,0:T(8,128)(2,1)S(1)} %all_to_all.59.g_ref), channel_id=1, source_target_pairs={{0,64},{8,72},{16,80},{24,88},{32,96},{40,104},{48,112},{56,120},{... | collective-permute-start | bytes 491528 | tf_op jit(solution)/shard_map/ppermute | solution.py:349
  182.8 8.7 %collective-permute-start.14 = (f32[152,512]{1,0:T(8,128)S(1)}, f32[152,512]{1,0:T(8,128)S(1)}, u32[]{:S(2)}, u32[]{:S(2)}) collective-permute-start(f32[152,512]{1,0:T(8,128)S(1)} %get-tuple-element.137), channel_id=1, source_target_pairs={{0,1},{1,0},{2,3},{3,2},{4,5},{5,4},{6,7},{7,6},{8,9},{9,8},{10,11... | collective-permute-start | bytes 933896 | tf_op jit(solution)/shard_map/ppermute | solution.py:402
  191.6 5.5 %collective-permute-start.17 = (s16[160,512]{1,0:T(8,128)(2,1)S(1)}, s16[160,512]{1,0:T(8,128)(2,1)S(1)}, u32[]{:S(2)}, u32[]{:S(2)}) collective-permute-start(s16[160,512]{1,0:T(8,128)(2,1)S(1)} %get-tuple-element.139), channel_id=1, source_target_pairs={{0,6},{1,7},{2,0},{3,1},{4,2},{5,3},{6,4},{7,5},{8,14},{9,15},{10,... | collective-permute-start | bytes 491528 | tf_op jit(solution)/shard_map/ppermute | solution.py:407
  191.7 7.3 %collective-permute-start.16 = (s16[160,512]{1,0:T(8,128)(2,1)S(1)}, s16[160,512]{1,0:T(8,128)(2,1)S(1)}, u32[]{:S(2)}, u32[]{:S(2)}) collective-permute-start(s16[160,512]{1,0:T(8,128)(2,1)S(1)} %get-tuple-element.139), channel_id=1, source_target_pairs={{0,2},{1,3},{2,4},{3,5},{4,6},{5,7},{6,0},{7,1},{8,10},{9,11},{10,... | collective-permute-start | bytes 491528 | tf_op jit(solution)/shard_map/ppermute | solution.py:407
  193.1 7.8 %collective-permute-start.15 = (s16[160,512]{1,0:T(8,128)(2,1)S(1)}, s16[160,512]{1,0:T(8,128)(2,1)S(1)}, u32[]{:S(2)}, u32[]{:S(2)}) collective-permute-start(s16[160,512]{1,0:T(8,128)(2,1)S(1)} %get-tuple-element.139), channel_id=1, source_target_pairs={{0,4},{1,5},{2,6},{3,7},{4,0},{5,1},{6,2},{7,3},{8,12},{9,13},{10,... | collective-permute-start | bytes 491528 | tf_op jit(solution)/shard_map/ppermute | solution.py:407
  201.0 3.5 %collective-permute-start.18 = (f32[152,512]{1,0:T(8,128)S(1)}, f32[152,512]{1,0:T(8,128)S(1)}, u32[]{:S(2)}, u32[]{:S(2)}) collective-permute-start(f32[152,512]{1,0:T(8,128)S(1)} %decode.3.mine_ref), channel_id=1, source_target_pairs={{0,1},{1,0},{2,3},{3,2},{4,5},{5,4},{6,7},{7,6},{8,9},{9,8},{10,11... | collective-permute-start | bytes 933896 | tf_op jit(solution)/shard_map/ppermute | solution.py:409
  240.5 4.2 %collective-permute-start.21 = (bf16[8,80,128]{2,1,0:T(8,128)(2,1)S(1)}, bf16[8,80,128]{2,1,0:T(8,128)(2,1)S(1)}, u32[]{:S(2)}, u32[]{:S(2)}) collective-permute-start(bf16[8,80,128]{2,1,0:T(8,128)(2,1)S(1)} %all_to_all.61.g_ref), channel_id=1, source_target_pairs={{0,192},{8,200},{16,208},{24,216},{32,224},{40,232},{48,240},{56,2... | collective-permute-start | bytes 491528 | tf_op jit(solution)/shard_map/ppermute | solution.py:349
  241.8 5.8 %collective-permute-start.20 = (bf16[8,80,128]{2,1,0:T(8,128)(2,1)S(1)}, bf16[8,80,128]{2,1,0:T(8,128)(2,1)S(1)}, u32[]{:S(2)}, u32[]{:S(2)}) collective-permute-start(bf16[8,80,128]{2,1,0:T(8,128)(2,1)S(1)} %all_to_all.61.g_ref), channel_id=1, source_target_pairs={{0,128},{8,136},{16,144},{24,152},{32,160},{40,168},{48,176},{56,1... | collective-permute-start | bytes 491528 | tf_op jit(solution)/shard_map/ppermute | solution.py:349
  243.1 6.5 %collective-permute-start.19 = (bf16[8,80,128]{2,1,0:T(8,128)(2,1)S(1)}, bf16[8,80,128]{2,1,0:T(8,128)(2,1)S(1)}, u32[]{:S(2)}, u32[]{:S(2)}) collective-permute-start(bf16[8,80,128]{2,1,0:T(8,128)(2,1)S(1)} %all_to_all.61.g_ref), channel_id=1, source_target_pairs={{0,64},{8,72},{16,80},{24,88},{32,96},{40,104},{48,112},{56,120},{... | collective-permute-start | bytes 491528 | tf_op jit(solution)/shard_map/ppermute | solution.py:349
  283.8 6.0 %collective-permute-start.24 = (bf16[8,80,128]{2,1,0:T(8,128)(2,1)S(1)}, bf16[8,80,128]{2,1,0:T(8,128)(2,1)S(1)}, u32[]{:S(2)}, u32[]{:S(2)}) collective-permute-start(bf16[8,80,128]{2,1,0:T(8,128)(2,1)S(1)} %all_to_all.63.g_ref), channel_id=1, source_target_pairs={{0,192},{8,200},{16,208},{24,216},{32,224},{40,232},{48,240},{56,2... | collective-permute-start | bytes 491528 | tf_op jit(solution)/shard_map/ppermute | solution.py:349
  285.7 5.8 %collective-permute-start.23 = (bf16[8,80,128]{2,1,0:T(8,128)(2,1)S(1)}, bf16[8,80,128]{2,1,0:T(8,128)(2,1)S(1)}, u32[]{:S(2)}, u32[]{:S(2)}) collective-permute-start(bf16[8,80,128]{2,1,0:T(8,128)(2,1)S(1)} %all_to_all.63.g_ref), channel_id=1, source_target_pairs={{0,128},{8,136},{16,144},{24,152},{32,160},{40,168},{48,176},{56,1... | collective-permute-start | bytes 491528 | tf_op jit(solution)/shard_map/ppermute | solution.py:349
  286.7 6.5 %collective-permute-start.22 = (bf16[8,80,128]{2,1,0:T(8,128)(2,1)S(1)}, bf16[8,80,128]{2,1,0:T(8,128)(2,1)S(1)}, u32[]{:S(2)}, u32[]{:S(2)}) collective-permute-start(bf16[8,80,128]{2,1,0:T(8,128)(2,1)S(1)} %all_to_all.63.g_ref), channel_id=1, source_target_pairs={{0,64},{8,72},{16,80},{24,88},{32,96},{40,104},{48,112},{56,120},{... | collective-permute-start | bytes 491528 | tf_op jit(solution)/shard_map/ppermute | solution.py:349
  294.3 8.6 %collective-permute-start.25 = (f32[4,152,128]{2,1,0:T(8,128)S(1)}, f32[4,152,128]{2,1,0:T(8,128)S(1)}, u32[]{:S(2)}, u32[]{:S(2)}) collective-permute-start(f32[4,152,128]{2,1,0:T(8,128)S(1)} %get-tuple-element.162), channel_id=1, source_target_pairs={{0,1},{1,0},{2,3},{3,2},{4,5},{5,4},{6,7},{7,6},{8,9},{9,8},{10,11... | collective-permute-start | bytes 933896 | tf_op jit(solution)/shard_map/ppermute | solution.py:480
  302.9 5.6 %collective-permute-start.26 = (f32[152,128]{1,0:T(8,128)S(1)}, f32[152,128]{1,0:T(8,128)S(1)}, u32[]{:S(2)}, u32[]{:S(2)}) collective-permute-start(f32[152,128]{1,0:T(8,128)S(1)} %get-tuple-element.164), channel_id=1, source_target_pairs={{0,4},{1,5},{2,6},{3,7},{4,0},{5,1},{6,2},{7,3},{8,12},{9,13},{10,... | collective-permute-start | bytes 233480 | tf_op jit(solution)/shard_map/ppermute | solution.py:482
  304.7 5.6 %collective-permute-start.27 = (f32[152,128]{1,0:T(8,128)S(1)}, f32[152,128]{1,0:T(8,128)S(1)}, u32[]{:S(2)}, u32[]{:S(2)}) collective-permute-start(f32[152,128]{1,0:T(8,128)S(1)} %get-tuple-element.165), channel_id=1, source_target_pairs={{0,2},{1,3},{2,4},{3,5},{4,6},{5,7},{6,0},{7,1},{8,10},{9,11},{10,... | collective-permute-start | bytes 233480 | tf_op jit(solution)/shard_map/ppermute | solution.py:482
  304.7 5.6 %collective-permute-start.28 = (f32[152,128]{1,0:T(8,128)S(1)}, f32[152,128]{1,0:T(8,128)S(1)}, u32[]{:S(2)}, u32[]{:S(2)}) collective-permute-start(f32[152,128]{1,0:T(8,128)S(1)} %get-tuple-element.166), channel_id=1, source_target_pairs={{0,6},{1,7},{2,0},{3,1},{4,2},{5,3},{6,4},{7,5},{8,14},{9,15},{10,... | collective-permute-start | bytes 233480 | tf_op jit(solution)/shard_map/ppermute | solution.py:482
  (1 other events, 4.0 us)
